TPU v7x, 32 devices: a whole 2x2x4 slice. The times are simulated.
32 devices in a mesh: segment: 2 (over core), dp: 4 (over z), mp: 4 (over y, x).
Axes of the slice: x: 2, y: 2, z: 4, core: 2. Of those that a mesh axis runs over, the one named last changes fastest.
Arguments:
- candidates: bfloat16 [2048, 4096], P(('segment', 'dp'), 'mp'), may hold values from -6 to 6
- scorer_value: bfloat16 [2, 4096, 1024], P('segment', 'mp'), may hold values from -0.09375 to 0.09375
- scorer_out: bfloat16 [2, 1024, 4096], P('segment', None, 'mp'), may hold values from -0.1875 to 0.1875
- learner_value: bfloat16 [2, 4096, 1024], P('segment', 'mp'), may hold values from -0.0625 to 0.0625
- learner_out: bfloat16 [2, 1024, 4096], P('segment', None, 'mp'), may hold values from -0.1875 to 0.1875
- keep_index: int32 [8, 128], P(('segment', 'dp')), may hold values from 0 to 255, as said below
- keep_dest: int32 [8, 128], P(('segment', 'dp')), may hold values from 0 to 3, as said below
- keep_count: int32 [8], P(('segment', 'dp')), may hold values from 64 to 128, as said below
Outputs:
- grad_value: float32 [2, 1024, 4096], P('segment', 'dp', 'mp')
- grad_out: float32 [2, 1024, 4096], P('segment', 'dp', 'mp')
Inputs may be any that keep to these rules, and one draw needn't show every extreme that they name: `keep_index`: the entries of one shard's list are distinct. `keep_dest`: no candidate shard sends more than 64 of its first keep_count kept tokens to one learner shard, and some shard sends exactly 64; every learner shard receives at least one kept token from its own segment. Entries of keep_index and keep_dest at positions keep_count or later are ignored.
All inputs are finite; a program needn't handle non-finite values.
Results may differ from a plain program's by a relative error of at most 0.008.
Values may be sent and summed in bfloat16 or wider, within the bound.
No kernel may reach another device: no remote copies, remote signals or barrier semaphores. Data moves between devices by JAX's collectives and lax.ppermute only.
A program may use at most 128 MiB of HBM per device.

v0:
```python
import jax
import jax.numpy as jnp
from jax import lax
from jax.sharding import PartitionSpec as P

DS = 4096
DL = 8192


EPSILON = 1e-05


def partner(value, axis, apart):
    mask = 2**apart
    pairs = [(source, source ^ mask) for source in range(lax.axis_size(axis))]
    return lax.ppermute(value, axis, pairs)


def model_sum(pieces):
    return lax.psum(pieces, "mp")


def section(hidden, w_value, w_out):
    widened = hidden.astype(jnp.float32)
    partial_value = jnp.dot(hidden, w_value, preferred_element_type=jnp.float32)
    partial_value, squares = model_sum((partial_value, jnp.sum(widened * widened, axis=1)))
    inverse = lax.rsqrt(squares / DS + EPSILON)
    values = (partial_value * inverse[:, None]).astype(jnp.bfloat16)
    return (widened + jnp.dot(values, w_out, preferred_element_type=jnp.float32)).astype(
        jnp.bfloat16
    )


def on_device(
    candidates,
    scorer_value,
    scorer_out,
    learner_value,
    learner_out,
    keep_index,
    keep_dest,
    keep_count,
):
    first_core = lax.axis_index("segment") == 0
    own_value = scorer_value[0]
    own_out = scorer_out[0]
    current = candidates
    handed = candidates
    produced = candidates
    for step_index in range(3):
        produced = section(current, own_value, own_out)
        if step_index == 0:
            outgoing = jnp.where(first_core, produced, current)
        else:
            outgoing = produced
        if step_index < 2:
            current = partner(outgoing, "segment", 0)
            handed = current
    scored = jnp.where(first_core, handed, produced)
    peer_count = lax.axis_size("dp")
    keep_width = keep_index.shape[1]
    per_slot = 2 * keep_width // peer_count
    row_total = peer_count * per_slot
    half_width = candidates.shape[1]
    kept_index = keep_index[0]
    kept_dest = keep_dest[0]
    kept_total = keep_count[0]
    is_live = jnp.arange(keep_width) < kept_total
    to_peer = (kept_dest[:, None] == jnp.arange(peer_count)[None, :]) & is_live[:, None]
    marked = to_peer.astype(jnp.int32)
    earlier = jnp.cumsum(marked, axis=0) - marked
    position = jnp.sum(earlier * marked, axis=1)
    target = kept_dest * per_slot + position
    place_rows = ((target[:, None] == jnp.arange(row_total)[None, :]) & is_live[:, None]).astype(
        jnp.bfloat16
    )
    pick_rows = (kept_index[:, None] == jnp.arange(candidates.shape[0])[None, :]).astype(
        jnp.bfloat16
    )
    placement = lax.dot_general(
        place_rows, pick_rows, (((0,), (0,)), ((), ())), preferred_element_type=jnp.float32
    ).astype(jnp.bfloat16)
    features = jnp.concatenate([candidates, scored], axis=1)
    outgoing_rows = jnp.dot(placement, features, preferred_element_type=jnp.float32).astype(
        jnp.bfloat16
    )
    outgoing_rows = outgoing_rows.reshape(peer_count, per_slot, 2 * half_width)
    sent_counts = jnp.sum(marked, axis=0).astype(jnp.bfloat16).reshape(peer_count, 1)
    arrived, arrived_counts = (
        lax.all_to_all(outgoing_rows, "dp", split_axis=0, concat_axis=0, tiled=True),
        lax.all_to_all(sent_counts, "dp", split_axis=0, concat_axis=0, tiled=True),
    )
    rows_in = arrived.reshape(row_total, 2 * half_width)
    local_total = jnp.sum(arrived_counts.astype(jnp.float32))
    both_value, both_out = (
        lax.all_gather(learner_value, "segment", axis=0, tiled=True),
        lax.all_gather(learner_out, "segment", axis=0, tiled=True),
    )
    widened = rows_in.astype(jnp.float32)
    partial_value = jnp.dot(
        rows_in, both_value.reshape(2 * half_width, -1), preferred_element_type=jnp.float32
    )
    partial_value, squares = model_sum((partial_value, jnp.sum(widened * widened, axis=1)))
    inverse = lax.rsqrt(squares / DL + EPSILON)
    values = (partial_value * inverse[:, None]).astype(jnp.bfloat16)
    normed = (widened * inverse[:, None]).astype(jnp.bfloat16)
    projected = jnp.einsum("rk,hkf->rhf", values, both_out, preferred_element_type=jnp.float32)
    output = widened + projected.reshape(row_total, 2 * half_width)
    slopes = (output / local_total).astype(jnp.bfloat16)
    slope_halves = slopes.reshape(row_total, 2, half_width)
    back_part = jnp.einsum(
        "rhf,hkf->rk", slope_halves, both_out, preferred_element_type=jnp.float32
    )
    back_terms = model_sum(back_part).astype(jnp.bfloat16)
    grad_part = jnp.einsum(
        "rk,rhf->hkf",
        back_terms,
        normed.reshape(row_total, 2, half_width),
        preferred_element_type=jnp.float32,
    )
    out_part = jnp.einsum("rk,rhf->hkf", values, slope_halves, preferred_element_type=jnp.float32)
    gradient = jnp.concatenate([grad_part, out_part], axis=2)
    gradient = gradient.reshape(2 * gradient.shape[1], 2 * half_width)
    summed = lax.psum_scatter(gradient, ("segment", "dp"), scatter_dimension=0, tiled=True)
    grad_value = summed[:, :half_width][None]
    grad_out = summed[:, half_width:][None]
    return (grad_value, grad_out)


def solution(mesh):
    placed = (
        P(("segment", "dp"), "mp"),
        P("segment", "mp", None),
        P("segment", None, "mp"),
        P("segment", "mp", None),
        P("segment", None, "mp"),
        P(("segment", "dp"), None),
        P(("segment", "dp"), None),
        P(("segment", "dp")),
    )
    return jax.shard_map(
        on_device,
        mesh=mesh,
        in_specs=placed,
        out_specs=(P("segment", "dp", "mp"), P("segment", "dp", "mp")),
        check_vma=False,
    )
```

profile of v0, /device:TPU:11, one launch (start us, length us, event | category | flops | bytes accessed | tf_op | source)
XLA Modules:
  0.0 687.0 jit_solution(12471011347492147870)
XLA Ops:
  9.6 2.7 fusion.10
  12.6 6.2 psum.64
  18.8 47.4 %all-reduce.6.cloned.1.call-done = f32[256,1024]{1,0:T(8,128)} async-done(((f32[256,1024]{1,0:T(8,128)}), f32[256,1024]{1,0:T(8,128)}) %all-reduce.6.cloned.1.call-update) | async-done | bytes 1048592 | tf_op jit(solution)/shard_map/psum | solution.py:20
  66.2 2.7 fusion.33
  73.1 6.0 psum.66
  79.1 46.2 %all-reduce.8.cloned.1.call-done = f32[256,1024]{1,0:T(8,128)} async-done(((f32[256,1024]{1,0:T(8,128)}), f32[256,1024]{1,0:T(8,128)}) %all-reduce.8.cloned.1.call-update) | async-done | bytes 1048592 | tf_op jit(solution)/shard_map/psum | solution.py:20
  125.3 2.7 fusion.27
  134.5 6.4 psum.68
  140.9 43.6 %all-reduce.10.cloned.1.call-done = f32[256,1024]{1,0:T(8,128)} async-done(((f32[256,1024]{1,0:T(8,128)}), f32[256,1024]{1,0:T(8,128)}) %all-reduce.10.cloned.1.call-update) | async-done | bytes 1048592 | tf_op jit(solution)/shard_map/psum | solution.py:20
  184.5 2.8 fusion.24
  187.3 2.7 convolution_convert_fusion
  190.0 4.6 all-to-all-start
  194.6 21.8 %all-to-all-done = bf16[4,64,2048]{2,1,0:T(8,128)(2,1)S(1)} async-done(((bf16[4,64,2048]{2,1,0:T(8,128)(2,1)}), bf16[4,64,2048]{2,1,0:T(8,128)(2,1)S(1)}, u32[]{:S(2)}, u32[]{:S(2)}) %all-to-all-start) | async-done | bytes 1048608 | tf_op jit(solution)/shard_map/all_to_all | solution.py:90
  216.4 4.4 fusion.64
  221.0 9.0 %all_to_all.11 = bf16[4,1,1]{2,1,0:T(2,128)(2,1)S(1)} all-to-all(bf16[4,1,1]{2,1,0:T(2,128)(2,1)S(1)} %copy.23), channel_id=1, replica_groups=mesh['segment'=2,'dp'=4,'mp'=4] {'dp'}, dimensions={0} | all-to-all | bytes 16 | tf_op jit(solution)/shard_map/all_to_all | solution.py:91
  230.9 3.1 reshape.76
  234.0 6.0 psum.69
  240.0 35.6 %all-reduce.12.cloned.1.call-done = f32[256,1024]{1,0:T(8,128)} async-done(((f32[256,1024]{1,0:T(8,128)}), f32[256,1024]{1,0:T(8,128)}) %all-reduce.12.cloned.1.call-update) | async-done | bytes 1048592 | tf_op jit(solution)/shard_map/psum | solution.py:20
  275.6 5.8 divide_convert_fusion
  284.7 37.9 %all-reduce.13 = bf16[256,1024]{1,0:T(8,128)(2,1)S(1)} all-reduce(f32[256,1024]{1,0:T(8,128)} %convolution_bitcast_fusion.2), channel_id=1, replica_groups=mesh['segment'=2,'dp'=4,'mp'=4] {'mp'}, use_global_device_ids=true, to_apply=%region_16.17 | all-reduce | flops 262144 | bytes 1572864 | tf_op jit(solution)/shard_map/psum | solution.py:20
  326.0 6.4 pad_maximum_fusion
  332.4 17.3 %copy.26 = f32[2,1024,2048]{2,1,0:T(8,128)} copy(f32[2,1024,2048]{1,2,0:T(8,128)} %pad_maximum_fusion) | data formatting | bytes 33554432 | tf_op jit(solution)/shard_map/concatenate | solution.py:122
  349.8 327.0 %reduce-scatter.2.cloned.1.call-done = f32[256,2048]{1,0:T(8,128)} async-done(((f32[2048,2048]{1,0:T(8,128)}), f32[256,2048]{1,0:T(8,128)}) %reduce-scatter.2.cloned.1.call-update) | async-done | bytes 2097168 | tf_op jit(solution)/shard_map/reduce_scatter | solution.py:124
  676.7 3.1 slice_bitcast_fusion
  (64 shorter events, 19.6 us)
Async XLA Ops:
  8.0 1.6 copy-start
  8.0 4.4 copy-start.4
  8.0 58.2 %all-reduce.6.cloned.1.call-start = ((), (), s32[]{:S(2)}) async-start(), calls=%async_computation.3 | async-start | bytes 2097152 | tf_op jit(solution)/shard_map/psum | solution.py:20
  12.3 113.0 %all-reduce.8.cloned.1.call-start = ((), (), s32[]{:S(2)}) async-start(), calls=%async_computation.4 | async-start | bytes 2097152 | tf_op jit(solution)/shard_map/psum | solution.py:20
  68.9 2.3 collective-permute-start
  72.9 111.6 %all-reduce.10.cloned.1.call-start = ((), (), s32[]{:S(2)}) async-start(), calls=%async_computation.5 | async-start | bytes 2097152 | tf_op jit(solution)/shard_map/psum | solution.py:20
  128.0 2.3 collective-permute-start.1
  132.0 1.9 copy-start.8
  132.0 52.5 %copy-start.3 = (bf16[1,1024,1024]{2,1,0:T(8,128)(2,1)S(1)}, bf16[1,1024,1024]{2,1,0:T(8,128)(2,1)}, u32[]{:S(2)}) copy-start(bf16[1,1024,1024]{2,1,0:T(8,128)(2,1)} %param.10) | copy-start | bytes 6291460
  132.0 62.6 %all-gather.3.cloned.1.call-start = ((), (), s32[]{:S(2)}) async-start(), calls=%async_computation.6 | async-start | bytes 6291456 | tf_op jit(solution)/shard_map/all_gather | solution.py:96
  132.6 107.4 %all-gather.5.cloned.1.call-start = ((), (), s32[]{:S(2)}) async-start(), calls=%async_computation.8 | async-start | bytes 6291456 | tf_op jit(solution)/shard_map/all_gather | solution.py:97
  140.9 46.4 %copy-start.10 = (s32[1,128]{1,0:T(1,128)S(1)}, s32[1,128]{1,0:T(1,128)}, u32[]{:S(2)}) copy-start(s32[1,128]{1,0:T(1,128)} %param.13) | copy-start | bytes 1540
  190.0 26.4 %all-to-all-start = ((bf16[4,64,2048]{2,1,0:T(8,128)(2,1)}), bf16[4,64,2048]{2,1,0:T(8,128)(2,1)S(1)}, u32[]{:S(2)}, u32[]{:S(2)}) async-start(bf16[4,64,2048]{2,1,0:T(8,128)(2,1)} %bitcast.5), calls=%async_computation | async-start | bytes 2097152 | tf_op jit(solution)/shard_map/all_to_all | solution.py:90
  194.6 81.0 %all-reduce.12.cloned.1.call-start = ((), (), s32[]{:S(2)}) async-start(), calls=%async_computation.7 | async-start | bytes 2097152 | tf_op jit(solution)/shard_map/psum | solution.py:20
  220.8 455.9 %reduce-scatter.2.cloned.1.call-start = ((), (), s32[]{:S(2)}) async-start(), calls=%async_computation.9 | async-start | bytes 18874368 | tf_op jit(solution)/shard_map/reduce_scatter | solution.py:124
  275.6 6.8 copy-start.9
  281.4 1.0 copy-start.6
  282.4 40.2 %copy-start.2 = (f32[256,2,1024]{2,1,0:T(2,128)S(1)}, f32[256,2,1024]{2,1,0:T(2,128)}, u32[]{:S(2)}) copy-start(f32[256,2,1024]{2,1,0:T(2,128)} %reshape.76) | copy-start | bytes 6291460
  322.6 2.1 copy-start.5
  322.6 2.1 copy-start.7
  349.7 330.1 %copy-start.1 = (bf16[1,1024,1024]{2,1,0:T(8,128)(2,1)S(1)}, bf16[1,1024,1024]{2,1,0:T(8,128)(2,1)}, u32[]{:S(2)}) copy-start(bf16[1,1024,1024]{2,1,0:T(8,128)(2,1)} %param.9) | copy-start | bytes 6291460
Sparse Core Ops, SparseCore 0:
  12.5 53.6 all-reduce.5
  73.0 52.2 all-reduce.7
  132.1 52.3 all-reduce.9
  220.9 54.6 all-reduce.11
  349.9 326.8 reduce-scatter.1
Sparse Core Ops, SparseCore 1:
  134.0 14.0 all-gather.2
  149.5 14.7 all-gather.4
where the time goes:
time: 692 us; the launch traced here: 687 us
  waiting for transfers between devices  526 us (76%)
  blocking collectives  71.4 us (10%)
  matrix products  32.8 us (5%)
  local copies, waits for them, and re-layouts  26.3 us (4%)
  between operations  16.1 us (2%)
  other arithmetic  8.32 us (1%)
    reduce_scatter x1, waiting for transfers between devices, on_device(): lax.psum_scatter(gradient, ('segment', 'dp'), scatter_dimension=0, tiled=...  327 us
    psum x4, waiting for transfers between devices, model_sum(): return lax.psum(pieces, 'mp')  173 us
    psum x5, blocking collectives, model_sum(): return lax.psum(pieces, 'mp')  62.5 us
    all_to_all x1, waiting for transfers between devices, on_device(): lax.all_to_all(outgoing_rows, 'dp', split_axis=0, concat_axis=0, tiled=True)  21.8 us
    concatenate x1, local copies, waits for them, and re-layouts, on_device(): gradient = jnp.concatenate([grad_part, out_part], axis=2)  17.3 us
  transfers between devices with their start and end apart: 10, of which 8 were waited for; matrix products, arithmetic and copies ran while one was open for 2% of the time, Pallas kernels for 0%

commit v1 on v0

v1 whole, which is shorter than its diff:
```python
import jax
import jax.numpy as jnp
from jax import lax
from jax.sharding import PartitionSpec as P

EPSILON = 1e-05
BF = jnp.bfloat16
F32 = jnp.float32
SIDE = 128


def flip(value, axis, mask):
    pairs = [(source, source ^ mask) for source in range(lax.axis_size(axis))]
    return lax.ppermute(value, axis, pairs)


def matmul(left, right):
    return jnp.dot(left, right, preferred_element_type=F32)


def matmul_nt(left, right):
    return lax.dot_general(left, right, (((1,), (1,)), ((), ())), preferred_element_type=F32)


def matmul_tn(left, right):
    return lax.dot_general(left, right, (((0,), (0,)), ((), ())), preferred_element_type=F32)


def pack(columns):
    lane = lax.broadcasted_iota(jnp.int32, (columns[0].shape[0], SIDE), 1)
    side = jnp.zeros(lane.shape, F32)
    for place, column in enumerate(columns):
        rest = column
        for part in range(3):
            piece = lax.reduce_precision(rest, 8, 7)
            side = jnp.where(lane == 3 * place + part, piece, side)
            rest = rest - piece
    return side.astype(BF)


def unpack(side, place):
    wide = side[:, 3 * place : 3 * place + 3].astype(F32)
    return wide[:, 0:1] + wide[:, 1:2] + wide[:, 2:3]


def square_sum(value):
    wide = value.astype(F32)
    return jnp.sum(wide * wide, axis=1, keepdims=True)


def reduce_rows(partial, squares):
    half = partial.shape[0] // 2
    width = partial.shape[1]

    def step(part, norm, mask):
        sent = jnp.concatenate([part.astype(BF), pack([norm])], axis=1)
        got = flip(sent, "mp", mask)
        return part + got[:, :width].astype(F32), norm + unpack(got[:, width:], 0)

    top, top_norm = step(partial[:half], squares[:half], 1)
    low, low_norm = step(partial[half:], squares[half:], 2)
    top, top_norm = step(top, top_norm, 2)
    low, low_norm = step(low, low_norm, 1)
    return (
        jnp.concatenate([top, low], axis=0),
        jnp.concatenate([top_norm, low_norm], axis=0),
    )


def on_device(
    candidates,
    scorer_value,
    scorer_out,
    learner_value,
    learner_out,
    keep_index,
    keep_dest,
    keep_count,
):
    first = lax.axis_index("segment") == 0
    dp_at = lax.axis_index("dp")
    mp_at = lax.axis_index("mp")
    dp_size = lax.axis_size("dp")
    mp_size = lax.axis_size("mp")
    keep = keep_index.shape[1]
    width = candidates.shape[1]
    scorer_width = width * mp_size
    learner_width = 2 * scorer_width
    inner = learner_value.shape[2]
    block = inner // dp_size
    share = keep // mp_size

    own_value, own_out = scorer_value[0], scorer_out[0]
    own_lvalue, own_lout = learner_value[0], learner_out[0]
    other_value = flip(own_value, "segment", 1)
    other_out = flip(own_out, "segment", 1)
    other_lvalue = flip(own_lvalue, "segment", 1)
    other_lout = flip(own_lout, "segment", 1)

    is_live = jnp.arange(keep) < keep_count[0]
    pick = (keep_index[0][:, None] == jnp.arange(candidates.shape[0])[None, :]) & is_live[:, None]
    rows = matmul(pick.astype(BF), candidates).astype(BF)
    to_peer = (keep_dest[0][:, None] == jnp.arange(dp_size)[None, :]) & is_live[:, None]
    marked = to_peer.astype(jnp.int32)
    own_counts = jnp.sum(marked, axis=0, keepdims=True)
    counts = own_counts
    for mask in range(1, dp_size):
        counts = counts + flip(own_counts, "dp", mask)
    token_count = jnp.sum(marked * counts, axis=1, keepdims=True)
    token_count = jnp.where(is_live[:, None], token_count, 1).astype(F32)

    rows_squares = square_sum(rows)
    nothing = jnp.zeros_like(rows)
    partial = matmul(jnp.where(first, rows, nothing), own_value) + matmul(
        jnp.where(first, nothing, rows), other_value
    )
    hidden = rows
    squares = rows_squares
    for index in range(2):
        total, norm = reduce_rows(partial, squares)
        inverse = lax.rsqrt(norm / scorer_width + EPSILON)
        values = (total * inverse).astype(BF)
        if index == 0:
            w_out = lax.optimization_barrier(jnp.where(first, own_out, other_out))
        else:
            w_out = lax.optimization_barrier(jnp.where(first, other_out, own_out))
        hidden = (hidden.astype(F32) + matmul(values, w_out)).astype(BF)
        squares = square_sum(hidden)
        if index == 0:
            w_value = lax.optimization_barrier(jnp.where(first, other_value, own_value))
            partial = matmul(hidden, w_value)
    scored = hidden

    gram = matmul_nt(own_lout, lax.dynamic_slice_in_dim(own_lout, dp_at * block, block, 0))
    half = inner // 2
    at = lax.axis_index("segment")
    kept_half = lax.dynamic_slice_in_dim(gram, at * half, half, 0)
    sent_half = lax.dynamic_slice_in_dim(gram, (1 - at) * half, half, 0)
    kept_half = kept_half + flip(sent_half.astype(BF), "segment", 1).astype(F32)
    top, low = kept_half[: half // 2], kept_half[half // 2 :]
    top, low = (
        top + flip(top.astype(BF), "mp", 1).astype(F32),
        low + flip(low.astype(BF), "mp", 2).astype(F32),
    )
    top, low = (
        top + flip(top.astype(BF), "mp", 2).astype(F32),
        low + flip(low.astype(BF), "mp", 1).astype(F32),
    )
    gram_half = jnp.concatenate([top, low], axis=0).astype(BF)
    gram_other = flip(gram_half, "segment", 1)
    gram = jnp.where(
        first,
        jnp.concatenate([gram_half, gram_other], axis=0),
        jnp.concatenate([gram_other, gram_half], axis=0),
    )

    own_x = jnp.where(first, rows, scored)
    other_x = jnp.where(first, scored, rows)
    partial = jnp.concatenate(
        [
            matmul(own_x, own_lvalue) + matmul(other_x, other_lvalue),
            matmul_nt(own_x, own_lout) + matmul_nt(other_x, other_lout),
        ],
        axis=1,
    )
    squares = rows_squares + squares

    def share_of(array, peer):
        return lax.dynamic_slice_in_dim(array, peer * share, share, 0)

    sent = jnp.concatenate([partial.astype(BF), pack([squares])], axis=1)
    total, norm = share_of(partial, mp_at), share_of(squares, mp_at)
    for mask in range(1, mp_size):
        got = flip(share_of(sent, mp_at ^ mask), "mp", mask)
        total = total + got[:, : 2 * inner].astype(F32)
        norm = norm + unpack(got[:, 2 * inner :], 0)
    inverse = lax.rsqrt(norm / learner_width + EPSILON)
    values = (total[:, :inner] * inverse).astype(BF)
    crossed = total[:, inner:].astype(BF)
    side = pack([inverse, share_of(token_count, mp_at)])

    def in_order(array):
        return jnp.concatenate([share_of(array, mp_at ^ mask) for mask in range(mp_size)], axis=0)

    rows_order, scored_order = in_order(rows), in_order(scored)
    column = dp_at * block

    def add(grads, piece, near_rows, near_scored):
        shares = [piece] + [flip(piece, "mp", mask) for mask in range(1, mp_size)]
        tokens = jnp.concatenate(shares, axis=0)
        tokens = jnp.concatenate([tokens, flip(tokens, "segment", 1)], axis=0)
        near = jnp.where(first, near_rows, near_scored)
        far = flip(jnp.where(first, near_scored, near_rows), "segment", 1)
        x = jnp.concatenate([near, far], axis=0).astype(F32)
        v = tokens[:, :inner]
        xo = tokens[:, inner : inner + block].astype(F32)
        scalars = tokens[:, inner + block :]
        inv = unpack(scalars, 0)
        share_count = 1.0 / unpack(scalars, 1)
        slopes = ((x + matmul(v, own_lout)) * share_count).astype(BF)
        normed = (x * inv).astype(BF)
        back = ((xo + matmul(v, gram)) * share_count).astype(BF)
        v_block = lax.dynamic_slice_in_dim(v, column, block, 1)
        return (grads[0] + matmul_tn(back, normed), grads[1] + matmul_tn(v_block, slopes))

    grads = (jnp.zeros((block, width), F32), jnp.zeros((block, width), F32))
    if dp_size <= 8:
        for away in range(dp_size):
            cross = lax.dynamic_slice_in_dim(crossed, (dp_at ^ away) * block, block, 1)
            piece = jnp.concatenate([values, cross, side], axis=1)
            near_rows, near_scored = rows_order, scored_order
            if away > 0:
                piece = flip(piece, "dp", away)
                near_rows = flip(rows_order, "dp", away)
                near_scored = flip(scored_order, "dp", away)
            grads = add(grads, piece, near_rows, near_scored)
    else:
        ring = [(source, (source + 1) % dp_size) for source in range(dp_size)]

        def turn(_, carry):
            grads, held = carry
            full, near_rows, near_scored = held
            cross = lax.dynamic_slice_in_dim(full, inner + column, block, 1)
            piece = jnp.concatenate([full[:, :inner], cross, full[:, 2 * inner :]], axis=1)
            grads = add(grads, piece, near_rows, near_scored)
            return grads, [lax.ppermute(array, "dp", ring) for array in held]

        full = jnp.concatenate([values, crossed, side], axis=1)
        grads, _ = lax.fori_loop(0, dp_size, turn, (grads, [full, rows_order, scored_order]))
    grad_value, grad_out = grads
    return (grad_value[None], grad_out[None])


def solution(mesh):
    placed = (
        P(("segment", "dp"), "mp"),
        P("segment", "mp", None),
        P("segment", None, "mp"),
        P("segment", "mp", None),
        P("segment", None, "mp"),
        P(("segment", "dp"), None),
        P(("segment", "dp"), None),
        P(("segment", "dp")),
    )
    return jax.shard_map(
        on_device,
        mesh=mesh,
        in_specs=placed,
        out_specs=(P("segment", "dp", "mp"), P("segment", "dp", "mp")),
        check_vma=False,
    )
```

time: 692 us -> 210 us (0.30)
  waiting for transfers between devices: 526 us -> 43.7 us
  blocking collectives: 71.4 us -> 0 us
  starting transfers between devices: 6.3 us -> 74.6 us
  other arithmetic: 8.32 us -> 30.2 us
  between operations: 16.1 us -> 2.34 us
  local copies, waits for them, and re-layouts: 26.3 us -> 13 us
  matrix products: 32.8 us -> 43.3 us
    reduce_scatter x1 -> x0, waiting for transfers between devices: 327 us -> none  [on_device(): lax.psum_scatter(gradient, ('segment', 'dp'), scatter_dimension=0, tiled=...]
    psum x4 -> x0, waiting for transfers between devices: 173 us -> none  [model_sum(): return lax.psum(pieces, 'mp')]
    ppermute x2 -> x53, starting transfers between devices: 1.48 us -> 74.6 us  [flip(): return lax.ppermute(value, axis, pairs)]
    psum x5 -> x0, blocking collectives: 62.5 us -> none  [model_sum(): return lax.psum(pieces, 'mp')]
    ppermute x2 -> x53, waiting for transfers between devices: 3.07 us -> 43.7 us  [flip(): return lax.ppermute(value, axis, pairs)]
    all_to_all x1 -> x0, waiting for transfers between devices: 21.8 us -> none  [on_device(): lax.all_to_all(outgoing_rows, 'dp', split_axis=0, concat_axis=0, tiled=True)]
    concatenate x1 -> x4, local copies, waits for them, and re-layouts: 17.3 us -> 2.11 us  [add(): tokens = jnp.concatenate([tokens, flip(tokens, 'segment', 1)], axis=0)]
    dot_general x12 -> x19, matrix products: 32.8 us -> 43.3 us  [the longest x8 26.2 us: matmul_tn(): lax.dot_general(left, right, (((0,), (0,)), ((), ())), preferred_element_...]
  transfers between devices with their start and end apart: 10 -> 53, of which waited for: 8 -> 19; matrix products, arithmetic and copies ran while one was open for 2% -> 33% of each run, Pallas kernels for 0% -> 0%
where the time goes in v1:
time: 210 us; the launch traced here: 207 us
  starting transfers between devices  74.6 us (36%)
  waiting for transfers between devices  43.7 us (21%)
  matrix products  43.3 us (21%)
  other arithmetic  30.2 us (14%)
  local copies, waits for them, and re-layouts  13 us (6%)
  between operations  2.34 us (1%)
    ppermute x53, starting transfers between devices, flip(): return lax.ppermute(value, axis, pairs)  74.6 us
    ppermute x53, waiting for transfers between devices, flip(): return lax.ppermute(value, axis, pairs)  43.7 us
    dot_general x8, matrix products, matmul_tn(): lax.dot_general(left, right, (((0,), (0,)), ((), ())), preferred_element_...  26.2 us
    dot_general x8, matrix products, matmul(): return jnp.dot(left, right, preferred_element_type=F32)  8.59 us
    dot_general x3, matrix products, matmul_nt(): lax.dot_general(left, right, (((1,), (1,)), ((), ())), preferred_element_...  8.45 us
    select_n x4, other arithmetic, add(): near = jnp.where(first, near_rows, near_scored)  4.58 us
  transfers between devices with their start and end apart: 53, of which 19 were waited for; matrix products, arithmetic and copies ran while one was open for 33% of the time, Pallas kernels for 0%

profile of v1, /device:TPU:11, one launch (start us, length us, event | category | flops | bytes accessed | tf_op | source)
XLA Modules:
  0.0 207.1 jit_solution(14700055490131784390)
XLA Ops:
  6.9 3.6 %fusion.31 = f32[256,1024]{1,0:T(8,128)} fusion(bf16[1,1024,1024]{2,1,0:T(8,128)(2,1)} %param.12, s32[]{:T(128)S(6)} %select_n.275), kind=kOutput, calls=%fused_computation.64 | convolution fusion | flops 536870912 | bytes 3670020 | tf_op jit(solution)/shard_map/dot_general | solution.py:22
  18.5 3.1 %collective-permute-done.23 = bf16[256,256]{0,1:T(8,128)(2,1)S(1)} collective-permute-done((bf16[256,256]{0,1:T(8,128)(2,1)S(1)}, bf16[256,256]{0,1:T(8,128)(2,1)S(1)}, u32[]{:S(2)}, u32[]{:S(2)}) %collective-permute-start.23) | collective-permute-done | bytes 131104 | tf_op jit(solution)/shard_map/ppermute | solution.py:14
  25.5 2.7 %collective-permute-start.10 = (bf16[1024,1024]{1,0:T(8,128)(2,1)}, bf16[1024,1024]{1,0:T(8,128)(2,1)}, u32[]{:S(2)}, u32[]{:S(2)}) collective-permute-start(bf16[1024,1024]{1,0:T(8,128)(2,1)} %bitcast.8), channel_id=1, source_target_pairs={{0,16},{16,0},{1,17},{17,1},{2,18},{18,2},{3,19},{19,3},{4,20},{20... | collective-permute-start | bytes 6291464 | tf_op jit(solution)/shard_map/ppermute | solution.py:14
  35.6 2.6 %collective-permute-done.1 = bf16[64,1152]{1,0:T(8,128)(2,1)S(1)} collective-permute-done((bf16[64,1152]{1,0:T(8,128)(2,1)S(1)}, bf16[64,1152]{1,0:T(8,128)(2,1)S(1)}, u32[]{:S(2)}, u32[]{:S(2)}) %collective-permute-start.1) | collective-permute-done | bytes 147488 | tf_op jit(solution)/shard_map/ppermute | solution.py:14
  39.1 4.2 %collective-permute-done.3 = bf16[64,1152]{1,0:T(8,128)(2,1)S(1)} collective-permute-done((bf16[64,1152]{1,0:T(8,128)(2,1)S(1)}, bf16[64,1152]{1,0:T(8,128)(2,1)S(1)}, u32[]{:S(2)}, u32[]{:S(2)}) %collective-permute-start.3) | collective-permute-done | bytes 147488 | tf_op jit(solution)/shard_map/ppermute | solution.py:14
  45.3 2.5 %collective-permute-done.4 = bf16[64,1152]{1,0:T(8,128)(2,1)S(1)} collective-permute-done((bf16[64,1152]{1,0:T(8,128)(2,1)S(1)}, bf16[64,1152]{1,0:T(8,128)(2,1)S(1)}, u32[]{:S(2)}, u32[]{:S(2)}) %collective-permute-start.4) | collective-permute-done | bytes 147488 | tf_op jit(solution)/shard_map/ppermute | solution.py:14
  52.7 3.2 %collective-permute-done.6 = bf16[64,1152]{1,0:T(8,128)(2,1)S(1)} collective-permute-done((bf16[64,1152]{1,0:T(8,128)(2,1)S(1)}, bf16[64,1152]{1,0:T(8,128)(2,1)S(1)}, u32[]{:S(2)}, u32[]{:S(2)}) %collective-permute-start.6) | collective-permute-done | bytes 147488 | tf_op jit(solution)/shard_map/ppermute | solution.py:14
  68.2 2.6 %collective-permute-done.9 = bf16[64,1152]{1,0:T(8,128)(2,1)S(1)} collective-permute-done((bf16[64,1152]{1,0:T(8,128)(2,1)S(1)}, bf16[64,1152]{1,0:T(8,128)(2,1)S(1)}, u32[]{:S(2)}, u32[]{:S(2)}) %collective-permute-start.9) | collective-permute-done | bytes 147488 | tf_op jit(solution)/shard_map/ppermute | solution.py:14
  95.2 3.6 %collective-permute-done.18 = bf16[32,1408]{1,0:T(8,128)(2,1)S(1)} collective-permute-done((bf16[32,1408]{1,0:T(8,128)(2,1)S(1)}, bf16[32,1408]{1,0:T(8,128)(2,1)S(1)}, u32[]{:S(2)}, u32[]{:S(2)}) %collective-permute-start.18) | collective-permute-done | bytes 90144 | tf_op jit(solution)/shard_map/ppermute | solution.py:14
  99.8 2.8 %collective-permute-done.19 = bf16[32,1408]{1,0:T(8,128)(2,1)S(1)} collective-permute-done((bf16[32,1408]{1,0:T(8,128)(2,1)S(1)}, bf16[32,1408]{1,0:T(8,128)(2,1)S(1)}, u32[]{:S(2)}, u32[]{:S(2)}) %collective-permute-start.19) | collective-permute-done | bytes 90144 | tf_op jit(solution)/shard_map/ppermute | solution.py:14
  104.3 3.8 %collective-permute-done.20 = bf16[32,1408]{1,0:T(8,128)(2,1)S(1)} collective-permute-done((bf16[32,1408]{1,0:T(8,128)(2,1)S(1)}, bf16[32,1408]{1,0:T(8,128)(2,1)S(1)}, u32[]{:S(2)}, u32[]{:S(2)}) %collective-permute-start.20) | collective-permute-done | bytes 90144 | tf_op jit(solution)/shard_map/ppermute | solution.py:14
  108.1 4.5 %collective-permute-done.29 = bf16[32,1408]{1,0:T(8,128)(2,1)S(1)} collective-permute-done((bf16[32,1408]{1,0:T(8,128)(2,1)S(1)}, bf16[32,1408]{1,0:T(8,128)(2,1)S(1)}, u32[]{:S(2)}, u32[]{:S(2)}) %collective-permute-start.29) | collective-permute-done | bytes 90144 | tf_op jit(solution)/shard_map/ppermute | solution.py:14
  112.7 3.1 %collective-permute-start.37 = (bf16[32,1408]{1,0:T(8,128)(2,1)S(1)}, bf16[32,1408]{1,0:T(8,128)(2,1)S(1)}, u32[]{:S(2)}, u32[]{:S(2)}) collective-permute-start(bf16[32,1408]{1,0:T(8,128)(2,1)S(1)} %get-tuple-element.75), channel_id=1, source_target_pairs={{0,8},{4,12},{8,0},{12,4},{1,9},{5,13},{9,1},{13,5},{2,10},{6,14},... | collective-permute-start | bytes 270344 | tf_op jit(solution)/shard_map/ppermute | solution.py:14
  118.2 3.2 %collective-permute-done.45 = bf16[32,1408]{1,0:T(8,128)(2,1)S(1)} collective-permute-done((bf16[32,1408]{1,0:T(8,128)(2,1)S(1)}, bf16[32,1408]{1,0:T(8,128)(2,1)S(1)}, u32[]{:S(2)}, u32[]{:S(2)}) %collective-permute-start.45) | collective-permute-done | bytes 90144 | tf_op jit(solution)/shard_map/ppermute | solution.py:14
  123.0 18.0 %collective-permute-start.28 = (bf16[128,1024]{1,0:T(8,128)(2,1)S(1)}, bf16[128,1024]{1,0:T(8,128)(2,1)S(1)}, u32[]{:S(2)}, u32[]{:S(2)}) collective-permute-start(bf16[128,1024]{1,0:T(8,128)(2,1)S(1)} %get-tuple-element.50), channel_id=1, source_target_pairs={{0,16},{16,0},{1,17},{17,1},{2,18},{18,2},{3,19},{19,3},{4,20},{20... | collective-permute-start | bytes 786440 | tf_op jit(solution)/shard_map/ppermute | solution.py:14
  157.6 9.6 %collective-permute-start.36 = (bf16[128,1024]{1,0:T(8,128)(2,1)}, bf16[128,1024]{1,0:T(8,128)(2,1)}, u32[]{:S(2)}, u32[]{:S(2)}) collective-permute-start(bf16[128,1024]{1,0:T(8,128)(2,1)} %get-tuple-element.42), channel_id=1, source_target_pairs={{0,16},{16,0},{1,17},{17,1},{2,18},{18,2},{3,19},{19,3},{4,20},{20... | collective-permute-start | bytes 786440 | tf_op jit(solution)/shard_map/ppermute | solution.py:14
  167.5 2.8 %collective-permute-start.52 = (bf16[128,1024]{1,0:T(8,128)(2,1)}, bf16[128,1024]{1,0:T(8,128)(2,1)}, u32[]{:S(2)}, u32[]{:S(2)}) collective-permute-start(bf16[128,1024]{1,0:T(8,128)(2,1)} %get-tuple-element.38), channel_id=1, source_target_pairs={{0,16},{16,0},{1,17},{17,1},{2,18},{18,2},{3,19},{19,3},{4,20},{20... | collective-permute-start | bytes 786440 | tf_op jit(solution)/shard_map/ppermute | solution.py:14
  173.2 3.0 %fusion.27 = f32[256,1024]{1,0:T(8,128)} fusion(f32[256]{0:T(256)S(1)} %fusion.74, bf16[128,1024]{1,0:T(8,128)(2,1)} %copy-done.15, bf16[128,1024]{1,0:T(8,128)(2,1)S(1)} %get-tuple-element.49, bf16[256,1408]{1,0:T(8,128)(2,1)} %copy-done.14, f32[256]{0:T(256)S(1)} %fusion.88, bf16[1024,256]{0,1:T(8,128)(2,1)S(1)} %maximum_select_fusion), kind=kOutput, calls=%fused_computation.53 | convolution fusion | flops 270270464 | bytes 2754560 | tf_op jit(solution)/shard_map/dot_general | solution.py:26
  183.8 3.7 %fusion.14 = f32[256,1024]{1,0:T(8,128)} fusion(bf16[256,1024]{1,0:T(8,128)(2,1)S(1)} %slice.553, f32[256]{0:T(256)S(1)} %fusion.89, bf16[128,1024]{1,0:T(8,128)(2,1)} %collective-permute-done.36, bf16[128,1024]{1,0:T(8,128)(2,1)} %get-tuple-element.41, s32[]{:T(128)S(6)} %select_n.275, bf16[1,1024,1024]{2,1,0:T(8,128)(2,1)} %param.12), kind=kOutput, calls=%fused_computation.32 | convolution fusion | flops 672923648 | bytes 4326404 | tf_op jit(solution)/shard_map/dot_general | solution.py:26
  187.5 2.4 %convolution_add_fusion.3 = f32[256,1024]{1,0:T(8,128)S(1)} fusion(f32[256,1024]{1,0:T(8,128)} %fusion.27, f32[256]{0:T(256)S(1)} %fusion.71, bf16[128,1024]{1,0:T(8,128)(2,1)} %collective-permute-done.36, bf16[128,1024]{1,0:T(8,128)(2,1)S(1)} %copy-done.11, bf16[256,1408]{1,0:T(8,128)(2,1)} %copy-done.9, f32[256]{0:T(256)S(1)} %fusion.89, ...), kind=kOutput, calls=%fused_computation.10 | convolution fusion | flops 270532608 | bytes 3803136 | tf_op jit(solution)/shard_map/dot_general | solution.py:26
  189.9 3.7 %fusion.13 = f32[256,1024]{1,0:T(8,128)} fusion(bf16[256,1024]{1,0:T(8,128)(2,1)} %slice.563, f32[256]{0:T(256)S(1)} %fusion.90, bf16[128,1024]{1,0:T(8,128)(2,1)} %collective-permute-done.44, bf16[128,1024]{1,0:T(8,128)(2,1)S(1)} %copy-done.12, s32[]{:T(128)S(6)} %select_n.275, bf16[1,1024,1024]{2,1,0:T(8,128)(2,1)} %param.12), kind=kOutput, calls=%fused_computation.31 | convolution fusion | flops 672923648 | bytes 4326404 | tf_op jit(solution)/shard_map/dot_general | solution.py:26
  195.8 3.8 %fusion.12 = f32[256,1024]{1,0:T(8,128)} fusion(bf16[256,1024]{1,0:T(8,128)(2,1)} %slice.573, f32[256]{0:T(256)S(1)} %fusion.91, bf16[128,1024]{1,0:T(8,128)(2,1)} %collective-permute-done.52, bf16[128,1024]{1,0:T(8,128)(2,1)} %get-tuple-element.37, s32[]{:T(128)S(6)} %select_n.275, bf16[1,1024,1024]{2,1,0:T(8,128)(2,1)} %param.12), kind=kOutput, calls=%fused_computation.30 | convolution fusion | flops 672923648 | bytes 4326404 | tf_op jit(solution)/shard_map/dot_general | solution.py:26
  199.6 2.8 %fusion.3 = f32[1,256,1024]{2,1,0:T(8,128)} fusion(f32[256,1024]{1,0:T(8,128)S(1)} %convolution_add_fusion.2, f32[256]{0:T(256)S(1)} %fusion.65, bf16[128,1024]{1,0:T(8,128)(2,1)} %collective-permute-done.52, bf16[128,1024]{1,0:T(8,128)(2,1)S(1)} %copy-done.13, bf16[256,1408]{1,0:T(8,128)(2,1)S(1)} %copy-done.7, f32[256]{0:T(256)S(1)} %fusion.91, ...), kind=kOutput, calls=%fused_computation.8 | convolution fusion | flops 270532608 | bytes 3803136 | tf_op jit(solution)/shard_map/dot_general | solution.py:26
  202.4 4.7 %fusion.2 = f32[1,256,1024]{2,1,0:T(8,128)} fusion(f32[256,1024]{1,0:T(8,128)} %fusion.12, f32[256,1024]{1,0:T(8,128)} %fusion.13, f32[256,1024]{1,0:T(8,128)} %fusion.14, bf16[256,1024]{1,0:T(8,128)(2,1)} %slice.541, f32[256]{0:T(256)S(1)} %fusion.88, bf16[128,1024]{1,0:T(8,128)(2,1)} %copy-done.15, bf16[128,1024]{1,0:T(8,128)(2,1)S(1)} %get-tuple-element.49, ...), kind=kOutput, calls=%fused_computation.6 | convolution fusion | flops 673710080 | bytes 7472132 | tf_op jit(solution)/shard_map/dot_general | solution.py:26
  (294 shorter events, 104.8 us)
Async XLA Ops:
  2.1 14.6 %collective-permute-start.17 = (s32[1,4]{1,0:T(1,128)S(1)}, s32[1,4]{1,0:T(1,128)S(1)}, u32[]{:S(2)}, u32[]{:S(2)}) collective-permute-start(s32[1,4]{1,0:T(1,128)S(1)} %bitcast.83), channel_id=1, source_target_pairs={{0,12},{4,8},{8,4},{12,0},{1,13},{5,9},{9,5},{13,1},{2,14},{6,10},... | collective-permute-start | bytes 56 | tf_op jit(solution)/shard_map/ppermute | solution.py:14
  3.5 13.4 %collective-permute-start.16 = (s32[1,4]{1,0:T(1,128)S(1)}, s32[1,4]{1,0:T(1,128)S(1)}, u32[]{:S(2)}, u32[]{:S(2)}) collective-permute-start(s32[1,4]{1,0:T(1,128)S(1)} %bitcast.84), channel_id=1, source_target_pairs={{0,8},{4,12},{8,0},{12,4},{1,9},{5,13},{9,1},{13,5},{2,10},{6,14},... | collective-permute-start | bytes 56 | tf_op jit(solution)/shard_map/ppermute | solution.py:14
  4.6 12.6 %collective-permute-start.15 = (s32[1,4]{1,0:T(1,128)S(1)}, s32[1,4]{1,0:T(1,128)S(1)}, u32[]{:S(2)}, u32[]{:S(2)}) collective-permute-start(s32[1,4]{1,0:T(1,128)S(1)} %bitcast.85), channel_id=1, source_target_pairs={{0,4},{4,0},{8,12},{12,8},{1,5},{5,1},{9,13},{13,9},{2,6},{6,2},{1... | collective-permute-start | bytes 56 | tf_op jit(solution)/shard_map/ppermute | solution.py:14
  5.7 24.8 %collective-permute-start = (bf16[1024,1024]{1,0:T(8,128)(2,1)}, bf16[1024,1024]{1,0:T(8,128)(2,1)}, u32[]{:S(2)}, u32[]{:S(2)}) collective-permute-start(bf16[1024,1024]{1,0:T(8,128)(2,1)} %bitcast.81), channel_id=1, source_target_pairs={{0,16},{16,0},{1,17},{17,1},{2,18},{18,2},{3,19},{19,3},{4,20},{20... | collective-permute-start | bytes 6291464 | tf_op jit(solution)/shard_map/ppermute | solution.py:14
  15.1 18.8 %collective-permute-start.5 = (bf16[1024,1024]{1,0:T(8,128)(2,1)S(1)}, bf16[1024,1024]{1,0:T(8,128)(2,1)S(1)}, u32[]{:S(2)}, u32[]{:S(2)}) collective-permute-start(bf16[1024,1024]{1,0:T(8,128)(2,1)S(1)} %bitcast.82), channel_id=1, source_target_pairs={{0,16},{16,0},{1,17},{17,1},{2,18},{18,2},{3,19},{19,3},{4,20},{20... | collective-permute-start | bytes 6291464 | tf_op jit(solution)/shard_map/ppermute | solution.py:14
  16.8 62.2 %collective-permute-start.11 = (bf16[1024,1024]{1,0:T(8,128)(2,1)}, bf16[1024,1024]{1,0:T(8,128)(2,1)}, u32[]{:S(2)}, u32[]{:S(2)}) collective-permute-start(bf16[1024,1024]{1,0:T(8,128)(2,1)} %bitcast.9), channel_id=1, source_target_pairs={{0,16},{16,0},{1,17},{17,1},{2,18},{18,2},{3,19},{19,3},{4,20},{20... | collective-permute-start | bytes 6291464 | tf_op jit(solution)/shard_map/ppermute | solution.py:14
  25.5 55.9 %collective-permute-start.10 = (bf16[1024,1024]{1,0:T(8,128)(2,1)}, bf16[1024,1024]{1,0:T(8,128)(2,1)}, u32[]{:S(2)}, u32[]{:S(2)}) collective-permute-start(bf16[1024,1024]{1,0:T(8,128)(2,1)} %bitcast.8), channel_id=1, source_target_pairs={{0,16},{16,0},{1,17},{17,1},{2,18},{18,2},{3,19},{19,3},{4,20},{20... | collective-permute-start | bytes 6291464 | tf_op jit(solution)/shard_map/ppermute | solution.py:14
  29.0 30.7 %collective-permute-start.27 = (bf16[512,256]{0,1:T(8,128)(2,1)}, bf16[512,256]{0,1:T(8,128)(2,1)}, u32[]{:S(2)}, u32[]{:S(2)}) collective-permute-start(bf16[512,256]{0,1:T(8,128)(2,1)} %pad_maximum_fusion.17), channel_id=1, source_target_pairs={{0,16},{16,0},{1,17},{17,1},{2,18},{18,2},{3,19},{19,3},{4,20},{20... | collective-permute-start | bytes 786440 | tf_op jit(solution)/shard_map/ppermute | solution.py:14
  87.2 6.5 %collective-permute-start.12 = (bf16[32,2176]{1,0:T(8,128)(2,1)S(1)}, bf16[32,2176]{1,0:T(8,128)(2,1)S(1)}, u32[]{:S(2)}, u32[]{:S(2)}) collective-permute-start(bf16[32,2176]{1,0:T(8,128)(2,1)S(1)} %get-tuple-element.34), channel_id=1, source_target_pairs={{0,1},{1,0},{2,3},{3,2},{4,5},{5,4},{6,7},{7,6},{8,9},{9,8},{10,11... | collective-permute-start | bytes 417800 | tf_op jit(solution)/shard_map/ppermute | solution.py:14
  88.0 33.9 %collective-permute-start.34 = (bf16[128,1024]{1,0:T(8,128)(2,1)}, bf16[128,1024]{1,0:T(8,128)(2,1)}, u32[]{:S(2)}, u32[]{:S(2)}) collective-permute-start(bf16[128,1024]{1,0:T(8,128)(2,1)} %pad_maximum_fusion.18), channel_id=1, source_target_pairs={{0,4},{4,0},{8,12},{12,8},{1,5},{5,1},{9,13},{13,9},{2,6},{6,2},{1... | collective-permute-start | bytes 786440 | tf_op jit(solution)/shard_map/ppermute | solution.py:14
  88.5 54.3 %collective-permute-start.42 = (bf16[128,1024]{1,0:T(8,128)(2,1)}, bf16[128,1024]{1,0:T(8,128)(2,1)}, u32[]{:S(2)}, u32[]{:S(2)}) collective-permute-start(bf16[128,1024]{1,0:T(8,128)(2,1)} %pad_maximum_fusion.18), channel_id=1, source_target_pairs={{0,8},{4,12},{8,0},{12,4},{1,9},{5,13},{9,1},{13,5},{2,10},{6,14},... | collective-permute-start | bytes 786440 | tf_op jit(solution)/shard_map/ppermute | solution.py:14
  90.7 32.2 %collective-permute-start.35 = (bf16[128,1024]{1,0:T(8,128)(2,1)S(1)}, bf16[128,1024]{1,0:T(8,128)(2,1)S(1)}, u32[]{:S(2)}, u32[]{:S(2)}) collective-permute-start(bf16[128,1024]{1,0:T(8,128)(2,1)S(1)} %pad_maximum_fusion.19), channel_id=1, source_target_pairs={{0,4},{4,0},{8,12},{12,8},{1,5},{5,1},{9,13},{13,9},{2,6},{6,2},{1... | collective-permute-start | bytes 786440 | tf_op jit(solution)/shard_map/ppermute | solution.py:14
  92.3 50.6 %collective-permute-start.43 = (bf16[128,1024]{1,0:T(8,128)(2,1)S(1)}, bf16[128,1024]{1,0:T(8,128)(2,1)S(1)}, u32[]{:S(2)}, u32[]{:S(2)}) collective-permute-start(bf16[128,1024]{1,0:T(8,128)(2,1)S(1)} %pad_maximum_fusion.19), channel_id=1, source_target_pairs={{0,8},{4,12},{8,0},{12,4},{1,9},{5,13},{9,1},{13,5},{2,10},{6,14},... | collective-permute-start | bytes 786440 | tf_op jit(solution)/shard_map/ppermute | solution.py:14
  121.4 25.5 %collective-permute-start.50 = (bf16[128,1024]{1,0:T(8,128)(2,1)}, bf16[128,1024]{1,0:T(8,128)(2,1)S(1)}, u32[]{:S(2)}, u32[]{:S(2)}) collective-permute-start(bf16[128,1024]{1,0:T(8,128)(2,1)} %pad_maximum_fusion.18), channel_id=1, source_target_pairs={{0,12},{4,8},{8,4},{12,0},{1,13},{5,9},{9,5},{13,1},{2,14},{6,10},... | collective-permute-start | bytes 786440 | tf_op jit(solution)/shard_map/ppermute | solution.py:14
  121.9 25.1 %collective-permute-start.51 = (bf16[128,1024]{1,0:T(8,128)(2,1)S(1)}, bf16[128,1024]{1,0:T(8,128)(2,1)S(1)}, u32[]{:S(2)}, u32[]{:S(2)}) collective-permute-start(bf16[128,1024]{1,0:T(8,128)(2,1)S(1)} %pad_maximum_fusion.19), channel_id=1, source_target_pairs={{0,12},{4,8},{8,4},{12,0},{1,13},{5,9},{9,5},{13,1},{2,14},{6,10},... | collective-permute-start | bytes 786440 | tf_op jit(solution)/shard_map/ppermute | solution.py:14
  123.0 49.0 %collective-permute-start.28 = (bf16[128,1024]{1,0:T(8,128)(2,1)S(1)}, bf16[128,1024]{1,0:T(8,128)(2,1)S(1)}, u32[]{:S(2)}, u32[]{:S(2)}) collective-permute-start(bf16[128,1024]{1,0:T(8,128)(2,1)S(1)} %get-tuple-element.50), channel_id=1, source_target_pairs={{0,16},{16,0},{1,17},{17,1},{2,18},{18,2},{3,19},{19,3},{4,20},{20... | collective-permute-start | bytes 786440 | tf_op jit(solution)/shard_map/ppermute | solution.py:14
  142.8 28.3 %collective-permute-start.21 = (bf16[128,1408]{1,0:T(8,128)(2,1)S(1)}, bf16[128,1408]{1,0:T(8,128)(2,1)S(1)}, u32[]{:S(2)}, u32[]{:S(2)}) collective-permute-start(bf16[128,1408]{1,0:T(8,128)(2,1)S(1)} %pad_maximum_fusion.5), channel_id=1, source_target_pairs={{0,16},{16,0},{1,17},{17,1},{2,18},{18,2},{3,19},{19,3},{4,20},{20... | collective-permute-start | bytes 1081352 | tf_op jit(solution)/shard_map/ppermute | solution.py:14
  154.7 12.5 %collective-permute-start.47 = (bf16[32,1408]{1,0:T(8,128)(2,1)S(1)}, bf16[32,1408]{1,0:T(8,128)(2,1)S(1)}, u32[]{:S(2)}, u32[]{:S(2)}) collective-permute-start(bf16[32,1408]{1,0:T(8,128)(2,1)S(1)} %collective-permute-done.45), channel_id=1, source_target_pairs={{0,2},{1,3},{2,0},{3,1},{4,6},{5,7},{6,4},{7,5},{8,10},{9,11},{10,... | collective-permute-start | bytes 270344 | tf_op jit(solution)/shard_map/ppermute | solution.py:14
  155.6 11.8 %collective-permute-start.48 = (bf16[32,1408]{1,0:T(8,128)(2,1)S(1)}, bf16[32,1408]{1,0:T(8,128)(2,1)S(1)}, u32[]{:S(2)}, u32[]{:S(2)}) collective-permute-start(bf16[32,1408]{1,0:T(8,128)(2,1)S(1)} %collective-permute-done.45), channel_id=1, source_target_pairs={{0,3},{1,2},{2,1},{3,0},{4,7},{5,6},{6,5},{7,4},{8,11},{9,10},{10,... | collective-permute-start | bytes 270344 | tf_op jit(solution)/shard_map/ppermute | solution.py:14
  157.6 26.2 %collective-permute-start.36 = (bf16[128,1024]{1,0:T(8,128)(2,1)}, bf16[128,1024]{1,0:T(8,128)(2,1)}, u32[]{:S(2)}, u32[]{:S(2)}) collective-permute-start(bf16[128,1024]{1,0:T(8,128)(2,1)} %get-tuple-element.42), channel_id=1, source_target_pairs={{0,16},{16,0},{1,17},{17,1},{2,18},{18,2},{3,19},{19,3},{4,20},{20... | collective-permute-start | bytes 786440 | tf_op jit(solution)/shard_map/ppermute | solution.py:14
  167.2 22.7 %collective-permute-start.44 = (bf16[128,1024]{1,0:T(8,128)(2,1)}, bf16[128,1024]{1,0:T(8,128)(2,1)}, u32[]{:S(2)}, u32[]{:S(2)}) collective-permute-start(bf16[128,1024]{1,0:T(8,128)(2,1)} %get-tuple-element.40), channel_id=1, source_target_pairs={{0,16},{16,0},{1,17},{17,1},{2,18},{18,2},{3,19},{19,3},{4,20},{20... | collective-permute-start | bytes 786440 | tf_op jit(solution)/shard_map/ppermute | solution.py:14
  167.5 28.3 %collective-permute-start.52 = (bf16[128,1024]{1,0:T(8,128)(2,1)}, bf16[128,1024]{1,0:T(8,128)(2,1)}, u32[]{:S(2)}, u32[]{:S(2)}) collective-permute-start(bf16[128,1024]{1,0:T(8,128)(2,1)} %get-tuple-element.38), channel_id=1, source_target_pairs={{0,16},{16,0},{1,17},{17,1},{2,18},{18,2},{3,19},{19,3},{4,20},{20... | collective-permute-start | bytes 786440 | tf_op jit(solution)/shard_map/ppermute | solution.py:14
  171.1 7.0 %collective-permute-start.49 = (bf16[128,1408]{1,0:T(8,128)(2,1)}, bf16[128,1408]{1,0:T(8,128)(2,1)}, u32[]{:S(2)}, u32[]{:S(2)}) collective-permute-start(bf16[128,1408]{1,0:T(8,128)(2,1)} %pad_maximum_fusion.8), channel_id=1, source_target_pairs={{0,16},{16,0},{1,17},{17,1},{2,18},{18,2},{3,19},{19,3},{4,20},{20... | collective-permute-start | bytes 1081352 | tf_op jit(solution)/shard_map/ppermute | solution.py:14
  172.7 7.4 %collective-permute-start.41 = (bf16[128,1408]{1,0:T(8,128)(2,1)}, bf16[128,1408]{1,0:T(8,128)(2,1)}, u32[]{:S(2)}, u32[]{:S(2)}) collective-permute-start(bf16[128,1408]{1,0:T(8,128)(2,1)} %pad_maximum_fusion.7), channel_id=1, source_target_pairs={{0,16},{16,0},{1,17},{17,1},{2,18},{18,2},{3,19},{19,3},{4,20},{20... | collective-permute-start | bytes 1081352 | tf_op jit(solution)/shard_map/ppermute | solution.py:14
  (61 other events, 403.9 us)

commit v2 on v1

v2 whole, which is shorter than its diff:
```python
import functools

import jax
import jax.numpy as jnp
from jax import lax
from jax.experimental import pallas as pl
from jax.experimental.pallas import tpu as pltpu
from jax.sharding import PartitionSpec as P

EPSILON = 1e-05
BF = jnp.bfloat16
F32 = jnp.float32
SIDE = 128


def flip(value, axis, mask):
    pairs = [(source, source ^ mask) for source in range(lax.axis_size(axis))]
    return lax.ppermute(value, axis, pairs)


def matmul(left, right):
    return jnp.dot(left, right, preferred_element_type=F32)


def matmul_nt(left, right):
    return lax.dot_general(left, right, (((1,), (1,)), ((), ())), preferred_element_type=F32)


def matmul_tn(left, right):
    return lax.dot_general(left, right, (((0,), (0,)), ((), ())), preferred_element_type=F32)


def pack(columns):
    lane = lax.broadcasted_iota(jnp.int32, (columns[0].shape[0], SIDE), 1)
    side = jnp.zeros(lane.shape, F32)
    for place, column in enumerate(columns):
        rest = column
        for part in range(3):
            piece = lax.reduce_precision(rest, 8, 7)
            side = jnp.where(lane == 3 * place + part, piece, side)
            rest = rest - piece
    return side.astype(BF)


def unpack(side, place):
    wide = side[:, 3 * place : 3 * place + 3].astype(F32)
    return wide[:, 0:1] + wide[:, 1:2] + wide[:, 2:3]


VMEM = pl.BlockSpec(memory_space=pltpu.VMEM)
SMEM = pl.BlockSpec(memory_space=pltpu.SMEM)
HBM = pl.BlockSpec(memory_space=pl.ANY)


def call(body, outs, in_specs, scratch=()):
    return pl.pallas_call(
        body,
        out_shape=outs,
        in_specs=in_specs,
        out_specs=jax.tree.map(lambda _: VMEM, outs),
        scratch_shapes=list(scratch),
        compiler_params=pltpu.CompilerParams(vmem_limit_bytes=48 << 20),
    )


def side_of(column):
    lane = lax.broadcasted_iota(jnp.int32, (column.shape[0], SIDE), 1)
    high = column.astype(BF).astype(F32)
    middle = (column - high).astype(BF).astype(F32)
    low = column - high - middle
    zero = jnp.zeros(lane.shape, F32)
    picked = jnp.where(lane == 0, high, jnp.where(lane == 1, middle, jnp.where(lane == 2, low, zero)))
    return picked.astype(BF)


def from_side(side):
    return jnp.sum(side.astype(F32), axis=1, keepdims=True)


def learn_kernel(features, share, where, total, norm, middle, rows, rows_squares, *refs):
    (out_a, out_b, value_a, value_b, lout_a, lout_b) = refs[:6]
    scored, kept, kept_norm = refs[6:9]
    peers, chosen, sent = refs[9:-2], refs[-2], refs[-1]
    first, at = where[0] == 1, where[1]
    values = (total[...] * lax.rsqrt(norm[...] / features + EPSILON)).astype(BF)

    @pl.when(first)
    def _():
        chosen[...] = matmul(values, out_b[...])

    @pl.when(jnp.logical_not(first))
    def _():
        chosen[...] = matmul(values, out_a[...])

    row = rows[...]
    score = (middle[...].astype(F32) + chosen[...]).astype(BF)
    scored[...] = score
    squares = rows_squares[...] + square_sum(score)
    own = jnp.where(first, row, score)
    other = jnp.where(first, score, row)
    inner = value_a.shape[1]
    part = matmul(own, value_a[...]) + matmul(other, value_b[...])
    cross = matmul_nt(own, lout_a[...]) + matmul_nt(other, lout_b[...])
    side = side_of(squares)
    sent[:, :inner] = part
    sent[:, inner : 2 * inner] = cross
    sent[:, 2 * inner :] = side.astype(F32)
    mine = sent[pl.ds(pl.multiple_of(at * share, share), share), :]
    kept[...] = mine[:, : 2 * inner]
    kept_norm[...] = from_side(mine[:, 2 * inner :])
    for place, peer in enumerate(peers):
        start = pl.multiple_of((at ^ (place + 1)) * share, share)
        peer[...] = sent[pl.ds(start, share), :].astype(BF)


def value_kernel(features, block, count, where, kept, norm, *refs):
    got, pieces, crossed = refs[:count], refs[count:-1], refs[-1]
    total, squares = kept[...], norm[...]
    inner = total.shape[1] // 2
    for one in got:
        total = total + one[:, : 2 * inner].astype(F32)
        squares = squares + from_side(one[:, 2 * inner :])
    inverse = lax.rsqrt(squares / features + EPSILON)
    values = (total[:, :inner] * inverse).astype(BF)
    side = side_of(inverse)
    crossed[...] = total[:, inner:].astype(BF)
    for away, piece in enumerate(pieces):
        if len(pieces) == 1:
            cross = crossed[...]
        else:
            cross = crossed[:, pl.ds(pl.multiple_of((where[0] ^ away) * block, block), block)]
        reach = inner + cross.shape[1]
        piece[:, :inner] = values
        piece[:, inner:reach] = cross
        piece[:, reach:] = side


def gradient_kernel(share, peers, dp_size, where, *refs):
    count = 4 * peers
    near, far = refs[:count:2], refs[1:count:2]
    every_row, every_scored, parts, lout, gram, grad_value, grad_out = refs[count : count + 7]
    tokens, x, slopes, normed, back, token_sem, x_sem = refs[count + 7 :]
    first, dp_at, mp_at = where[0] == 1, where[1], where[2]
    keep = share * peers
    width, inner, block = x.shape[1], lout.shape[0], gram.shape[1]
    piece = inner + block + SIDE

    def x_copy(source):
        return pltpu.make_async_copy(source, x, x_sem)

    @pl.when(first)
    def _():
        x_copy(every_row.at[:, pl.ds(0, width)]).start()

    @pl.when(jnp.logical_not(first))
    def _():
        x_copy(every_scored).start()

    copies = []
    for side, group in enumerate((near, far)):
        segment = jnp.where(first, side, 1 - side)
        for mask in range(peers):
            own, rest = group[mask], group[peers + mask]
            for away in range(dp_size):
                source = own if away == 0 else rest.at[:, pl.ds((away - 1) * piece, piece)]
                start = ((segment * dp_size + (dp_at ^ away)) * peers + (mp_at ^ mask)) * share
                target = tokens.at[pl.ds(pl.multiple_of(start, share), share), :]
                copy = pltpu.make_async_copy(source, target, token_sem.at[len(copies)])
                copy.start()
                copies.append(copy)
    for copy in copies:
        copy.wait()
    x_copy(every_scored).wait()
    step = 2 * keep
    for at in range(0, tokens.shape[0], step):
        here = pl.ds(at, step)
        wide = x[here, :].astype(F32)
        values = tokens[here, :inner]
        share_count = parts[here, :]
        inverse = from_side(tokens[here, inner + block :])
        slopes[here, :] = ((wide + matmul(values, lout[...])) * share_count).astype(BF)
        normed[here, :] = (wide * inverse).astype(BF)
        crossed = tokens[here, inner : inner + block].astype(F32)
        back[here, :] = ((crossed + matmul(values, gram[...])) * share_count).astype(BF)
    grad_value[...] = matmul_tn(back[...], normed[...])
    column = pl.multiple_of(dp_at * block, block)
    grad_out[...] = matmul_tn(tokens[:, pl.ds(column, block)], slopes[...])


def square_sum(value):
    wide = value.astype(F32)
    return jnp.sum(wide * wide, axis=1, keepdims=True)


def exchange(first, second, first_mask, second_mask):
    first, second = lax.optimization_barrier((first, second))
    return lax.optimization_barrier(
        (flip(first, "mp", first_mask), flip(second, "mp", second_mask))
    )


def reduce_rows(partial, squares):
    half = partial.shape[0] // 2
    width = partial.shape[1]

    def sent(part, norm):
        return jnp.concatenate([part.astype(BF), pack([norm])], axis=1)

    top, low = (partial[:half], squares[:half]), (partial[half:], squares[half:])
    for top_mask, low_mask in ((1, 2), (2, 1)):
        got = exchange(sent(*top), sent(*low), top_mask, low_mask)
        top, low = (
            (part + new[:, :width].astype(F32), norm + unpack(new[:, width:], 0))
            for (part, norm), new in zip((top, low), got)
        )
    return (
        jnp.concatenate([top[0], low[0]], axis=0),
        jnp.concatenate([top[1], low[1]], axis=0),
    )


def on_device(
    candidates,
    scorer_value,
    scorer_out,
    learner_value,
    learner_out,
    keep_index,
    keep_dest,
    keep_count,
):
    first = lax.axis_index("segment") == 0
    dp_at = lax.axis_index("dp")
    mp_at = lax.axis_index("mp")
    dp_size = lax.axis_size("dp")
    mp_size = lax.axis_size("mp")
    keep = keep_index.shape[1]
    width = candidates.shape[1]
    scorer_width = width * mp_size
    learner_width = 2 * scorer_width
    inner = learner_value.shape[2]
    block = inner // dp_size
    share = keep // mp_size

    own_value, own_out = scorer_value[0], scorer_out[0]
    own_lvalue, own_lout = learner_value[0], learner_out[0]
    other_value = flip(own_value, "segment", 1)
    other_out = flip(own_out, "segment", 1)
    other_lvalue = flip(own_lvalue, "segment", 1)
    other_lout = flip(own_lout, "segment", 1)

    is_live = jnp.arange(keep) < keep_count[0]
    pick = (keep_index[0][:, None] == jnp.arange(candidates.shape[0])[None, :]) & is_live[:, None]
    rows = matmul(pick.astype(BF), candidates).astype(BF)
    goal = jnp.where(is_live, keep_dest[0] + 1, 0).astype(F32)[:, None]
    every_row = lax.all_gather(
        jnp.concatenate([rows, jnp.broadcast_to(goal, (keep, SIDE)).astype(BF)], axis=1),
        ("segment", "dp"),
        axis=0,
        tiled=False,
    )

    gram = matmul_nt(own_lout, lax.dynamic_slice_in_dim(own_lout, dp_at * block, block, 0))
    half = inner // 2
    at = lax.axis_index("segment")
    kept_half = lax.dynamic_slice_in_dim(gram, at * half, half, 0)
    sent_half = lax.dynamic_slice_in_dim(gram, (1 - at) * half, half, 0)
    half_sum = (kept_half + flip(sent_half.astype(BF), "segment", 1).astype(F32)).astype(BF)
    gram_parts = lax.all_gather(half_sum, "mp", axis=0, tiled=False)

    rows_squares = square_sum(rows)
    nothing = jnp.zeros_like(rows)
    partial = matmul(jnp.where(first, rows, nothing), own_value) + matmul(
        jnp.where(first, nothing, rows), other_value
    )
    total, norm = reduce_rows(partial, rows_squares)
    inverse = lax.rsqrt(norm / scorer_width + EPSILON)
    values = (total * inverse).astype(BF)
    w_out = lax.optimization_barrier(jnp.where(first, own_out, other_out))
    middle = (rows.astype(F32) + matmul(values, w_out)).astype(BF)
    w_value = lax.optimization_barrier(jnp.where(first, other_value, own_value))
    total, norm = reduce_rows(matmul(middle, w_value), square_sum(middle))
    total, every_row = lax.optimization_barrier((total, every_row))

    flag = first.astype(jnp.int32)
    long = 2 * inner + SIDE
    outs = call(
        functools.partial(learn_kernel, scorer_width, share),
        [
            jax.ShapeDtypeStruct((keep, width), BF),
            jax.ShapeDtypeStruct((share, 2 * inner), F32),
            jax.ShapeDtypeStruct((share, 1), F32),
        ]
        + [jax.ShapeDtypeStruct((share, long), BF)] * (mp_size - 1),
        [SMEM] + [VMEM] * 11,
        [pltpu.VMEM((keep, width), F32), pltpu.VMEM((keep, long), F32)],
    )(
        jnp.stack([flag, mp_at]),
        total,
        norm,
        middle,
        rows,
        rows_squares,
        own_out,
        other_out,
        own_lvalue,
        other_lvalue,
        own_lout,
        other_lout,
    )
    scored, kept, kept_norm = outs[:3]
    every_scored = lax.all_gather(scored, ("segment", "dp"), axis=0, tiled=False)
    got = lax.optimization_barrier(
        tuple(flip(peer, "mp", mask) for mask, peer in enumerate(outs[3:], 1))
    )
    direct = dp_size <= 8 and block % SIDE == 0
    pieces = call(
        functools.partial(value_kernel, learner_width, block, mp_size - 1),
        [jax.ShapeDtypeStruct((share, inner + block + SIDE), BF)] * dp_size
        if direct
        else [jax.ShapeDtypeStruct((share, long), BF)],
        [SMEM] + [VMEM] * (mp_size + 1),
        [pltpu.VMEM((share, inner), BF)],
    )(jnp.stack([dp_at]), kept, kept_norm, *got)

    gram_half = jnp.sum(gram_parts.astype(F32), axis=0).astype(BF)
    gram_other = flip(gram_half, "segment", 1)
    gram = jnp.where(
        first,
        jnp.concatenate([gram_half, gram_other], axis=0),
        jnp.concatenate([gram_other, gram_half], axis=0),
    )

    goals = every_row[:, :, width].astype(jnp.int32).reshape(2, dp_size, keep)
    hits = goals[:, :, :, None] == jnp.arange(1, dp_size + 1)
    counts = jnp.sum(hits.astype(F32), axis=(1, 2), keepdims=True)
    parts = 1.0 / jnp.maximum(jnp.sum(jnp.where(hits, counts, 0.0), axis=3), 1.0)
    column = dp_at * block

    def spread(piece):
        whole = jnp.zeros((keep, piece.shape[1]), BF)
        for mask in range(mp_size):
            got = flip(piece, "mp", mask) if mask else piece
            whole = lax.dynamic_update_slice(whole, got, ((mp_at ^ mask) * share, 0))
        return whole

    def add(grads, pieces, places):
        pieces = jnp.concatenate(pieces, axis=0)
        tokens = jnp.concatenate([pieces, flip(pieces, "segment", 1)], axis=0)
        x, share_count = [], []
        for segment in (at, 1 - at):
            for place in places:
                row = lax.dynamic_index_in_dim(every_row, segment * dp_size + place, 0, False)
                score = lax.dynamic_index_in_dim(every_scored, segment * dp_size + place, 0, False)
                x.append(jnp.where(first, row[:, :width], score))
                share_count.append(lax.dynamic_slice(parts, (segment, place, 0), (1, 1, keep)))
        x = jnp.concatenate(x, axis=0).astype(F32)
        share_count = jnp.concatenate([part.reshape(keep, 1) for part in share_count], axis=0)
        v = tokens[:, :inner]
        xo = tokens[:, inner : inner + block].astype(F32)
        inv = unpack(tokens[:, inner + block :], 0)
        slopes = ((x + matmul(v, own_lout)) * share_count).astype(BF)
        normed = (x * inv).astype(BF)
        back = ((xo + matmul(v, gram)) * share_count).astype(BF)
        v_block = lax.dynamic_slice_in_dim(v, column, block, 1)
        return (grads[0] + matmul_tn(back, normed), grads[1] + matmul_tn(v_block, slopes))

    if direct:
        moved = [flip(pieces[away], "dp", away) for away in range(1, dp_size)]
        rest = jnp.concatenate(lax.optimization_barrier(tuple(moved)), axis=1)
        groups = []
        for piece in (pieces[0], rest):
            for mask in range(mp_size):
                near = flip(piece, "mp", mask) if mask else piece
                groups += [near, flip(near, "segment", 1)]
        tokens = 2 * dp_size * keep
        grads = call(
            functools.partial(gradient_kernel, share, mp_size, dp_size),
            [jax.ShapeDtypeStruct((block, width), F32)] * 2,
            [SMEM] + [HBM] * (len(groups) + 2) + [VMEM] * 3,
            [
                pltpu.VMEM((tokens, inner + block + SIDE), BF),
                pltpu.VMEM((tokens, width), BF),
                pltpu.VMEM((tokens, width), BF),
                pltpu.VMEM((tokens, width), BF),
                pltpu.VMEM((tokens, block), BF),
                pltpu.SemaphoreType.DMA((tokens // share,)),
                pltpu.SemaphoreType.DMA,
            ],
        )(
            jnp.stack([flag, dp_at, mp_at]),
            *groups,
            every_row.reshape(tokens, width + SIDE),
            every_scored.reshape(tokens, width),
            parts.reshape(tokens, 1),
            own_lout,
            gram,
        )
    else:
        ring = [(source, (source + 1) % dp_size) for source in range(dp_size)]

        def turn(step, carry):
            grads, full = carry
            cross = lax.dynamic_slice_in_dim(full, inner + column, block, 1)
            piece = jnp.concatenate([full[:, :inner], cross, full[:, 2 * inner :]], axis=1)
            grads = add(grads, [spread(piece)], [(dp_at - step) % dp_size])
            return grads, lax.ppermute(full, "dp", ring)

        grads = (jnp.zeros((block, width), F32), jnp.zeros((block, width), F32))
        grads, _ = lax.fori_loop(0, dp_size, turn, (grads, pieces[0]))
    return (grads[0][None], grads[1][None])


def solution(mesh):
    placed = (
        P(("segment", "dp"), "mp"),
        P("segment", "mp", None),
        P("segment", None, "mp"),
        P("segment", "mp", None),
        P("segment", None, "mp"),
        P(("segment", "dp"), None),
        P(("segment", "dp"), None),
        P(("segment", "dp")),
    )
    return jax.shard_map(
        on_device,
        mesh=mesh,
        in_specs=placed,
        out_specs=(P("segment", "dp", "mp"), P("segment", "dp", "mp")),
        check_vma=False,
    )
```

time: 210 us -> 152 us (0.72)
  matrix products: 43.3 us -> 7.89 us
  starting transfers between devices: 74.6 us -> 43.4 us
  waiting for transfers between devices: 43.7 us -> 23.9 us
  Pallas kernels: 0 us -> 16.9 us
  between operations: 2.34 us -> 14.9 us
  local copies, waits for them, and re-layouts: 13 us -> 24.4 us
  other arithmetic: 30.2 us -> 19.3 us
    ppermute x53 -> x34, starting transfers between devices: 74.6 us -> 43.2 us  [flip(): return lax.ppermute(value, axis, pairs)]
    dot_general x8 -> x0, matrix products: 26.2 us -> none  [matmul_tn(): lax.dot_general(left, right, (((0,), (0,)), ((), ())), preferred_element_...]
    ppermute x53 -> x34, waiting for transfers between devices: 43.7 us -> 23.8 us  [flip(): return lax.ppermute(value, axis, pairs)]
    pallas_call x0 -> x3, Pallas kernels: none -> 16.9 us  [the longest x1 9.65 us: on_device(): call(functools.partial(gradient_kernel, share, mp_size, dp_size), [jax.Sh...]
    unnamed x79 -> x46, local copies, waits for them, and re-layouts: 3.14 us -> 13.8 us
    dot_general x3 -> x1, matrix products: 8.45 us -> 2.51 us  [matmul_nt(): lax.dot_general(left, right, (((1,), (1,)), ((), ())), preferred_element_...]
    select_n x4 -> x0, other arithmetic: 4.58 us -> none  [add(): near = jnp.where(first, near_rows, near_scored)]
    optimization_barrier x0 -> x1, local copies, waits for them, and re-layouts: none -> 4.5 us  [on_device(): total, every_row = lax.optimization_barrier((total, every_row))]
  transfers between devices with their start and end apart: 53 -> 37, of which waited for: 19 -> 11; matrix products, arithmetic and copies ran while one was open for 33% -> 23% of each run, Pallas kernels for 0% -> 5%
where the time goes in v2:
time: 152 us; the launch traced here: 151 us
  starting transfers between devices  43.4 us (29%)
  local copies, waits for them, and re-layouts  24.4 us (16%)
  waiting for transfers between devices  23.9 us (16%)
  other arithmetic  19.3 us (13%)
  Pallas kernels  16.9 us (11%)
  between operations  14.9 us (10%)
  matrix products  7.89 us (5%)
    ppermute x34, starting transfers between devices, flip(): return lax.ppermute(value, axis, pairs)  43.2 us
    ppermute x34, waiting for transfers between devices, flip(): return lax.ppermute(value, axis, pairs)  23.8 us
    unnamed x46, local copies, waits for them, and re-layouts  13.8 us
    pallas_call x1, Pallas kernels, on_device(): call(functools.partial(gradient_kernel, share, mp_size, dp_size), [jax.Sh...  9.65 us
    pallas_call x1, Pallas kernels, on_device(): call(functools.partial(learn_kernel, scorer_width, share), [jax.ShapeDtyp...  7.02 us
    dot_general x5, matrix products, matmul(): return jnp.dot(left, right, preferred_element_type=F32)  5.38 us
    optimization_barrier x1, local copies, waits for them, and re-layouts, on_device(): total, every_row = lax.optimization_barrier((total, every_row))  4.5 us
  transfers between devices with their start and end apart: 37, of which 11 were waited for; matrix products, arithmetic and copies ran while one was open for 23% of the time, Pallas kernels for 5%

profile of v2, /device:TPU:11, one launch (start us, length us, event | category | flops | bytes accessed | tf_op | source)
XLA Modules:
  0.0 150.6 jit_solution(5407311963659029057)
XLA Ops:
  11.9 2.5 %fusion.4 = f32[256,1024]{1,0:T(8,128)S(1)} fusion(bf16[1,1024,1024]{2,1,0:T(8,128)(2,1)} %param.12, s32[]{:T(128)S(6)} %select_n.159), kind=kOutput, calls=%fused_computation.14 | convolution fusion | flops 536870912 | bytes 3670020 | tf_op jit(solution)/shard_map/dot_general | solution.py:26
  17.5 7.7 %collective-permute-done.32 = bf16[512,256]{0,1:T(8,128)(2,1)} collective-permute-done((bf16[512,256]{0,1:T(8,128)(2,1)}, bf16[512,256]{0,1:T(8,128)(2,1)}, u32[]{:S(2)}, u32[]{:S(2)}) %collective-permute-start.32) | collective-permute-done | bytes 262176 | tf_op jit(solution)/shard_map/ppermute | solution.py:18
  25.2 1.7 %fusion.3 = bf16[512,256]{0,1:T(8,128)(2,1)} fusion(bf16[512,256]{0,1:T(8,128)(2,1)} %collective-permute-done.32, f32[256,1024]{1,0:T(8,128)S(1)} %copy-done.21, s32[]{:T(128)S(6)} %select_n.160), kind=kLoop, calls=%fused_computation.13 | loop fusion | flops 393216 | bytes 1048580 | tf_op jit(solution)/shard_map/convert_element_type | solution.py:268
  27.0 2.1 %convolution_add_fusion.1 = f32[128,1024]{1,0:T(8,128)S(1)} fusion(f32[128,1024]{1,0:T(8,128)S(1)} %fusion.11, bf16[1024,1024]{1,0:T(8,128)(2,1)} %collective-permute-done, bf16[128,1024]{1,0:T(8,128)(2,1)S(1)} %get-tuple-element.127.rows, pred[]{:T(512)S(6)} %eq.106), kind=kOutput, calls=%fused_computation.3 | convolution fusion | flops 268697600 | bytes 3407873 | tf_op jit(solution)/shard_map/dot_general | solution.py:22
  31.0 3.4 %collective-permute-done.1 = bf16[64,1152]{1,0:T(8,128)(2,1)S(1)} collective-permute-done((bf16[64,1152]{1,0:T(8,128)(2,1)S(1)}, bf16[64,1152]{1,0:T(8,128)(2,1)S(1)}, u32[]{:S(2)}, u32[]{:S(2)}) %collective-permute-start.1) | collective-permute-done | bytes 147488 | tf_op jit(solution)/shard_map/ppermute | solution.py:18
  37.6 1.8 %broadcast_select_fusion.1 = bf16[1024,1024]{1,0:T(8,128)(2,1)S(1)} fusion(bf16[1024,1024]{1,0:T(8,128)(2,1)} %collective-permute-done.5.refs_1_, pred[]{:T(512)S(6)} %eq.106, bf16[1,1024,1024]{2,1,0:T(8,128)(2,1)S(1)} %copy-done.1), kind=kLoop, calls=%fused_computation.1 | loop fusion | flops 1048576 | bytes 6291457 | tf_op jit(solution)/shard_map/jit(_where)/select_n | solution.py:279
  45.7 1.3 collective-permute-start.6
  47.3 2.6 %collective-permute-done.6 = bf16[64,1152]{1,0:T(8,128)(2,1)S(1)} collective-permute-done((bf16[64,1152]{1,0:T(8,128)(2,1)}, bf16[64,1152]{1,0:T(8,128)(2,1)S(1)}, u32[]{:S(2)}, u32[]{:S(2)}) %collective-permute-start.6) | collective-permute-done | bytes 147488 | tf_op jit(solution)/shard_map/ppermute | solution.py:18
  49.9 1.5 collective-permute-done.7
  56.3 3.1 %collective-permute-done.8 = bf16[64,1152]{1,0:T(8,128)(2,1)} collective-permute-done((bf16[64,1152]{1,0:T(8,128)(2,1)}, bf16[64,1152]{1,0:T(8,128)(2,1)}, u32[]{:S(2)}, u32[]{:S(2)}) %collective-permute-start.8) | collective-permute-done | bytes 147488 | tf_op jit(solution)/shard_map/ppermute | solution.py:18
  64.9 7.0 %shard_map.95 = (bf16[128,1024]{1,0:T(8,128)(2,1)}, f32[32,2048]{1,0:T(8,128)S(1)}, f32[32,1]{1,0:T(8,128)S(1)}, bf16[32,2176]{1,0:T(8,128)(2,1)S(1)}, bf16[32,2...) custom-call(s32[2]{0:T(128)S(1)} %copy-done.15, f32[128,1024]{1,0:T(8,128)S(1)} %copy-done.3, ...), custom_call_target="tpu_custom_call" | custom-call | tf_op jit(solution)/shard_map/pallas_call | solution.py:287
  76.6 1.5 collective-permute-done.12.refs_0_
  78.6 2.2 %collective-permute-done.14.refs_2_ = bf16[32,2176]{1,0:T(8,128)(2,1)S(1)} collective-permute-done((bf16[32,2176]{1,0:T(8,128)(2,1)}, bf16[32,2176]{1,0:T(8,128)(2,1)S(1)}, u32[]{:S(2)}, u32[]{:S(2)}) %collective-permute-start.14) | collective-permute-done | bytes 139296 | tf_op jit(solution)/shard_map/ppermute | solution.py:18
  81.2 2.4 %collective-permute-start.23 = (bf16[32,1408]{1,0:T(8,128)(2,1)S(1)}, bf16[32,1408]{1,0:T(8,128)(2,1)S(1)}, u32[]{:S(2)}, u32[]{:S(2)}) collective-permute-start(bf16[32,1408]{1,0:T(8,128)(2,1)S(1)} %get-tuple-element.65), channel_id=1, source_target_pairs={{0,8},{4,12},{8,0},{12,4},{1,9},{5,13},{9,1},{13,5},{2,10},{6,14},... | collective-permute-start | bytes 270344 | tf_op jit(solution)/shard_map/ppermute | solution.py:18
  84.3 1.8 %reshape.121 = bf16[4,512,256]{1,0,2:T(4,128)(2,1)S(1)} reshape(bf16[2048,256]{0,1:T(8,128)(2,1)} %all-gather.11.cloned.1.call-done) | data formatting | bytes 2097152 | tf_op jit(solution)/shard_map/all_gather | solution.py:269
  86.1 1.4 reduce_sum.52
  87.7 7.9 %collective-permute-start.33 = (bf16[512,256]{1,0:T(8,128)(2,1)S(1)}, bf16[512,256]{1,0:T(8,128)(2,1)S(1)}, u32[]{:S(2)}, u32[]{:S(2)}) collective-permute-start(bf16[512,256]{1,0:T(8,128)(2,1)S(1)} %copy.42), channel_id=1, source_target_pairs={{0,16},{16,0},{1,17},{17,1},{2,18},{18,2},{3,19},{19,3},{4,20},{20... | collective-permute-start | bytes 786440 | tf_op jit(solution)/shard_map/ppermute | solution.py:18
  95.7 1.7 %collective-permute-start.26 = (bf16[32,4224]{1,0:T(8,128)(2,1)S(1)}, bf16[32,4224]{1,0:T(8,128)(2,1)S(1)}, u32[]{:S(2)}, u32[]{:S(2)}) collective-permute-start(bf16[32,4224]{1,0:T(8,128)(2,1)S(1)} %constant_dynamic-update-slice_fusion.refs_8_), channel_id=1, source_target_pairs={{0,1},{1,0},{2,3},{3,2},{4,5},{5,4},{6,7},{7,6},{8,9},{9,8},{10,11... | collective-permute-start | bytes 811016 | tf_op jit(solution)/shard_map/ppermute | solution.py:18
  98.7 1.4 collective-permute-start.16
  100.7 4.5 %copy.40 = bf16[8,128,1152]{1,0,2:T(8,128)(2,1)} copy(bf16[8,128,1152]{2,1,0:T(8,128)(2,1)} %bitcast.57) | data formatting | bytes 4718592 | tf_op jit(solution)/shard_map/optimization_barrier | solution.py:283
  107.1 11.9 %collective-permute-start.17 = (bf16[32,1408]{1,0:T(8,128)(2,1)S(1)}, bf16[32,1408]{1,0:T(8,128)(2,1)S(1)}, u32[]{:S(2)}, u32[]{:S(2)}) collective-permute-start(bf16[32,1408]{1,0:T(8,128)(2,1)S(1)} %collective-permute-done.16.refs_2_), channel_id=1, source_target_pairs={{0,16},{16,0},{1,17},{17,1},{2,18},{18,2},{3,19},{19,3},{4,20},{20... | collective-permute-start | bytes 270344 | tf_op jit(solution)/shard_map/ppermute | solution.py:18
  119.8 3.2 %collective-permute-start.25 = (bf16[32,4224]{1,0:T(8,128)(2,1)S(1)}, bf16[32,4224]{1,0:T(8,128)(2,1)S(1)}, u32[]{:S(2)}, u32[]{:S(2)}) collective-permute-start(bf16[32,4224]{1,0:T(8,128)(2,1)S(1)} %constant_dynamic-update-slice_fusion.refs_8_), channel_id=1, source_target_pairs={{0,16},{16,0},{1,17},{17,1},{2,18},{18,2},{3,19},{19,3},{4,20},{20... | collective-permute-start | bytes 811016 | tf_op jit(solution)/shard_map/ppermute | solution.py:18
  127.7 1.6 %copy-done.2 = bf16[1024,1024]{1,0:T(8,128)(2,1)S(1)} copy-done((bf16[1024,1024]{1,0:T(8,128)(2,1)S(1)}, bf16[1024,1024]{1,0:T(8,128)(2,1)}, u32[]{:S(2)}) %copy-start.2) | copy-done | bytes 2097176
  134.4 9.6 %shard_map.97 = (f32[256,1024]{1,0:T(8,128)}, f32[256,1024]{1,0:T(8,128)}) custom-call(s32[3]{0:T(128)S(1)} %copy-done.14, bf16[32,1408]{1,0:T(8,128)(2,1)S(1)} %copy-done.5, bf16[32,1408]{1,0:T(8,128)(2,1)S(1)} %collective-permute-done.15.refs_1_, bf16[32,1408]{1,0:T(8,128)(2,1)S(1)} %copy-done.7, bf16[32,1408]{1,0:T(8,128)(2,1)S(1)} %copy-done.11, ...), custom_call_target="tpu_custom_call" | custom-call | tf_op jit(solution)/shard_map/pallas_call | solution.py:377
  (179 shorter events, 49.8 us)
Async XLA Ops:
  7.2 56.0 %all-gather.7.cloned.1.call-start = ((), (), s32[]{:S(2)}) async-start(), calls=%async_computation | async-start | bytes 2654208 | tf_op jit(solution)/shard_map/all_gather | solution.py:256
  10.5 73.8 %all-gather.11.cloned.1.call-start = ((), (), s32[]{:S(2)}) async-start(), calls=%async_computation.2 | async-start | bytes 1310720 | tf_op jit(solution)/shard_map/all_gather | solution.py:269
  10.5 16.5 %collective-permute-start = (bf16[1024,1024]{1,0:T(8,128)(2,1)}, bf16[1024,1024]{1,0:T(8,128)(2,1)}, u32[]{:S(2)}, u32[]{:S(2)}) collective-permute-start(bf16[1024,1024]{1,0:T(8,128)(2,1)} %bitcast.58), channel_id=1, source_target_pairs={{0,16},{16,0},{1,17},{17,1},{2,18},{18,2},{3,19},{19,3},{4,20},{20... | collective-permute-start | bytes 6291464 | tf_op jit(solution)/shard_map/ppermute | solution.py:18
  11.3 26.3 %collective-permute-start.5 = (bf16[1024,1024]{1,0:T(8,128)(2,1)}, bf16[1024,1024]{1,0:T(8,128)(2,1)}, u32[]{:S(2)}, u32[]{:S(2)}) collective-permute-start(bf16[1024,1024]{1,0:T(8,128)(2,1)} %bitcast.55), channel_id=1, source_target_pairs={{0,16},{16,0},{1,17},{17,1},{2,18},{18,2},{3,19},{19,3},{4,20},{20... | collective-permute-start | bytes 6291464 | tf_op jit(solution)/shard_map/ppermute | solution.py:18
  11.4 51.9 %collective-permute-start.10 = (bf16[1024,1024]{1,0:T(8,128)(2,1)}, bf16[1024,1024]{1,0:T(8,128)(2,1)}, u32[]{:S(2)}, u32[]{:S(2)}) collective-permute-start(bf16[1024,1024]{1,0:T(8,128)(2,1)} %bitcast.62), channel_id=1, source_target_pairs={{0,16},{16,0},{1,17},{17,1},{2,18},{18,2},{3,19},{19,3},{4,20},{20... | collective-permute-start | bytes 6291464 | tf_op jit(solution)/shard_map/ppermute | solution.py:18
  11.8 51.4 %collective-permute-start.11 = (bf16[1024,1024]{1,0:T(8,128)(2,1)}, bf16[1024,1024]{1,0:T(8,128)(2,1)}, u32[]{:S(2)}, u32[]{:S(2)}) collective-permute-start(bf16[1024,1024]{1,0:T(8,128)(2,1)} %bitcast.59), channel_id=1, source_target_pairs={{0,16},{16,0},{1,17},{17,1},{2,18},{18,2},{3,19},{19,3},{4,20},{20... | collective-permute-start | bytes 6291464 | tf_op jit(solution)/shard_map/ppermute | solution.py:18
  16.1 9.1 %collective-permute-start.32 = (bf16[512,256]{0,1:T(8,128)(2,1)}, bf16[512,256]{0,1:T(8,128)(2,1)}, u32[]{:S(2)}, u32[]{:S(2)}) collective-permute-start(bf16[512,256]{0,1:T(8,128)(2,1)} %fusion.7), channel_id=1, source_target_pairs={{0,16},{16,0},{1,17},{17,1},{2,18},{18,2},{3,19},{19,3},{4,20},{20... | collective-permute-start | bytes 786440 | tf_op jit(solution)/shard_map/ppermute | solution.py:18
  27.0 100.7 %all-gather.9.cloned.1.call-start = ((), (), s32[]{:S(2)}) async-start(), calls=%async_computation.1 | async-start | bytes 2359296 | tf_op jit(solution)/shard_map/all_gather | solution.py:312
  29.2 5.2 %collective-permute-start.1 = (bf16[64,1152]{1,0:T(8,128)(2,1)S(1)}, bf16[64,1152]{1,0:T(8,128)(2,1)S(1)}, u32[]{:S(2)}, u32[]{:S(2)}) collective-permute-start(bf16[64,1152]{1,0:T(8,128)(2,1)S(1)} %get-tuple-element.38), channel_id=1, source_target_pairs={{0,1},{1,0},{2,3},{3,2},{4,5},{5,4},{6,7},{7,6},{8,9},{9,8},{10,11... | collective-permute-start | bytes 442376 | tf_op jit(solution)/shard_map/ppermute | solution.py:18
  29.5 4.9 %collective-permute-start.2 = (bf16[64,1152]{1,0:T(8,128)(2,1)S(1)}, bf16[64,1152]{1,0:T(8,128)(2,1)S(1)}, u32[]{:S(2)}, u32[]{:S(2)}) collective-permute-start(bf16[64,1152]{1,0:T(8,128)(2,1)S(1)} %get-tuple-element.39), channel_id=1, source_target_pairs={{0,2},{1,3},{2,0},{3,1},{4,6},{5,7},{6,4},{7,5},{8,10},{9,11},{10,... | collective-permute-start | bytes 442376 | tf_op jit(solution)/shard_map/ppermute | solution.py:18
  75.5 5.2 %collective-permute-start.14 = (bf16[32,2176]{1,0:T(8,128)(2,1)}, bf16[32,2176]{1,0:T(8,128)(2,1)S(1)}, u32[]{:S(2)}, u32[]{:S(2)}) collective-permute-start(bf16[32,2176]{1,0:T(8,128)(2,1)} %copy-done.16), channel_id=1, source_target_pairs={{0,3},{1,2},{2,1},{3,0},{4,7},{5,6},{6,5},{7,4},{8,11},{9,10},{10,... | collective-permute-start | bytes 417800 | tf_op jit(solution)/shard_map/ppermute | solution.py:18
  81.0 14.7 %collective-permute-start.22 = (bf16[32,1408]{1,0:T(8,128)(2,1)S(1)}, bf16[32,1408]{1,0:T(8,128)(2,1)S(1)}, u32[]{:S(2)}, u32[]{:S(2)}) collective-permute-start(bf16[32,1408]{1,0:T(8,128)(2,1)S(1)} %get-tuple-element.64), channel_id=1, source_target_pairs={{0,4},{4,0},{8,12},{12,8},{1,5},{5,1},{9,13},{13,9},{2,6},{6,2},{1... | collective-permute-start | bytes 270344 | tf_op jit(solution)/shard_map/ppermute | solution.py:18
  81.2 14.5 %collective-permute-start.23 = (bf16[32,1408]{1,0:T(8,128)(2,1)S(1)}, bf16[32,1408]{1,0:T(8,128)(2,1)S(1)}, u32[]{:S(2)}, u32[]{:S(2)}) collective-permute-start(bf16[32,1408]{1,0:T(8,128)(2,1)S(1)} %get-tuple-element.65), channel_id=1, source_target_pairs={{0,8},{4,12},{8,0},{12,4},{1,9},{5,13},{9,1},{13,5},{2,10},{6,14},... | collective-permute-start | bytes 270344 | tf_op jit(solution)/shard_map/ppermute | solution.py:18
  83.5 12.1 %collective-permute-start.24 = (bf16[32,1408]{1,0:T(8,128)(2,1)S(1)}, bf16[32,1408]{1,0:T(8,128)(2,1)S(1)}, u32[]{:S(2)}, u32[]{:S(2)}) collective-permute-start(bf16[32,1408]{1,0:T(8,128)(2,1)S(1)} %get-tuple-element.66), channel_id=1, source_target_pairs={{0,12},{4,8},{8,4},{12,0},{1,13},{5,9},{9,5},{13,1},{2,14},{6,10},... | collective-permute-start | bytes 270344 | tf_op jit(solution)/shard_map/ppermute | solution.py:18
  87.7 11.1 %collective-permute-start.33 = (bf16[512,256]{1,0:T(8,128)(2,1)S(1)}, bf16[512,256]{1,0:T(8,128)(2,1)S(1)}, u32[]{:S(2)}, u32[]{:S(2)}) collective-permute-start(bf16[512,256]{1,0:T(8,128)(2,1)S(1)} %copy.42), channel_id=1, source_target_pairs={{0,16},{16,0},{1,17},{17,1},{2,18},{18,2},{3,19},{19,3},{4,20},{20... | collective-permute-start | bytes 786440 | tf_op jit(solution)/shard_map/ppermute | solution.py:18
  95.6 4.5 %collective-permute-start.15 = (bf16[32,1408]{1,0:T(8,128)(2,1)S(1)}, bf16[32,1408]{1,0:T(8,128)(2,1)S(1)}, u32[]{:S(2)}, u32[]{:S(2)}) collective-permute-start(bf16[32,1408]{1,0:T(8,128)(2,1)S(1)} %get-tuple-element.63.refs_0_), channel_id=1, source_target_pairs={{0,16},{16,0},{1,17},{17,1},{2,18},{18,2},{3,19},{19,3},{4,20},{20... | collective-permute-start | bytes 270344 | tf_op jit(solution)/shard_map/ppermute | solution.py:18
  95.7 28.5 %collective-permute-start.26 = (bf16[32,4224]{1,0:T(8,128)(2,1)S(1)}, bf16[32,4224]{1,0:T(8,128)(2,1)S(1)}, u32[]{:S(2)}, u32[]{:S(2)}) collective-permute-start(bf16[32,4224]{1,0:T(8,128)(2,1)S(1)} %constant_dynamic-update-slice_fusion.refs_8_), channel_id=1, source_target_pairs={{0,1},{1,0},{2,3},{3,2},{4,5},{5,4},{6,7},{7,6},{8,9},{9,8},{10,11... | collective-permute-start | bytes 811016 | tf_op jit(solution)/shard_map/ppermute | solution.py:18
  97.4 27.3 %collective-permute-start.28 = (bf16[32,4224]{1,0:T(8,128)(2,1)S(1)}, bf16[32,4224]{1,0:T(8,128)(2,1)S(1)}, u32[]{:S(2)}, u32[]{:S(2)}) collective-permute-start(bf16[32,4224]{1,0:T(8,128)(2,1)S(1)} %constant_dynamic-update-slice_fusion.refs_8_), channel_id=1, source_target_pairs={{0,2},{1,3},{2,0},{3,1},{4,6},{5,7},{6,4},{7,5},{8,10},{9,11},{10,... | collective-permute-start | bytes 811016 | tf_op jit(solution)/shard_map/ppermute | solution.py:18
  97.8 27.1 %collective-permute-start.30 = (bf16[32,4224]{1,0:T(8,128)(2,1)S(1)}, bf16[32,4224]{1,0:T(8,128)(2,1)S(1)}, u32[]{:S(2)}, u32[]{:S(2)}) collective-permute-start(bf16[32,4224]{1,0:T(8,128)(2,1)S(1)} %constant_dynamic-update-slice_fusion.refs_8_), channel_id=1, source_target_pairs={{0,3},{1,2},{2,1},{3,0},{4,7},{5,6},{6,5},{7,4},{8,11},{9,10},{10,... | collective-permute-start | bytes 811016 | tf_op jit(solution)/shard_map/ppermute | solution.py:18
  98.7 7.1 %collective-permute-start.16 = (bf16[32,1408]{1,0:T(8,128)(2,1)S(1)}, bf16[32,1408]{1,0:T(8,128)(2,1)S(1)}, u32[]{:S(2)}, u32[]{:S(2)}) collective-permute-start(bf16[32,1408]{1,0:T(8,128)(2,1)S(1)} %get-tuple-element.63.refs_0_), channel_id=1, source_target_pairs={{0,1},{1,0},{2,3},{3,2},{4,5},{5,4},{6,7},{7,6},{8,9},{9,8},{10,11... | collective-permute-start | bytes 270344 | tf_op jit(solution)/shard_map/ppermute | solution.py:18
  100.1 7.0 %collective-permute-start.18 = (bf16[32,1408]{1,0:T(8,128)(2,1)S(1)}, bf16[32,1408]{1,0:T(8,128)(2,1)S(1)}, u32[]{:S(2)}, u32[]{:S(2)}) collective-permute-start(bf16[32,1408]{1,0:T(8,128)(2,1)S(1)} %get-tuple-element.63.refs_0_), channel_id=1, source_target_pairs={{0,2},{1,3},{2,0},{3,1},{4,6},{5,7},{6,4},{7,5},{8,10},{9,11},{10,... | collective-permute-start | bytes 270344 | tf_op jit(solution)/shard_map/ppermute | solution.py:18
  105.8 14.0 %collective-permute-start.20 = (bf16[32,1408]{1,0:T(8,128)(2,1)S(1)}, bf16[32,1408]{1,0:T(8,128)(2,1)}, u32[]{:S(2)}, u32[]{:S(2)}) collective-permute-start(bf16[32,1408]{1,0:T(8,128)(2,1)S(1)} %get-tuple-element.63.refs_0_), channel_id=1, source_target_pairs={{0,3},{1,2},{2,1},{3,0},{4,7},{5,6},{6,5},{7,4},{8,11},{9,10},{10,... | collective-permute-start | bytes 270344 | tf_op jit(solution)/shard_map/ppermute | solution.py:18
  107.1 15.9 %collective-permute-start.17 = (bf16[32,1408]{1,0:T(8,128)(2,1)S(1)}, bf16[32,1408]{1,0:T(8,128)(2,1)S(1)}, u32[]{:S(2)}, u32[]{:S(2)}) collective-permute-start(bf16[32,1408]{1,0:T(8,128)(2,1)S(1)} %collective-permute-done.16.refs_2_), channel_id=1, source_target_pairs={{0,16},{16,0},{1,17},{17,1},{2,18},{18,2},{3,19},{19,3},{4,20},{20... | collective-permute-start | bytes 270344 | tf_op jit(solution)/shard_map/ppermute | solution.py:18
  119.8 7.8 %collective-permute-start.25 = (bf16[32,4224]{1,0:T(8,128)(2,1)S(1)}, bf16[32,4224]{1,0:T(8,128)(2,1)S(1)}, u32[]{:S(2)}, u32[]{:S(2)}) collective-permute-start(bf16[32,4224]{1,0:T(8,128)(2,1)S(1)} %constant_dynamic-update-slice_fusion.refs_8_), channel_id=1, source_target_pairs={{0,16},{16,0},{1,17},{17,1},{2,18},{18,2},{3,19},{19,3},{4,20},{20... | collective-permute-start | bytes 811016 | tf_op jit(solution)/shard_map/ppermute | solution.py:18
  (35 other events, 108.4 us)
Sparse Core Ops, SparseCore 0:
  10.6 32.6 all-gather.6
  45.1 25.7 all-gather.10
  74.0 38.9 all-gather.8

commit v3 on v2

v3 whole, which is shorter than its diff:
```python
import functools

import jax
import jax.numpy as jnp
from jax import lax
from jax.experimental import pallas as pl
from jax.experimental.pallas import tpu as pltpu
from jax.sharding import PartitionSpec as P

EPSILON = 1e-05
BF = jnp.bfloat16
F32 = jnp.float32
SIDE = 128


def flip(value, axis, mask):
    pairs = [(source, source ^ mask) for source in range(lax.axis_size(axis))]
    return lax.ppermute(value, axis, pairs)


def matmul(left, right):
    return jnp.dot(left, right, preferred_element_type=F32)


def matmul_nt(left, right):
    return lax.dot_general(left, right, (((1,), (1,)), ((), ())), preferred_element_type=F32)


def matmul_tn(left, right):
    return lax.dot_general(left, right, (((0,), (0,)), ((), ())), preferred_element_type=F32)


def unpack(side, place):
    wide = side[:, 3 * place : 3 * place + 3].astype(F32)
    return wide[:, 0:1] + wide[:, 1:2] + wide[:, 2:3]


VMEM = pl.BlockSpec(memory_space=pltpu.VMEM)
SMEM = pl.BlockSpec(memory_space=pltpu.SMEM)
HBM = pl.BlockSpec(memory_space=pltpu.HBM)


def call(body, outs, in_specs, scratch=(), mebibytes=4, out_specs=None):
    return pl.pallas_call(
        body,
        out_shape=outs,
        in_specs=in_specs,
        out_specs=out_specs or [VMEM] * len(outs),
        scratch_shapes=list(scratch),
        compiler_params=pltpu.CompilerParams(vmem_limit_bytes=mebibytes << 20),
    )


def fetch(take_left, left, right, target, sem):
    @pl.when(take_left)
    def _():
        pltpu.make_async_copy(left, target, sem).start()

    @pl.when(jnp.logical_not(take_left))
    def _():
        pltpu.make_async_copy(right, target, sem).start()


def start_copy(source, target, sem):
    copy = pltpu.make_async_copy(source, target, sem)
    copy.start()
    return copy


def side_of(column):
    lane = lax.broadcasted_iota(jnp.int32, (column.shape[0], SIDE), 1)
    high = column.astype(BF).astype(F32)
    middle = (column - high).astype(BF).astype(F32)
    low = column - high - middle
    zero = jnp.zeros(lane.shape, F32)
    picked = jnp.where(lane == 0, high, jnp.where(lane == 1, middle, jnp.where(lane == 2, low, zero)))
    return picked.astype(BF)


def from_side(side):
    return jnp.sum(side.astype(F32), axis=1, keepdims=True)


def emit(part, norm, sents, gram=None):
    half, width = sents[0].shape[0], part.shape[1]
    for place, sent in enumerate(sents):
        start = place * half
        sent[:, :width] = part[start : start + half, :].astype(BF)
        sent[:, width : width + SIDE] = side_of(norm[start : start + half, :])
        if gram is not None:
            for rows, columns in gram_blocks(gram, place, half, width):
                sent[:, columns] = gram[rows, :].astype(BF)


def gram_blocks(gram, place, half, width):
    count, block = gram.shape[0] // 2 // half, gram.shape[1]
    for index in range(count):
        row = (place * count + index) * half
        column = width + SIDE + index * block
        yield slice(row, row + half), slice(column, column + block)


def absorb(part, norm, gots, gram=None, gram_sum=None):
    half, width = gots[0].shape[0], part.shape[1]
    parts, norms = [], []
    for place, got in enumerate(gots):
        start = place * half
        parts.append(part[start : start + half, :] + got[:, :width].astype(F32))
        side = got[:, width : width + SIDE]
        norms.append(norm[start : start + half, :] + from_side(side))
        if gram is not None:
            for rows, columns in gram_blocks(gram, place, half, width):
                summed = gram[rows, :] + got[:, columns].astype(F32)
                gram_sum[rows, :] = summed.astype(gram_sum.dtype)
    return jnp.concatenate(parts, axis=0), jnp.concatenate(norms, axis=0)


def start_kernel(with_gram, where, rows, value_a, value_b, *refs):
    gram_a, gram_b = refs[:2] if with_gram else (None, None)
    refs = refs[2:] if with_gram else refs
    part, norm, top, low = refs[:4]
    gram, (weight, sem) = refs[4] if with_gram else None, refs[-2:]
    fetch(where[0] == 1, value_a, value_b, weight, sem)
    row = rows[...]
    norm[...] = square_sum(row)
    if with_gram:
        gram[...] = gram_a[...] + gram_b[...].astype(F32)
    pltpu.make_async_copy(value_a, weight, sem).wait()
    part[...] = matmul(row, weight[...])
    emit(part, norm, (top, low), gram)


def between_kernel(with_gram, part_in, norm_in, got_top, got_low, *refs):
    gram_in, refs = (refs[0], refs[1:]) if with_gram else (None, refs)
    part, norm, top, low = refs[:4]
    gram = refs[4] if with_gram else None
    part[...], norm[...] = absorb(part_in, norm_in, (got_top, got_low), gram_in, gram)
    emit(part, norm, (top, low), gram)


def section_kernel(features, with_gram, where, *refs):
    part_in, norm_in, got_top, got_low, rows, out_a, out_b, value_a, value_b = refs[:9]
    gram_in, refs = (refs[9], refs[10:]) if with_gram else (None, refs[9:])
    middle, part, norm, top, low = refs[:5]
    gram, (out, value, sems) = refs[5] if with_gram else None, refs[-3:]
    first = where[0] == 1
    fetch(first, out_a, out_b, out, sems.at[0])
    fetch(first, value_b, value_a, value, sems.at[1])
    total, squares = absorb(part_in, norm_in, (got_top, got_low), gram_in, gram)
    values = (total * lax.rsqrt(squares / features + EPSILON)).astype(BF)
    pltpu.make_async_copy(out_a, out, sems.at[0]).wait()
    hidden = (rows[...].astype(F32) + matmul(values, out[...])).astype(BF)
    middle[...] = hidden
    norm[...] = square_sum(hidden)
    pltpu.make_async_copy(value_a, value, sems.at[1]).wait()
    part[...] = matmul(hidden, value[...])
    emit(part, norm, (top, low))


def learn_kernel(where, rows, value_a, value_b, lout_a, lout_b, part, value, lout, sems):
    first = where[0] == 1
    fetch(first, value_a, value_b, value, sems.at[0])
    fetch(first, lout_a, lout_b, lout, sems.at[1])
    inner = value.shape[1]
    pltpu.make_async_copy(value_a, value, sems.at[0]).wait()
    part[:, :inner] = matmul(rows[...], value[...])
    pltpu.make_async_copy(lout_a, lout, sems.at[1]).wait()
    part[:, inner:] = matmul_nt(rows[...], lout[...])


def score_kernel(features, where, *refs):
    part_in, norm_in, got_top, got_low, middle, rows_squares, out_a, out_b = refs[:8]
    scored, norm, out, sem = refs[8:]
    fetch(where[0] == 1, out_b, out_a, out, sem)
    total, squares = absorb(part_in, norm_in, (got_top, got_low))
    values = (total * lax.rsqrt(squares / features + EPSILON)).astype(BF)
    pltpu.make_async_copy(out_a, out, sem).wait()
    score = (middle[...].astype(F32) + matmul(values, out[...])).astype(BF)
    scored[...] = score
    norm[...] = rows_squares[...] + square_sum(score)


def share_kernel(share, where, scored, norm, given, value_a, value_b, lout_a, lout_b, *refs):
    kept, kept_norm = refs[:2]
    peers, (value, lout, part, sent, sems) = refs[2:-5], refs[-5:]
    first, at = where[0] == 1, where[1]
    fetch(first, value_b, value_a, value, sems.at[0])
    fetch(first, lout_b, lout_a, lout, sems.at[1])
    inner = value.shape[1]
    score = scored[...]
    sent[:, 2 * inner :] = side_of(norm[...])
    pltpu.make_async_copy(value_a, value, sems.at[0]).wait()
    part[:, :inner] = given[:, :inner] + matmul(score, value[...])
    sent[:, :inner] = part[:, :inner].astype(BF)
    pltpu.make_async_copy(lout_a, lout, sems.at[1]).wait()
    part[:, inner:] = given[:, inner:] + matmul_nt(score, lout[...])
    sent[:, inner : 2 * inner] = part[:, inner:].astype(BF)
    copies = []
    for place, peer in enumerate(peers):
        start = pl.multiple_of((at ^ (place + 1)) * share, share)
        copies.append(start_copy(sent.at[pl.ds(start, share), :], peer, sems.at[2 + place]))
    mine = pl.ds(pl.multiple_of(at * share, share), share)
    kept[...] = part[mine, :]
    kept_norm[...] = norm[mine, :]
    for copy in copies:
        copy.wait()


def value_kernel(features, block, count, where, kept, norm, *refs):
    got, pieces, crossed = refs[:count], refs[count:-1], refs[-1]
    total, squares = kept[...], norm[...]
    inner = total.shape[1] // 2
    for one in got:
        total = total + one[:, : 2 * inner].astype(F32)
        squares = squares + from_side(one[:, 2 * inner :])
    inverse = lax.rsqrt(squares / features + EPSILON)
    values = (total[:, :inner] * inverse).astype(BF)
    side = side_of(inverse)
    crossed[...] = total[:, inner:].astype(BF)
    for away, piece in enumerate(pieces):
        if len(pieces) == 1:
            cross = crossed[...]
        else:
            cross = crossed[:, pl.ds(pl.multiple_of((where[0] ^ away) * block, block), block)]
        reach = inner + cross.shape[1]
        piece[:, :inner] = values
        piece[:, inner:reach] = cross
        piece[:, reach:] = side


def gradient_kernel(share, peers, aways, spots, dp_size, where, *refs):
    groups = 1 + max(group for group, _ in spots)
    count = 2 * peers * groups
    sources, refs = refs[:count], refs[count:]
    inputs, dense = refs[:2], refs[2:-12]
    parts, grad_value, grad_out, tokens, x, slopes, normed, back, share_count = refs[-12:-3]
    lout, gram, sems = refs[-3:]
    given = dense[2:]
    first, dp_at, mp_at = where[0] == 1, where[1], where[2]
    keep = share * peers
    width, inner, block = x.shape[1], lout.shape[0], gram.shape[1]
    piece = inner + block + SIDE
    total = tokens.shape[0]
    copies = []

    def begin(source, target):
        copies.append(start_copy(source, target, sems.at[len(copies)]))

    begin(dense[0], lout)
    begin(dense[1], gram)
    for array, target in zip(given, (grad_value, grad_out)):
        begin(array, target)
    ready = []
    for number, (away, (group, place)) in enumerate(zip(aways, spots)):
        for side in range(2):
            segment = jnp.where(first, side, 1 - side)
            start = (2 * number + side) * keep
            row = pl.multiple_of((segment * dp_size + (dp_at ^ away)) * keep, keep)
            share_count[start : start + keep, :] = parts[pl.ds(row, keep), :]
            target = x.at[pl.ds(start, keep), :]
            if away == 0:
                begin(inputs[side], target)
            else:
                here, sem = pl.ds(row, keep), sems.at[len(copies)]
                fetch(first, inputs[0].at[here, pl.ds(0, width)], inputs[1].at[here, :], target, sem)
                copies.append(pltpu.make_async_copy(inputs[1].at[here, :], target, sem))
            for mask in range(peers):
                source = sources[2 * (group * peers + mask) + side]
                at = pl.multiple_of(start + (mp_at ^ mask) * share, share)
                begin(
                    source.at[:, pl.ds(place * piece, piece)],
                    tokens.at[pl.ds(at, share), :],
                )
        ready.append(len(copies))
    fixed = 2 + len(given)
    for copy in copies[:2]:
        copy.wait()
    done = fixed
    for number, until in enumerate(ready):
        for copy in copies[done:until]:
            copy.wait()
        done = until
        here = pl.ds(2 * keep * number, 2 * keep)
        wide = x[here, :].astype(F32)
        values = tokens[here, :inner]
        inverse = from_side(tokens[here, inner + block :])
        portion = share_count[here, :]
        slopes[here, :] = ((wide + matmul(values, lout[...])) * portion).astype(BF)
        normed[here, :] = (wide * inverse).astype(BF)
        crossed = tokens[here, inner : inner + block].astype(F32)
        back[here, :] = ((crossed + matmul(values, gram[...])) * portion).astype(BF)
    for copy in copies[2:fixed]:
        copy.wait()
    column = pl.ds(pl.multiple_of(dp_at * block, block), block)
    value_sum = matmul_tn(back[...], normed[...])
    out_sum = matmul_tn(tokens[:, column], slopes[...])
    if given:
        value_sum = value_sum + grad_value[...]
        out_sum = out_sum + grad_out[...]
    grad_value[...] = value_sum
    grad_out[...] = out_sum


def square_sum(value):
    wide = value.astype(F32)
    return jnp.sum(wide * wide, axis=1, keepdims=True)


def exchange(first, second, first_mask, second_mask):
    first, second = lax.optimization_barrier((first, second))
    return lax.optimization_barrier(
        (flip(first, "mp", first_mask), flip(second, "mp", second_mask))
    )


def on_device(
    candidates,
    scorer_value,
    scorer_out,
    learner_value,
    learner_out,
    keep_index,
    keep_dest,
    keep_count,
):
    first = lax.axis_index("segment") == 0
    dp_at = lax.axis_index("dp")
    mp_at = lax.axis_index("mp")
    dp_size = lax.axis_size("dp")
    mp_size = lax.axis_size("mp")
    keep = keep_index.shape[1]
    width = candidates.shape[1]
    scorer_width = width * mp_size
    learner_width = 2 * scorer_width
    inner = learner_value.shape[2]
    block = inner // dp_size
    share = keep // mp_size

    own_value, own_out = scorer_value[0], scorer_out[0]
    own_lvalue, own_lout = learner_value[0], learner_out[0]
    other_value = flip(own_value, "segment", 1)

    is_live = jnp.arange(keep) < keep_count[0]
    pick = (keep_index[0][:, None] == jnp.arange(candidates.shape[0])[None, :]) & is_live[:, None]
    rows = matmul(pick.astype(BF), candidates).astype(BF)
    goal = jnp.where(is_live, keep_dest[0] + 1, 0).astype(F32)[:, None]
    every_row = lax.all_gather(
        jnp.concatenate([rows, jnp.broadcast_to(goal, (keep, SIDE)).astype(BF)], axis=1),
        ("segment", "dp"),
        axis=0,
        tiled=False,
    )

    gram = matmul_nt(own_lout, lax.dynamic_slice_in_dim(own_lout, dp_at * block, block, 0))
    half = inner // 2
    at = lax.axis_index("segment")
    kept_half = lax.dynamic_slice_in_dim(gram, at * half, half, 0)
    sent_half = lax.dynamic_slice_in_dim(gram, (1 - at) * half, half, 0)
    got_half = flip(sent_half.astype(BF), "segment", 1)

    direct = dp_size <= 8 and block % SIDE == 0
    flag = first.astype(jnp.int32)
    half_rows = keep // 2
    sums = [jax.ShapeDtypeStruct((keep, inner), F32), jax.ShapeDtypeStruct((keep, 1), F32)]
    state = sums + [jax.ShapeDtypeStruct((half_rows, inner + SIDE), BF)] * 2
    wide_state = state
    if direct:
        extra = half * block // keep
        wide_state = sums + [jax.ShapeDtypeStruct((half_rows, inner + SIDE + extra), BF)] * 2
        wide_state.append(jax.ShapeDtypeStruct((half, block), F32))
    hidden_type = jax.ShapeDtypeStruct((keep, width), BF)
    where = jnp.stack([flag, mp_at])
    weight = pltpu.VMEM(own_value.shape, BF)

    def placed(*arrays):
        return [pltpu.with_memory_space_constraint(array, pltpu.HBM) for array in arrays]

    def halves(outs):
        return outs[0], outs[1], outs[2:4], list(outs[4:])

    outs = call(
        functools.partial(start_kernel, direct),
        wide_state,
        [SMEM, VMEM, HBM, HBM] + [VMEM] * (2 * direct),
        [weight, pltpu.SemaphoreType.DMA],
        mebibytes=12,
    )(where, rows, *placed(own_value, other_value), *((kept_half, got_half) if direct else ()))
    part, rows_squares, sents, gram_sum = halves(outs)
    own_out, own_lvalue, own_lout, sents = lax.optimization_barrier(
        (own_out, own_lvalue, own_lout, sents)
    )
    other_out = flip(own_out, "segment", 1)
    other_lvalue = flip(own_lvalue, "segment", 1)
    other_lout = flip(own_lout, "segment", 1)
    got = exchange(*sents, 1, 2)
    outs = call(
        functools.partial(between_kernel, direct), wide_state, [VMEM] * (4 + direct), mebibytes=8
    )(part, rows_squares, *got, *gram_sum)
    part, norm, sents, gram_sum = halves(outs)
    got = exchange(*sents, 2, 1)
    outs = call(
        functools.partial(section_kernel, scorer_width, direct),
        [hidden_type] + state + [jax.ShapeDtypeStruct((half, block), BF)] * direct,
        [SMEM] + [VMEM] * 5 + [HBM] * 4 + [VMEM] * direct,
        [weight, weight, pltpu.SemaphoreType.DMA((2,))],
        mebibytes=12,
    )(where, part, norm, *got, rows, *placed(own_out, other_out, own_value, other_value), *gram_sum)
    middle, outs = outs[0], outs[1:]
    part, norm, sents, gram_sum = halves(outs)
    learner_weights = placed(own_lvalue, other_lvalue, own_lout, other_lout)
    given = call(
        learn_kernel,
        [jax.ShapeDtypeStruct((keep, 2 * inner), F32)],
        [SMEM, VMEM] + [HBM] * 4,
        [weight, weight, pltpu.SemaphoreType.DMA((2,))],
        mebibytes=10,
    )(where, rows, *learner_weights)[0]
    got = exchange(*sents, 1, 2)
    outs = call(functools.partial(between_kernel, False), state, [VMEM] * 4)(part, norm, *got)
    part, norm, sents, _ = halves(outs)
    sents, given = lax.optimization_barrier((sents, given))
    got = exchange(*sents, 2, 1)
    part, goals = lax.optimization_barrier((part, every_row[:, :, width]))

    long = 2 * inner + SIDE
    scored, norm = call(
        functools.partial(score_kernel, scorer_width),
        [hidden_type, sums[1]],
        [SMEM] + [VMEM] * 6 + [HBM] * 2,
        [weight, pltpu.SemaphoreType.DMA],
        mebibytes=8,
    )(where, part, norm, *got, middle, rows_squares, *placed(own_out, other_out))
    every_scored = lax.all_gather(scored, ("segment", "dp"), axis=0, tiled=False)
    outs = call(
        functools.partial(share_kernel, share),
        [
            jax.ShapeDtypeStruct((share, 2 * inner), F32),
            jax.ShapeDtypeStruct((share, 1), F32),
        ]
        + [pltpu.HBM((share, long), BF)] * (mp_size - 1),
        [SMEM] + [VMEM] * 3 + [HBM] * 4,
        [
            weight,
            weight,
            pltpu.VMEM((keep, 2 * inner), F32),
            pltpu.VMEM((keep, long), BF),
            pltpu.SemaphoreType.DMA((mp_size + 1,)),
        ],
        mebibytes=12,
        out_specs=[VMEM] * 2 + [HBM] * (mp_size - 1),
    )(where, scored, norm, given, *learner_weights)
    kept, kept_norm = outs[:2]
    got = lax.optimization_barrier(
        tuple(flip(peer, "mp", mask) for mask, peer in enumerate(outs[2:], 1))
    )
    pieces = call(
        functools.partial(value_kernel, learner_width, block, mp_size - 1),
        [jax.ShapeDtypeStruct((share, inner + block + SIDE), BF)] * dp_size
        if direct
        else [jax.ShapeDtypeStruct((share, long), BF)],
        [SMEM] + [VMEM] * (mp_size + 1),
        [pltpu.VMEM((share, inner), BF)],
    )(jnp.stack([dp_at]), kept, kept_norm, *got)

    if direct:
        gram_half = gram_sum[0]
    else:
        gram_half = lax.psum(kept_half + got_half.astype(F32), "mp").astype(BF)
    gram_other = flip(gram_half, "segment", 1)
    gram = jnp.where(
        first,
        jnp.concatenate([gram_half, gram_other], axis=0),
        jnp.concatenate([gram_other, gram_half], axis=0),
    )

    goals = goals.astype(jnp.int32).reshape(2, dp_size, keep)
    hits = goals[:, :, :, None] == jnp.arange(1, dp_size + 1)
    counts = jnp.sum(hits.astype(F32), axis=(1, 2), keepdims=True)
    parts = 1.0 / jnp.maximum(jnp.sum(jnp.where(hits, counts, 0.0), axis=3), 1.0)
    column = dp_at * block

    def spread(piece):
        whole = jnp.zeros((keep, piece.shape[1]), BF)
        for mask in range(mp_size):
            got = flip(piece, "mp", mask) if mask else piece
            whole = lax.dynamic_update_slice(whole, got, ((mp_at ^ mask) * share, 0))
        return whole

    def add(grads, pieces, places):
        pieces = jnp.concatenate(pieces, axis=0)
        tokens = jnp.concatenate([pieces, flip(pieces, "segment", 1)], axis=0)
        x, share_count = [], []
        for segment in (at, 1 - at):
            for place in places:
                row = lax.dynamic_index_in_dim(every_row, segment * dp_size + place, 0, False)
                score = lax.dynamic_index_in_dim(every_scored, segment * dp_size + place, 0, False)
                x.append(jnp.where(first, row[:, :width], score))
                share_count.append(lax.dynamic_slice(parts, (segment, place, 0), (1, 1, keep)))
        x = jnp.concatenate(x, axis=0).astype(F32)
        share_count = jnp.concatenate([part.reshape(keep, 1) for part in share_count], axis=0)
        v = tokens[:, :inner]
        xo = tokens[:, inner : inner + block].astype(F32)
        inv = unpack(tokens[:, inner + block :], 0)
        slopes = ((x + matmul(v, own_lout)) * share_count).astype(BF)
        normed = (x * inv).astype(BF)
        back = ((xo + matmul(v, gram)) * share_count).astype(BF)
        v_block = lax.dynamic_slice_in_dim(v, column, block, 1)
        return (grads[0] + matmul_tn(back, normed), grads[1] + matmul_tn(v_block, slopes))

    if direct:
        moved = [flip(pieces[away], "dp", away) for away in range(1, dp_size)]
        stacks = [[pieces[0]] + moved[:1], moved[1:]]

        def all_shares(stack):
            stack = jnp.concatenate(stack, axis=1) if len(stack) > 1 else stack[0]
            return [stack] + [flip(stack, "mp", mask) for mask in range(1, mp_size)]

        def both_cores(nears):
            return [array for near in nears for array in (near, flip(near, "segment", 1))]

        swap = flip(jnp.where(first, scored, rows), "segment", 1)
        near_x = jnp.where(first, rows, scored)
        whole = parts.reshape(2 * dp_size * keep, 1)
        where = jnp.stack([flag, dp_at, mp_at])

        def gradients(aways, spots, groups, inputs, given, mebibytes):
            tokens = 2 * len(aways) * keep
            dense = [own_lout, gram, *given]
            return call(
                functools.partial(gradient_kernel, share, mp_size, aways, spots, dp_size),
                [jax.ShapeDtypeStruct((block, width), F32)] * 2,
                [SMEM] + [HBM] * (len(groups) + 2 + len(dense)) + [VMEM],
                [
                    pltpu.VMEM((tokens, inner + block + SIDE), BF),
                    pltpu.VMEM((tokens, width), BF),
                    pltpu.VMEM((tokens, width), BF),
                    pltpu.VMEM((tokens, width), BF),
                    pltpu.VMEM((tokens, block), BF),
                    pltpu.VMEM((tokens, 1), F32),
                    pltpu.VMEM(own_lout.shape, BF),
                    pltpu.VMEM(gram.shape, BF),
                    pltpu.SemaphoreType.DMA((2 * len(aways) * (mp_size + 1) + len(dense),)),
                ],
                mebibytes=mebibytes,
            )(where, *placed(*groups, *inputs, *dense), whole)

        early = all_shares(stacks[0])
        early[1:] = lax.optimization_barrier(early[1:])
        groups = both_cores(early)
        grads = gradients((0,), ((0, 0),), groups, (near_x, swap), (), 14)
        if dp_size > 1:
            spots = ((0, 1),)
            if dp_size > 2:
                *stack, _ = lax.optimization_barrier((*stacks[1], early[1:]))
                late = all_shares(stack)
                last, grads = lax.optimization_barrier((late[-1], grads))
                groups = groups + both_cores(late[:-1] + [last])
                spots += tuple((1, place) for place in range(dp_size - 2))
            tokens = 2 * dp_size * keep
            inputs = (
                every_row.reshape(tokens, width + SIDE),
                every_scored.reshape(tokens, width),
            )
            grads = gradients(tuple(range(1, dp_size)), spots, groups, inputs, grads, 22)
    else:
        ring = [(source, (source + 1) % dp_size) for source in range(dp_size)]

        def turn(step, carry):
            grads, full = carry
            cross = lax.dynamic_slice_in_dim(full, inner + column, block, 1)
            piece = jnp.concatenate([full[:, :inner], cross, full[:, 2 * inner :]], axis=1)
            grads = add(grads, [spread(piece)], [(dp_at - step) % dp_size])
            return grads, lax.ppermute(full, "dp", ring)

        grads = (jnp.zeros((block, width), F32), jnp.zeros((block, width), F32))
        grads, _ = lax.fori_loop(0, dp_size, turn, (grads, pieces[0]))
    return (grads[0][None], grads[1][None])


def solution(mesh):
    placed = (
        P(("segment", "dp"), "mp"),
        P("segment", "mp", None),
        P("segment", None, "mp"),
        P("segment", "mp", None),
        P("segment", None, "mp"),
        P(("segment", "dp"), None),
        P(("segment", "dp"), None),
        P(("segment", "dp")),
    )
    return jax.shard_map(
        on_device,
        mesh=mesh,
        in_specs=placed,
        out_specs=(P("segment", "dp", "mp"), P("segment", "dp", "mp")),
        check_vma=False,
    )
```

time: 152 us -> 127 us (0.84)
  Pallas kernels: 16.9 us -> 32.3 us
  other arithmetic: 19.3 us -> 4.56 us
  local copies, waits for them, and re-layouts: 24.4 us -> 10.5 us
  starting transfers between devices: 43.4 us -> 36.7 us
  matrix products: 7.89 us -> 3.44 us
    pallas_call x2 -> x9, Pallas kernels: 16.7 us -> 32.1 us  [the longest x2 13.1 us: gradients(): call(functools.partial(gradient_kernel, share, mp_size, aways, spots, dp_...]
    ppermute x34 -> x35, starting transfers between devices: 43.2 us -> 36.7 us  [flip(): return lax.ppermute(value, axis, pairs)]
    convert_element_type x16 -> x0, other arithmetic: 5.62 us -> none  [the longest x8 2.23 us: unpack(): wide = side[:, 3 * place:3 * place + 3].astype(F32)]
    unnamed x46 -> x49, local copies, waits for them, and re-layouts: 13.8 us -> 8.47 us
    optimization_barrier x1 -> x0, local copies, waits for them, and re-layouts: 4.5 us -> none  [on_device(): total, every_row = lax.optimization_barrier((total, every_row))]
    dot_general x5 -> x1, matrix products: 5.38 us -> 0.92 us  [matmul(): return jnp.dot(left, right, preferred_element_type=F32)]
    concatenate x9 -> x0, other arithmetic: 3.58 us -> none  [the longest x7 2.74 us: sent(): return jnp.concatenate([part.astype(BF), pack([norm])], axis=1)]
    add x6 -> x0, other arithmetic: 1.85 us -> none  [the longest x2 1.32 us: reduce_rows(): part + new[:, :width].astype(F32)]
  transfers between devices with their start and end apart: 37 -> 37, of which waited for: 11 -> 12; matrix products, arithmetic and copies ran while one was open for 23% -> 9% of each run, Pallas kernels for 5% -> 16%
where the time goes in v3:
time: 127 us; the launch traced here: 126 us
  starting transfers between devices  36.7 us (29%)
  Pallas kernels  32.3 us (25%)
  waiting for transfers between devices  23 us (18%)
  between operations  15 us (12%)
  local copies, waits for them, and re-layouts  10.5 us (8%)
  other arithmetic  4.56 us (4%)
  matrix products  3.44 us (3%)
    ppermute x35, starting transfers between devices, flip(): return lax.ppermute(value, axis, pairs)  36.7 us
    ppermute x35, waiting for transfers between devices, flip(): return lax.ppermute(value, axis, pairs)  22.9 us
    pallas_call x2, Pallas kernels, gradients(): call(functools.partial(gradient_kernel, share, mp_size, aways, spots, dp_...  13.1 us
    unnamed x49, local copies, waits for them, and re-layouts  8.47 us
    pallas_call x1, Pallas kernels, on_device(): call(functools.partial(share_kernel, share), [jax.ShapeDtypeStruct((share...  4.8 us
    pallas_call x1, Pallas kernels, on_device(): call(learn_kernel, [jax.ShapeDtypeStruct((keep, 2 * inner), F32)], [SMEM,...  3.61 us
    pallas_call x1, Pallas kernels, on_device(): call(functools.partial(score_kernel, scorer_width), [hidden_type, sums[1]...  3.41 us
    pallas_call x1, Pallas kernels, on_device(): call(functools.partial(section_kernel, scorer_width, direct), [hidden_typ...  3.29 us
  transfers between devices with their start and end apart: 37, of which 12 were waited for; matrix products, arithmetic and copies ran while one was open for 9% of the time, Pallas kernels for 16%

profile of v3, /device:TPU:11, one launch (start us, length us, event | category | flops | bytes accessed | tf_op | source)
XLA Modules:
  0.0 125.6 jit_solution(14629667187567871448)
XLA Ops:
  11.1 2.5 %fusion = f32[256,1024]{0,1:T(8,128)S(1)} fusion(bf16[1,1024,1024]{2,1,0:T(8,128)(2,1)} %param.12, s32[]{:T(128)S(6)} %select_n.41), kind=kOutput, calls=%fused_computation.2 | convolution fusion | flops 536870912 | bytes 3670020 | tf_op jit(solution)/shard_map/dot_general | solution.py:26
  15.3 2.7 %shard_map.95 = (f32[128,1024]{1,0:T(8,128)S(1)}, f32[128,1]{1,0:T(8,128)S(1)}, bf16[64,2176]{1,0:T(8,128)(2,1)S(1)}, bf16[64,2176]{1,0:T(8,128)(2,1)S(1)}, f32[512,256]{1,0:T(8,128)S(1)}) custom-call(s32[2]{0:T(128)S(1)} %pad_add_fusion.1.where, bf16[128,1024]{1,0:T(8,128)(2,1)S(1)} %convolution_convert_fusion.rows.refs_4_, bf16[1024,1024]{1,0:T(8,128)(2,1)} %bitcast.43, ...), custom_call_target="tpu_custom_call" | custom-call | tf_op jit(solution)/shard_map/pallas_call | solution.py:381
  20.4 6.6 %collective-permute-done.2.got_top = bf16[64,2176]{1,0:T(8,128)(2,1)S(1)} collective-permute-done((bf16[64,2176]{1,0:T(8,128)(2,1)S(1)}, bf16[64,2176]{1,0:T(8,128)(2,1)S(1)}, u32[]{:S(2)}, u32[]{:S(2)}) %collective-permute-start.2) | collective-permute-done | bytes 278560 | tf_op jit(solution)/shard_map/ppermute | solution.py:18
  27.3 1.3 %collective-permute-start.4 = (bf16[64,2176]{1,0:T(8,128)(2,1)S(1)}, bf16[64,2176]{1,0:T(8,128)(2,1)S(1)}, u32[]{:S(2)}, u32[]{:S(2)}) collective-permute-start(bf16[64,2176]{1,0:T(8,128)(2,1)S(1)} %get-tuple-element.89), channel_id=1, source_target_pairs={{0,2},{1,3},{2,0},{3,1},{4,6},{5,7},{6,4},{7,5},{8,10},{9,11},{10,... | collective-permute-start | bytes 835592 | tf_op jit(solution)/shard_map/ppermute | solution.py:18
  29.8 4.7 %collective-permute-done.4.refs_2_ = bf16[64,2176]{1,0:T(8,128)(2,1)S(1)} collective-permute-done((bf16[64,2176]{1,0:T(8,128)(2,1)S(1)}, bf16[64,2176]{1,0:T(8,128)(2,1)S(1)}, u32[]{:S(2)}, u32[]{:S(2)}) %collective-permute-start.4) | collective-permute-done | bytes 278560 | tf_op jit(solution)/shard_map/ppermute | solution.py:18
  36.8 3.3 %shard_map.97 = (bf16[128,1024]{1,0:T(8,128)(2,1)S(1)}, f32[128,1024]{1,0:T(8,128)S(1)}, f32[128,1]{1,0:T(8,128)S(1)}, bf16[64,1152]{1,0:T(8,128)(2,1)S(1)}, bf1...) custom-call(s32[2]{0:T(128)S(1)} %pad_add_fusion.1.where, f32[128,1024]{1,0:T(8,128)S(1)} %get-tuple-element.85.refs_0_, ...), custom_call_target="tpu_custom_call" | custom-call | tf_op jit(solution)/shard_map/pallas_call | solution.py:401
  41.5 1.3 %copy-done.5 = bf16[1024,1024]{1,0:T(8,128)(2,1)} copy-done((bf16[1024,1024]{1,0:T(8,128)(2,1)}, bf16[1024,1024]{1,0:T(8,128)(2,1)S(1)}, u32[]{:S(2)}) %copy-start.5) | copy-done | bytes 2097176
  42.8 1.4 %copy-done.6 = bf16[1024,1024]{1,0:T(8,128)(2,1)} copy-done((bf16[1024,1024]{1,0:T(8,128)(2,1)}, bf16[1024,1024]{1,0:T(8,128)(2,1)S(1)}, u32[]{:S(2)}) %copy-start.6) | copy-done | bytes 2097176
  44.2 3.6 %shard_map.99.given = f32[128,2048]{1,0:T(8,128)S(1)} custom-call(s32[2]{0:T(128)S(1)} %pad_add_fusion.1.where, bf16[128,1024]{1,0:T(8,128)(2,1)S(1)} %convolution_convert_fusion.rows.refs_4_, bf16[1024,1024]{1,0:T(8,128)(2,1)} %bitcast.39, bf16[1024,1024]{1,0:T(8,128)(2,1)} %copy-done.5, bf16[1024,1024]{1,0:T(8,128)(2,1)} %bitcast.34, ...), custom_call_target="tpu_custom_call" | custom-call | tf_op jit(solution)/shard_map/pallas_call | solution.py:411
  50.3 1.7 %slice.4 = bf16[8,128,1]{2,1,0:T(8,128)(2,1)} slice(bf16[8,128,1152]{2,1,0:T(8,128)(2,1)} %bitcast.48), slice={[0:8], [0:128], [1024:1025]} | slice | bytes 4096 | tf_op jit(solution)/shard_map/slice | solution.py:423
  53.8 3.4 %shard_map.100 = (bf16[128,1024]{1,0:T(8,128)(2,1)}, f32[128,1]{1,0:T(8,128)S(1)}) custom-call(s32[2]{0:T(128)S(1)} %pad_add_fusion.1.where, f32[128,1024]{1,0:T(8,128)S(1)} %get-tuple-element.104.refs_0_, f32[128,1]{1,0:T(8,128)S(1)} %get-tuple-element.105.refs_1_, bf16[64,1152]{1,0:T(8,128)(2,1)S(1)} %collective-permute-done.11.refs_2_, ...), custom_call_target="tpu_custom_call" | custom-call | tf_op jit(solution)/shard_map/pallas_call | solution.py:426
  57.4 4.8 %shard_map.101 = (f32[32,2048]{1,0:T(8,128)S(1)}, f32[32,1]{1,0:T(8,128)S(1)}, bf16[32,2176]{1,0:T(8,128)(2,1)}, bf16[32,2176]{1,0:T(8,128)(2,1)}, bf16[32,2176]{1,0:T(8,128)(2,1)}) custom-call(s32[2]{0:T(128)S(1)} %pad_add_fusion.1.where, bf16[128,1024]{1,0:T(8,128)(2,1)} %get-tuple-element.117.scored, f32[128,1]{1,0:T(8,128)S(1)} %get-tuple-element.118.norm, ...), custom_call_target="tpu_custom_call" | custom-call | tf_op jit(solution)/shard_map/pallas_call | solution.py:434
  63.0 1.9 %collective-permute-start.15 = (bf16[32,2176]{1,0:T(8,128)(2,1)}, bf16[32,2176]{1,0:T(8,128)(2,1)S(1)}, u32[]{:S(2)}, u32[]{:S(2)}) collective-permute-start(bf16[32,2176]{1,0:T(8,128)(2,1)} %get-tuple-element.124), channel_id=1, source_target_pairs={{0,3},{1,2},{2,1},{3,0},{4,7},{5,6},{6,5},{7,4},{8,11},{9,10},{10,... | collective-permute-start | bytes 417800 | tf_op jit(solution)/shard_map/ppermute | solution.py:18
  66.4 2.0 %collective-permute-done.14.refs_1_ = bf16[32,2176]{1,0:T(8,128)(2,1)S(1)} collective-permute-done((bf16[32,2176]{1,0:T(8,128)(2,1)}, bf16[32,2176]{1,0:T(8,128)(2,1)S(1)}, u32[]{:S(2)}, u32[]{:S(2)}) %collective-permute-start.14) | collective-permute-done | bytes 139296 | tf_op jit(solution)/shard_map/ppermute | solution.py:18
  68.8 2.4 %collective-permute-start.24 = (bf16[32,1408]{1,0:T(8,128)(2,1)S(1)}, bf16[32,1408]{1,0:T(8,128)(2,1)S(1)}, u32[]{:S(2)}, u32[]{:S(2)}) collective-permute-start(bf16[32,1408]{1,0:T(8,128)(2,1)S(1)} %get-tuple-element.133), channel_id=1, source_target_pairs={{0,8},{4,12},{8,0},{12,4},{1,9},{5,13},{9,1},{13,5},{2,10},{6,14},... | collective-permute-start | bytes 270344 | tf_op jit(solution)/shard_map/ppermute | solution.py:18
  71.4 2.7 %collective-permute-done.16 = bf16[32,1408]{1,0:T(8,128)(2,1)S(1)} collective-permute-done((bf16[32,1408]{1,0:T(8,128)(2,1)S(1)}, bf16[32,1408]{1,0:T(8,128)(2,1)S(1)}, u32[]{:S(2)}, u32[]{:S(2)}) %collective-permute-start.16) | collective-permute-done | bytes 90144 | tf_op jit(solution)/shard_map/ppermute | solution.py:18
  74.1 1.6 %collective-permute-start.20 = (bf16[32,2816]{1,0:T(8,128)(2,1)S(1)}, bf16[32,2816]{1,0:T(8,128)(2,1)S(1)}, u32[]{:S(2)}, u32[]{:S(2)}) collective-permute-start(bf16[32,2816]{1,0:T(8,128)(2,1)S(1)} %constant_dynamic-update-slice_fusion.refs_0_), channel_id=1, source_target_pairs={{0,3},{1,2},{2,1},{3,0},{4,7},{5,6},{6,5},{7,4},{8,11},{9,10},{10,... | collective-permute-start | bytes 540680 | tf_op jit(solution)/shard_map/ppermute | solution.py:18
  76.8 1.7 %broadcast_select_fusion = (bf16[128,1024]{1,0:T(8,128)(2,1)S(1)}, bf16[128,1024]{1,0:T(8,128)(2,1)}) fusion(bf16[128,1024]{1,0:T(8,128)(2,1)} %get-tuple-element.117.scored, bf16[128,1024]{1,0:T(8,128)(2,1)S(1)} %convolution_convert_fusion.rows.refs_4_, pred[]{:T(512)S(6)} %eq.36), kind=kLoop, calls=%fused_computation.9 | loop fusion | flops 262144 | bytes 1048577 | tf_op jit(solution)/shard_map/jit(_where)/select_n | solution.py:521
  79.8 8.4 %collective-permute-start.33 = (bf16[512,256]{1,0:T(8,128)(2,1)S(1)}, bf16[512,256]{1,0:T(8,128)(2,1)S(1)}, u32[]{:S(2)}, u32[]{:S(2)}) collective-permute-start(bf16[512,256]{1,0:T(8,128)(2,1)S(1)} %get-tuple-element.137), channel_id=1, source_target_pairs={{0,16},{16,0},{1,17},{17,1},{2,18},{18,2},{3,19},{19,3},{4,20},{20... | collective-permute-start | bytes 786440 | tf_op jit(solution)/shard_map/ppermute | solution.py:18
  88.2 1.8 %collective-permute-start.32 = (bf16[128,1024]{1,0:T(8,128)(2,1)S(1)}, bf16[128,1024]{1,0:T(8,128)(2,1)S(1)}, u32[]{:S(2)}, u32[]{:S(2)}) collective-permute-start(bf16[128,1024]{1,0:T(8,128)(2,1)S(1)} %get-tuple-element.146), channel_id=1, source_target_pairs={{0,16},{16,0},{1,17},{17,1},{2,18},{18,2},{3,19},{19,3},{4,20},{20... | collective-permute-start | bytes 786440 | tf_op jit(solution)/shard_map/ppermute | solution.py:18
  90.6 1.8 %collective-permute-start.31 = (bf16[32,2816]{1,0:T(8,128)(2,1)S(1)}, bf16[32,2816]{1,0:T(8,128)(2,1)}, u32[]{:S(2)}, u32[]{:S(2)}) collective-permute-start(bf16[32,2816]{1,0:T(8,128)(2,1)S(1)} %constant_dynamic-update-slice_fusion.2.refs_8_), channel_id=1, source_target_pairs={{0,3},{1,2},{2,1},{3,0},{4,7},{5,6},{6,5},{7,4},{8,11},{9,10},{10,... | collective-permute-start | bytes 540680 | tf_op jit(solution)/shard_map/ppermute | solution.py:18
  93.3 5.0 %collective-permute-start.22 = (bf16[32,2816]{1,0:T(8,128)(2,1)S(1)}, bf16[32,2816]{1,0:T(8,128)(2,1)S(1)}, u32[]{:S(2)}, u32[]{:S(2)}) collective-permute-start(bf16[32,2816]{1,0:T(8,128)(2,1)S(1)} %collective-permute-done.19.refs_4_), channel_id=1, source_target_pairs={{0,16},{16,0},{1,17},{17,1},{2,18},{18,2},{3,19},{19,3},{4,20},{20... | collective-permute-start | bytes 540680 | tf_op jit(solution)/shard_map/ppermute | solution.py:18
  100.8 4.3 %shard_map.103 = (f32[256,1024]{1,0:T(8,128)S(1)}, f32[256,1024]{1,0:T(8,128)S(1)}) custom-call(s32[3]{0:T(128)S(1)} %pad_add_fusion.where, bf16[32,2816]{1,0:T(8,128)(2,1)} %copy-done.9, bf16[32,2816]{1,0:T(8,128)(2,1)} %copy-done.13, bf16[32,2816]{1,0:T(8,128)(2,1)} %copy-done.12, bf16[32,2816]{1,0:T(8,128)(2,1)} %copy-done.14, ...), custom_call_target="tpu_custom_call" | custom-call | tf_op jit(solution)/shard_map/pallas_call | solution.py:529
  109.9 8.8 %shard_map.104 = (f32[256,1024]{1,0:T(8,128)}, f32[256,1024]{1,0:T(8,128)}) custom-call(s32[3]{0:T(128)S(1)} %pad_add_fusion.where, bf16[32,2816]{1,0:T(8,128)(2,1)} %copy-done.9, bf16[32,2816]{1,0:T(8,128)(2,1)} %copy-done.13, bf16[32,2816]{1,0:T(8,128)(2,1)} %copy-done.12, bf16[32,2816]{1,0:T(8,128)(2,1)} %copy-done.14, bf16[32,2816]{1,0:T(8,128)(2,1)} %copy-done.11, ...), custom_call_target="tpu_custom_call" | custom-call | tf_op jit(solution)/shard_map/pallas_call | solution.py:529
  (132 shorter events, 30.9 us)
Async XLA Ops:
  7.2 43.2 %all-gather.5.cloned.1.call-start = ((), (), s32[]{:S(2)}) async-start(), calls=%async_computation | async-start | bytes 2654208 | tf_op jit(solution)/shard_map/all_gather | solution.py:347
  7.2 8.1 %collective-permute-start = (bf16[1024,1024]{1,0:T(8,128)(2,1)}, bf16[1024,1024]{1,0:T(8,128)(2,1)}, u32[]{:S(2)}, u32[]{:S(2)}) collective-permute-start(bf16[1024,1024]{1,0:T(8,128)(2,1)} %bitcast.42), channel_id=1, source_target_pairs={{0,16},{16,0},{1,17},{17,1},{2,18},{18,2},{3,19},{19,3},{4,20},{20... | collective-permute-start | bytes 6291464 | tf_op jit(solution)/shard_map/ppermute | solution.py:18
  11.1 98.2 %all-gather.7.cloned.1.call-start = ((), (), s32[]{:S(2)}) async-start(), calls=%async_computation.1 | async-start | bytes 2359296 | tf_op jit(solution)/shard_map/all_gather | solution.py:433
  18.1 17.4 %collective-permute-start.6 = (bf16[1024,1024]{1,0:T(8,128)(2,1)S(1)}, bf16[1024,1024]{1,0:T(8,128)(2,1)S(1)}, u32[]{:S(2)}, u32[]{:S(2)}) collective-permute-start(bf16[1024,1024]{1,0:T(8,128)(2,1)S(1)} %bitcast.47), channel_id=1, source_target_pairs={{0,16},{16,0},{1,17},{17,1},{2,18},{18,2},{3,19},{19,3},{4,20},{20... | collective-permute-start | bytes 6291464 | tf_op jit(solution)/shard_map/ppermute | solution.py:18
  18.4 23.1 %collective-permute-start.9 = (bf16[1024,1024]{1,0:T(8,128)(2,1)S(1)}, bf16[1024,1024]{1,0:T(8,128)(2,1)S(1)}, u32[]{:S(2)}, u32[]{:S(2)}) collective-permute-start(bf16[1024,1024]{1,0:T(8,128)(2,1)S(1)} %bitcast.41), channel_id=1, source_target_pairs={{0,16},{16,0},{1,17},{17,1},{2,18},{18,2},{3,19},{19,3},{4,20},{20... | collective-permute-start | bytes 6291464 | tf_op jit(solution)/shard_map/ppermute | solution.py:18
  18.6 22.8 %collective-permute-start.10 = (bf16[1024,1024]{1,0:T(8,128)(2,1)S(1)}, bf16[1024,1024]{1,0:T(8,128)(2,1)S(1)}, u32[]{:S(2)}, u32[]{:S(2)}) collective-permute-start(bf16[1024,1024]{1,0:T(8,128)(2,1)S(1)} %bitcast.38), channel_id=1, source_target_pairs={{0,16},{16,0},{1,17},{17,1},{2,18},{18,2},{3,19},{19,3},{4,20},{20... | collective-permute-start | bytes 6291464 | tf_op jit(solution)/shard_map/ppermute | solution.py:18
  18.9 8.1 %collective-permute-start.2 = (bf16[64,2176]{1,0:T(8,128)(2,1)S(1)}, bf16[64,2176]{1,0:T(8,128)(2,1)S(1)}, u32[]{:S(2)}, u32[]{:S(2)}) collective-permute-start(bf16[64,2176]{1,0:T(8,128)(2,1)S(1)} %get-tuple-element.80), channel_id=1, source_target_pairs={{0,1},{1,0},{2,3},{3,2},{4,5},{5,4},{6,7},{7,6},{8,9},{9,8},{10,11... | collective-permute-start | bytes 835592 | tf_op jit(solution)/shard_map/ppermute | solution.py:18
  19.2 7.9 %collective-permute-start.3 = (bf16[64,2176]{1,0:T(8,128)(2,1)S(1)}, bf16[64,2176]{1,0:T(8,128)(2,1)S(1)}, u32[]{:S(2)}, u32[]{:S(2)}) collective-permute-start(bf16[64,2176]{1,0:T(8,128)(2,1)S(1)} %get-tuple-element.81), channel_id=1, source_target_pairs={{0,2},{1,3},{2,0},{3,1},{4,6},{5,7},{6,4},{7,5},{8,10},{9,11},{10,... | collective-permute-start | bytes 835592 | tf_op jit(solution)/shard_map/ppermute | solution.py:18
  27.3 7.1 %collective-permute-start.4 = (bf16[64,2176]{1,0:T(8,128)(2,1)S(1)}, bf16[64,2176]{1,0:T(8,128)(2,1)S(1)}, u32[]{:S(2)}, u32[]{:S(2)}) collective-permute-start(bf16[64,2176]{1,0:T(8,128)(2,1)S(1)} %get-tuple-element.89), channel_id=1, source_target_pairs={{0,2},{1,3},{2,0},{3,1},{4,6},{5,7},{6,4},{7,5},{8,10},{9,11},{10,... | collective-permute-start | bytes 835592 | tf_op jit(solution)/shard_map/ppermute | solution.py:18
  28.7 6.8 %collective-permute-start.5 = (bf16[64,2176]{1,0:T(8,128)(2,1)S(1)}, bf16[64,2176]{1,0:T(8,128)(2,1)S(1)}, u32[]{:S(2)}, u32[]{:S(2)}) collective-permute-start(bf16[64,2176]{1,0:T(8,128)(2,1)S(1)} %get-tuple-element.90), channel_id=1, source_target_pairs={{0,1},{1,0},{2,3},{3,2},{4,5},{5,4},{6,7},{7,6},{8,9},{9,8},{10,11... | collective-permute-start | bytes 835592 | tf_op jit(solution)/shard_map/ppermute | solution.py:18
  40.1 7.8 %collective-permute-start.7 = (bf16[64,1152]{1,0:T(8,128)(2,1)S(1)}, bf16[64,1152]{1,0:T(8,128)(2,1)S(1)}, u32[]{:S(2)}, u32[]{:S(2)}) collective-permute-start(bf16[64,1152]{1,0:T(8,128)(2,1)S(1)} %get-tuple-element.99), channel_id=1, source_target_pairs={{0,1},{1,0},{2,3},{3,2},{4,5},{5,4},{6,7},{7,6},{8,9},{9,8},{10,11... | collective-permute-start | bytes 442376 | tf_op jit(solution)/shard_map/ppermute | solution.py:18
  41.1 6.8 %collective-permute-start.8 = (bf16[64,1152]{1,0:T(8,128)(2,1)S(1)}, bf16[64,1152]{1,0:T(8,128)(2,1)S(1)}, u32[]{:S(2)}, u32[]{:S(2)}) collective-permute-start(bf16[64,1152]{1,0:T(8,128)(2,1)S(1)} %get-tuple-element.100), channel_id=1, source_target_pairs={{0,2},{1,3},{2,0},{3,1},{4,6},{5,7},{6,4},{7,5},{8,10},{9,11},{10,... | collective-permute-start | bytes 442376 | tf_op jit(solution)/shard_map/ppermute | solution.py:18
  68.8 21.3 %collective-permute-start.24 = (bf16[32,1408]{1,0:T(8,128)(2,1)S(1)}, bf16[32,1408]{1,0:T(8,128)(2,1)S(1)}, u32[]{:S(2)}, u32[]{:S(2)}) collective-permute-start(bf16[32,1408]{1,0:T(8,128)(2,1)S(1)} %get-tuple-element.133), channel_id=1, source_target_pairs={{0,8},{4,12},{8,0},{12,4},{1,9},{5,13},{9,1},{13,5},{2,10},{6,14},... | collective-permute-start | bytes 270344 | tf_op jit(solution)/shard_map/ppermute | solution.py:18
  71.2 19.4 %collective-permute-start.25 = (bf16[32,1408]{1,0:T(8,128)(2,1)S(1)}, bf16[32,1408]{1,0:T(8,128)(2,1)S(1)}, u32[]{:S(2)}, u32[]{:S(2)}) collective-permute-start(bf16[32,1408]{1,0:T(8,128)(2,1)S(1)} %get-tuple-element.134), channel_id=1, source_target_pairs={{0,12},{4,8},{8,4},{12,0},{1,13},{5,9},{9,5},{13,1},{2,14},{6,10},... | collective-permute-start | bytes 270344 | tf_op jit(solution)/shard_map/ppermute | solution.py:18
  74.1 5.7 %collective-permute-start.20 = (bf16[32,2816]{1,0:T(8,128)(2,1)S(1)}, bf16[32,2816]{1,0:T(8,128)(2,1)S(1)}, u32[]{:S(2)}, u32[]{:S(2)}) collective-permute-start(bf16[32,2816]{1,0:T(8,128)(2,1)S(1)} %constant_dynamic-update-slice_fusion.refs_0_), channel_id=1, source_target_pairs={{0,3},{1,2},{2,1},{3,0},{4,7},{5,6},{6,5},{7,4},{8,11},{9,10},{10,... | collective-permute-start | bytes 540680 | tf_op jit(solution)/shard_map/ppermute | solution.py:18
  75.6 12.5 %collective-permute-start.19 = (bf16[32,2816]{1,0:T(8,128)(2,1)S(1)}, bf16[32,2816]{1,0:T(8,128)(2,1)S(1)}, u32[]{:S(2)}, u32[]{:S(2)}) collective-permute-start(bf16[32,2816]{1,0:T(8,128)(2,1)S(1)} %constant_dynamic-update-slice_fusion.refs_0_), channel_id=1, source_target_pairs={{0,2},{1,3},{2,0},{3,1},{4,6},{5,7},{6,4},{7,5},{8,10},{9,11},{10,... | collective-permute-start | bytes 540680 | tf_op jit(solution)/shard_map/ppermute | solution.py:18
  76.5 13.5 %collective-permute-start.18 = (bf16[32,2816]{1,0:T(8,128)(2,1)S(1)}, bf16[32,2816]{1,0:T(8,128)(2,1)S(1)}, u32[]{:S(2)}, u32[]{:S(2)}) collective-permute-start(bf16[32,2816]{1,0:T(8,128)(2,1)S(1)} %constant_dynamic-update-slice_fusion.refs_0_), channel_id=1, source_target_pairs={{0,1},{1,0},{2,3},{3,2},{4,5},{5,4},{6,7},{7,6},{8,9},{9,8},{10,11... | collective-permute-start | bytes 540680 | tf_op jit(solution)/shard_map/ppermute | solution.py:18
  79.8 12.6 %collective-permute-start.33 = (bf16[512,256]{1,0:T(8,128)(2,1)S(1)}, bf16[512,256]{1,0:T(8,128)(2,1)S(1)}, u32[]{:S(2)}, u32[]{:S(2)}) collective-permute-start(bf16[512,256]{1,0:T(8,128)(2,1)S(1)} %get-tuple-element.137), channel_id=1, source_target_pairs={{0,16},{16,0},{1,17},{17,1},{2,18},{18,2},{3,19},{19,3},{4,20},{20... | collective-permute-start | bytes 786440 | tf_op jit(solution)/shard_map/ppermute | solution.py:18
  90.1 8.2 %collective-permute-start.21 = (bf16[32,2816]{1,0:T(8,128)(2,1)S(1)}, bf16[32,2816]{1,0:T(8,128)(2,1)S(1)}, u32[]{:S(2)}, u32[]{:S(2)}) collective-permute-start(bf16[32,2816]{1,0:T(8,128)(2,1)S(1)} %collective-permute-done.18.refs_2_), channel_id=1, source_target_pairs={{0,16},{16,0},{1,17},{17,1},{2,18},{18,2},{3,19},{19,3},{4,20},{20... | collective-permute-start | bytes 540680 | tf_op jit(solution)/shard_map/ppermute | solution.py:18
  90.6 16.5 %collective-permute-start.31 = (bf16[32,2816]{1,0:T(8,128)(2,1)S(1)}, bf16[32,2816]{1,0:T(8,128)(2,1)}, u32[]{:S(2)}, u32[]{:S(2)}) collective-permute-start(bf16[32,2816]{1,0:T(8,128)(2,1)S(1)} %constant_dynamic-update-slice_fusion.2.refs_8_), channel_id=1, source_target_pairs={{0,3},{1,2},{2,1},{3,0},{4,7},{5,6},{6,5},{7,4},{8,11},{9,10},{10,... | collective-permute-start | bytes 540680 | tf_op jit(solution)/shard_map/ppermute | solution.py:18
  92.4 14.7 %collective-permute-start.29 = (bf16[32,2816]{1,0:T(8,128)(2,1)S(1)}, bf16[32,2816]{1,0:T(8,128)(2,1)}, u32[]{:S(2)}, u32[]{:S(2)}) collective-permute-start(bf16[32,2816]{1,0:T(8,128)(2,1)S(1)} %constant_dynamic-update-slice_fusion.2.refs_8_), channel_id=1, source_target_pairs={{0,2},{1,3},{2,0},{3,1},{4,6},{5,7},{6,4},{7,5},{8,10},{9,11},{10,... | collective-permute-start | bytes 540680 | tf_op jit(solution)/shard_map/ppermute | solution.py:18
  92.9 14.3 %collective-permute-start.27 = (bf16[32,2816]{1,0:T(8,128)(2,1)S(1)}, bf16[32,2816]{1,0:T(8,128)(2,1)}, u32[]{:S(2)}, u32[]{:S(2)}) collective-permute-start(bf16[32,2816]{1,0:T(8,128)(2,1)S(1)} %constant_dynamic-update-slice_fusion.2.refs_8_), channel_id=1, source_target_pairs={{0,1},{1,0},{2,3},{3,2},{4,5},{5,4},{6,7},{7,6},{8,9},{9,8},{10,11... | collective-permute-start | bytes 540680 | tf_op jit(solution)/shard_map/ppermute | solution.py:18
  93.3 6.4 %collective-permute-start.22 = (bf16[32,2816]{1,0:T(8,128)(2,1)S(1)}, bf16[32,2816]{1,0:T(8,128)(2,1)S(1)}, u32[]{:S(2)}, u32[]{:S(2)}) collective-permute-start(bf16[32,2816]{1,0:T(8,128)(2,1)S(1)} %collective-permute-done.19.refs_4_), channel_id=1, source_target_pairs={{0,16},{16,0},{1,17},{17,1},{2,18},{18,2},{3,19},{19,3},{4,20},{20... | collective-permute-start | bytes 540680 | tf_op jit(solution)/shard_map/ppermute | solution.py:18
  99.7 8.0 %collective-permute-start.26 = (bf16[32,2816]{1,0:T(8,128)(2,1)S(1)}, bf16[32,2816]{1,0:T(8,128)(2,1)S(1)}, u32[]{:S(2)}, u32[]{:S(2)}) collective-permute-start(bf16[32,2816]{1,0:T(8,128)(2,1)S(1)} %constant_dynamic-update-slice_fusion.2.refs_8_), channel_id=1, source_target_pairs={{0,16},{16,0},{1,17},{17,1},{2,18},{18,2},{3,19},{19,3},{4,20},{20... | collective-permute-start | bytes 540680 | tf_op jit(solution)/shard_map/ppermute | solution.py:18
  (36 other events, 169.8 us)
Sparse Core Ops, SparseCore 0:
  11.2 32.3 all-gather.4
  57.4 41.0 all-gather.6

commit v4 on v3

--- a/solution.py
+++ b/solution.py
@@ -40,7 +40,7 @@
 HBM = pl.BlockSpec(memory_space=pltpu.HBM)
 
 
-def call(body, outs, in_specs, scratch=(), mebibytes=4, out_specs=None):
+def call(body, outs, in_specs, scratch=(), mebibytes=4, out_specs=None, cost=None):
     return pl.pallas_call(
         body,
         out_shape=outs,
@@ -48,6 +48,7 @@
         out_specs=out_specs or [VMEM] * len(outs),
         scratch_shapes=list(scratch),
         compiler_params=pltpu.CompilerParams(vmem_limit_bytes=mebibytes << 20),
+        cost_estimate=cost,
     )
 
 
@@ -67,18 +68,21 @@
     return copy
 
 
-def side_of(column):
-    lane = lax.broadcasted_iota(jnp.int32, (column.shape[0], SIDE), 1)
-    high = column.astype(BF).astype(F32)
-    middle = (column - high).astype(BF).astype(F32)
-    low = column - high - middle
-    zero = jnp.zeros(lane.shape, F32)
-    picked = jnp.where(lane == 0, high, jnp.where(lane == 1, middle, jnp.where(lane == 2, low, zero)))
+def side_of(*columns):
+    lane = lax.broadcasted_iota(jnp.int32, (columns[0].shape[0], SIDE), 1)
+    picked = jnp.zeros(lane.shape, F32)
+    for place, column in enumerate(columns):
+        high = column.astype(BF).astype(F32)
+        middle = (column - high).astype(BF).astype(F32)
+        for part, piece in enumerate((high, middle, column - high - middle)):
+            picked = jnp.where(lane == 3 * place + part, piece, picked)
     return picked.astype(BF)
 
 
-def from_side(side):
-    return jnp.sum(side.astype(F32), axis=1, keepdims=True)
+def from_side(side, place=0):
+    lane = lax.broadcasted_iota(jnp.int32, side.shape, 1)
+    own = (lane >= 3 * place) & (lane < 3 * place + 3)
+    return jnp.sum(jnp.where(own, side.astype(F32), 0.0), axis=1, keepdims=True)
 
 
 def emit(part, norm, sents, gram=None):
@@ -113,6 +117,16 @@
                 summed = gram[rows, :] + got[:, columns].astype(F32)
                 gram_sum[rows, :] = summed.astype(gram_sum.dtype)
     return jnp.concatenate(parts, axis=0), jnp.concatenate(norms, axis=0)
+
+
+def repeat_kernel(array, repeated, sems):
+    rows = array.shape[0]
+    copies = [
+        start_copy(array, repeated.at[pl.ds(place * rows, rows), :], sems.at[place])
+        for place in range(repeated.shape[0] // rows)
+    ]
+    for copy in copies:
+        copy.wait()
 
 
 def start_kernel(with_gram, where, rows, value_a, value_b, *refs):
@@ -170,19 +184,28 @@
 
 def score_kernel(features, where, *refs):
     part_in, norm_in, got_top, got_low, middle, rows_squares, out_a, out_b = refs[:8]
-    scored, norm, out, sem = refs[8:]
-    fetch(where[0] == 1, out_b, out_a, out, sem)
+    scored, norm, repeated, out, sems = refs[8:]
+    fetch(where[0] == 1, out_b, out_a, out, sems.at[0])
     total, squares = absorb(part_in, norm_in, (got_top, got_low))
     values = (total * lax.rsqrt(squares / features + EPSILON)).astype(BF)
-    pltpu.make_async_copy(out_a, out, sem).wait()
+    pltpu.make_async_copy(out_a, out, sems.at[0]).wait()
     score = (middle[...].astype(F32) + matmul(values, out[...])).astype(BF)
     scored[...] = score
+    keep = score.shape[0]
+    copies = [
+        start_copy(scored, repeated.at[pl.ds(place * keep, keep), :], sems.at[1 + place])
+        for place in range(repeated.shape[0] // keep)
+    ]
     norm[...] = rows_squares[...] + square_sum(score)
+    for copy in copies:
+        copy.wait()
 
 
 def share_kernel(share, where, scored, norm, given, value_a, value_b, lout_a, lout_b, *refs):
-    kept, kept_norm = refs[:2]
-    peers, (value, lout, part, sent, sems) = refs[2:-5], refs[-5:]
+    every_row, kept, kept_norm, kept_count = refs[:4]
+    peers, (value, lout, part, sent, goals, sems) = refs[4:-6], refs[-6:]
+    sides = every_row.at[:, pl.ds(scored.shape[1], SIDE)]
+    goal_copy = start_copy(sides, goals, sems.at[sems.shape[0] - 1])
     first, at = where[0] == 1, where[1]
     fetch(first, value_b, value_a, value, sems.at[0])
     fetch(first, lout_b, lout_a, lout, sems.at[1])
@@ -202,11 +225,21 @@
     mine = pl.ds(pl.multiple_of(at * share, share), share)
     kept[...] = part[mine, :]
     kept_norm[...] = norm[mine, :]
+    goal_copy.wait()
+
+    def hits(goal):
+        shard = 1 + lax.broadcasted_iota(jnp.int32, goal.shape, 1)
+        return jnp.where(goal.astype(F32) == shard.astype(F32), 1.0, 0.0)
+
+    counts = jnp.sum(hits(goals[...]), axis=0, keepdims=True)
+    row = where[2] * scored.shape[0] + at * share
+    own = goals[pl.ds(pl.multiple_of(row, share), share), :]
+    kept_count[...] = jnp.maximum(jnp.sum(hits(own) * counts, axis=1, keepdims=True), 1.0)
     for copy in copies:
         copy.wait()
 
 
-def value_kernel(features, block, count, where, kept, norm, *refs):
+def value_kernel(features, block, count, where, kept, norm, shard_count, *refs):
     got, pieces, crossed = refs[:count], refs[count:-1], refs[-1]
     total, squares = kept[...], norm[...]
     inner = total.shape[1] // 2
@@ -215,7 +248,7 @@
         squares = squares + from_side(one[:, 2 * inner :])
     inverse = lax.rsqrt(squares / features + EPSILON)
     values = (total[:, :inner] * inverse).astype(BF)
-    side = side_of(inverse)
+    side = side_of(inverse, shard_count[...])
     crossed[...] = total[:, inner:].astype(BF)
     for away, piece in enumerate(pieces):
         if len(pieces) == 1:
@@ -228,77 +261,58 @@
         piece[:, reach:] = side
 
 
-def gradient_kernel(share, peers, aways, spots, dp_size, where, *refs):
-    groups = 1 + max(group for group, _ in spots)
-    count = 2 * peers * groups
+def gradient_kernel(share, peers, aways, spots, other, where, *refs):
+    count = peers * (1 + max(group for group, _ in spots))
     sources, refs = refs[:count], refs[count:]
-    inputs, dense = refs[:2], refs[2:-12]
-    parts, grad_value, grad_out, tokens, x, slopes, normed, back, share_count = refs[-12:-3]
-    lout, gram, sems = refs[-3:]
-    given = dense[2:]
+    every_row, every_scored, lout_in, gram_in, grad_value, grad_out = refs[:6]
+    tokens, x, slopes, normed, back, lout, gram, sems = refs[6:]
     first, dp_at, mp_at = where[0] == 1, where[1], where[2]
+    take_row = jnp.logical_not(first) if other else first
     keep = share * peers
     width, inner, block = x.shape[1], lout.shape[0], gram.shape[1]
     piece = inner + block + SIDE
-    total = tokens.shape[0]
     copies = []
 
     def begin(source, target):
         copies.append(start_copy(source, target, sems.at[len(copies)]))
 
-    begin(dense[0], lout)
-    begin(dense[1], gram)
-    for array, target in zip(given, (grad_value, grad_out)):
-        begin(array, target)
+    begin(lout_in, lout)
+    begin(gram_in, gram)
     ready = []
     for number, (away, (group, place)) in enumerate(zip(aways, spots)):
-        for side in range(2):
-            segment = jnp.where(first, side, 1 - side)
-            start = (2 * number + side) * keep
-            row = pl.multiple_of((segment * dp_size + (dp_at ^ away)) * keep, keep)
-            share_count[start : start + keep, :] = parts[pl.ds(row, keep), :]
-            target = x.at[pl.ds(start, keep), :]
-            if away == 0:
-                begin(inputs[side], target)
-            else:
-                here, sem = pl.ds(row, keep), sems.at[len(copies)]
-                fetch(first, inputs[0].at[here, pl.ds(0, width)], inputs[1].at[here, :], target, sem)
-                copies.append(pltpu.make_async_copy(inputs[1].at[here, :], target, sem))
-            for mask in range(peers):
-                source = sources[2 * (group * peers + mask) + side]
-                at = pl.multiple_of(start + (mp_at ^ mask) * share, share)
-                begin(
-                    source.at[:, pl.ds(place * piece, piece)],
-                    tokens.at[pl.ds(at, share), :],
-                )
+        start = number * keep
+        here = pl.ds(pl.multiple_of((dp_at ^ away) * keep, keep), keep)
+        target, sem = x.at[pl.ds(start, keep), :], sems.at[len(copies)]
+        scored = every_scored.at[here, :]
+        fetch(take_row, every_row.at[here, pl.ds(0, width)], scored, target, sem)
+        copies.append(pltpu.make_async_copy(scored, target, sem))
+        for mask in range(peers):
+            at = pl.multiple_of(start + (mp_at ^ mask) * share, share)
+            source = sources[group * peers + mask].at[:, pl.ds(place * piece, piece)]
+            begin(source, tokens.at[pl.ds(at, share), :])
         ready.append(len(copies))
-    fixed = 2 + len(given)
-    for copy in copies[:2]:
-        copy.wait()
-    done = fixed
+    done = 0
     for number, until in enumerate(ready):
         for copy in copies[done:until]:
             copy.wait()
         done = until
-        here = pl.ds(2 * keep * number, 2 * keep)
+        here = pl.ds(keep * number, keep)
         wide = x[here, :].astype(F32)
         values = tokens[here, :inner]
-        inverse = from_side(tokens[here, inner + block :])
-        portion = share_count[here, :]
+        side = tokens[here, inner + block :]
+        portion = 1.0 / from_side(side, 1)
         slopes[here, :] = ((wide + matmul(values, lout[...])) * portion).astype(BF)
-        normed[here, :] = (wide * inverse).astype(BF)
+        normed[here, :] = (wide * from_side(side)).astype(BF)
         crossed = tokens[here, inner : inner + block].astype(F32)
         back[here, :] = ((crossed + matmul(values, gram[...])) * portion).astype(BF)
-    for copy in copies[2:fixed]:
-        copy.wait()
     column = pl.ds(pl.multiple_of(dp_at * block, block), block)
-    value_sum = matmul_tn(back[...], normed[...])
-    out_sum = matmul_tn(tokens[:, column], slopes[...])
-    if given:
-        value_sum = value_sum + grad_value[...]
-        out_sum = out_sum + grad_out[...]
-    grad_value[...] = value_sum
-    grad_out[...] = out_sum
+    grad_value[...] = matmul_tn(back[...], normed[...]).astype(grad_value.dtype)
+    grad_out[...] = matmul_tn(tokens[:, column], slopes[...]).astype(grad_out.dtype)
+
+
+def add_kernel(value_near, out_near, value_far, out_far, grad_value, grad_out):
+    grad_value[...] = value_near[...] + value_far[...].astype(F32)
+    grad_out[...] = out_near[...] + out_far[...].astype(F32)
 
 
 def square_sum(value):
@@ -344,12 +358,17 @@
     pick = (keep_index[0][:, None] == jnp.arange(candidates.shape[0])[None, :]) & is_live[:, None]
     rows = matmul(pick.astype(BF), candidates).astype(BF)
     goal = jnp.where(is_live, keep_dest[0] + 1, 0).astype(F32)[:, None]
-    every_row = lax.all_gather(
-        jnp.concatenate([rows, jnp.broadcast_to(goal, (keep, SIDE)).astype(BF)], axis=1),
-        ("segment", "dp"),
-        axis=0,
-        tiled=False,
-    )
+    rows_wide = jnp.concatenate([rows, jnp.broadcast_to(goal, (keep, SIDE)).astype(BF)], axis=1)
+
+    def repeat(array):
+        return call(
+            repeat_kernel,
+            [pltpu.HBM((dp_size * keep, array.shape[1]), BF)],
+            [VMEM],
+            [pltpu.SemaphoreType.DMA((dp_size,))],
+            out_specs=[HBM],
+
+        )(array)[0]
 
     gram = matmul_nt(own_lout, lax.dynamic_slice_in_dim(own_lout, dp_at * block, block, 0))
     half = inner // 2
@@ -369,7 +388,7 @@
         wide_state = sums + [jax.ShapeDtypeStruct((half_rows, inner + SIDE + extra), BF)] * 2
         wide_state.append(jax.ShapeDtypeStruct((half, block), F32))
     hidden_type = jax.ShapeDtypeStruct((keep, width), BF)
-    where = jnp.stack([flag, mp_at])
+    where = jnp.stack([flag, mp_at, dp_at])
     weight = pltpu.VMEM(own_value.shape, BF)
 
     def placed(*arrays):
@@ -386,6 +405,7 @@
         mebibytes=12,
     )(where, rows, *placed(own_value, other_value), *((kept_half, got_half) if direct else ()))
     part, rows_squares, sents, gram_sum = halves(outs)
+    every_row = lax.all_to_all(repeat(rows_wide), "dp", 0, 0, tiled=True)
     own_out, own_lvalue, own_lout, sents = lax.optimization_barrier(
         (own_out, own_lvalue, own_lout, sents)
     )
@@ -420,47 +440,58 @@
     part, norm, sents, _ = halves(outs)
     sents, given = lax.optimization_barrier((sents, given))
     got = exchange(*sents, 2, 1)
-    part, goals = lax.optimization_barrier((part, every_row[:, :, width]))
 
     long = 2 * inner + SIDE
-    scored, norm = call(
+    scored, norm, repeated = call(
         functools.partial(score_kernel, scorer_width),
-        [hidden_type, sums[1]],
+        [hidden_type, sums[1], pltpu.HBM((dp_size * keep, width), BF)],
         [SMEM] + [VMEM] * 6 + [HBM] * 2,
-        [weight, pltpu.SemaphoreType.DMA],
-        mebibytes=8,
-    )(where, part, norm, *got, middle, rows_squares, *placed(own_out, other_out))
-    every_scored = lax.all_gather(scored, ("segment", "dp"), axis=0, tiled=False)
+        [weight, pltpu.SemaphoreType.DMA((dp_size + 1,))],
+        mebibytes=10,
+        out_specs=[VMEM, VMEM, HBM],
+    )(
+        where,
+        part,
+        norm,
+        *got,
+        middle,
+        rows_squares,
+        *placed(own_out, other_out),
+    )
+    every_scored = lax.all_to_all(repeated, "dp", 0, 0, tiled=True)
     outs = call(
         functools.partial(share_kernel, share),
         [
             jax.ShapeDtypeStruct((share, 2 * inner), F32),
             jax.ShapeDtypeStruct((share, 1), F32),
+            jax.ShapeDtypeStruct((share, 1), F32),
         ]
         + [pltpu.HBM((share, long), BF)] * (mp_size - 1),
-        [SMEM] + [VMEM] * 3 + [HBM] * 4,
+        [SMEM] + [VMEM] * 3 + [HBM] * 5,
         [
             weight,
             weight,
             pltpu.VMEM((keep, 2 * inner), F32),
             pltpu.VMEM((keep, long), BF),
-            pltpu.SemaphoreType.DMA((mp_size + 1,)),
+            pltpu.VMEM((dp_size * keep, SIDE), BF),
+            pltpu.SemaphoreType.DMA((mp_size + 2,)),
         ],
         mebibytes=12,
-        out_specs=[VMEM] * 2 + [HBM] * (mp_size - 1),
-    )(where, scored, norm, given, *learner_weights)
-    kept, kept_norm = outs[:2]
+        out_specs=[VMEM] * 3 + [HBM] * (mp_size - 1),
+    )(where, scored, norm, given, *learner_weights, every_row)
+    kept, kept_norm, shard_count = outs[:3]
+
     got = lax.optimization_barrier(
-        tuple(flip(peer, "mp", mask) for mask, peer in enumerate(outs[2:], 1))
+        tuple(flip(peer, "mp", mask) for mask, peer in enumerate(outs[3:], 1))
     )
     pieces = call(
         functools.partial(value_kernel, learner_width, block, mp_size - 1),
         [jax.ShapeDtypeStruct((share, inner + block + SIDE), BF)] * dp_size
         if direct
         else [jax.ShapeDtypeStruct((share, long), BF)],
-        [SMEM] + [VMEM] * (mp_size + 1),
+        [SMEM] + [VMEM] * (mp_size + 2),
         [pltpu.VMEM((share, inner), BF)],
-    )(jnp.stack([dp_at]), kept, kept_norm, *got)
+    )(jnp.stack([dp_at]), kept, kept_norm, shard_count, *got)
 
     if direct:
         gram_half = gram_sum[0]
@@ -473,10 +504,6 @@
         jnp.concatenate([gram_other, gram_half], axis=0),
     )
 
-    goals = goals.astype(jnp.int32).reshape(2, dp_size, keep)
-    hits = goals[:, :, :, None] == jnp.arange(1, dp_size + 1)
-    counts = jnp.sum(hits.astype(F32), axis=(1, 2), keepdims=True)
-    parts = 1.0 / jnp.maximum(jnp.sum(jnp.where(hits, counts, 0.0), axis=3), 1.0)
     column = dp_at * block
 
     def spread(piece):
@@ -486,82 +513,62 @@
             whole = lax.dynamic_update_slice(whole, got, ((mp_at ^ mask) * share, 0))
         return whole
 
-    def add(grads, pieces, places):
-        pieces = jnp.concatenate(pieces, axis=0)
-        tokens = jnp.concatenate([pieces, flip(pieces, "segment", 1)], axis=0)
-        x, share_count = [], []
-        for segment in (at, 1 - at):
-            for place in places:
-                row = lax.dynamic_index_in_dim(every_row, segment * dp_size + place, 0, False)
-                score = lax.dynamic_index_in_dim(every_scored, segment * dp_size + place, 0, False)
-                x.append(jnp.where(first, row[:, :width], score))
-                share_count.append(lax.dynamic_slice(parts, (segment, place, 0), (1, 1, keep)))
-        x = jnp.concatenate(x, axis=0).astype(F32)
-        share_count = jnp.concatenate([part.reshape(keep, 1) for part in share_count], axis=0)
+    def add(grads, tokens, place):
         v = tokens[:, :inner]
         xo = tokens[:, inner : inner + block].astype(F32)
         inv = unpack(tokens[:, inner + block :], 0)
-        slopes = ((x + matmul(v, own_lout)) * share_count).astype(BF)
-        normed = (x * inv).astype(BF)
+        share_count = 1.0 / unpack(tokens[:, inner + block :], 1)
         back = ((xo + matmul(v, gram)) * share_count).astype(BF)
         v_block = lax.dynamic_slice_in_dim(v, column, block, 1)
-        return (grads[0] + matmul_tn(back, normed), grads[1] + matmul_tn(v_block, slopes))
+        row = lax.dynamic_slice(every_row, (place * keep, 0), (keep, width))
+        score = lax.dynamic_slice_in_dim(every_scored, place * keep, keep, 0)
+        added = []
+        for x, lout in (
+            (jnp.where(first, row, score), own_lout),
+            (jnp.where(first, score, row), other_lout),
+        ):
+            x = x.astype(F32)
+            slopes = ((x + matmul(v, lout)) * share_count).astype(BF)
+            normed = (x * inv).astype(BF)
+            added += [matmul_tn(back, normed), matmul_tn(v_block, slopes)]
+        return [grad + new for grad, new in zip(grads, added)]
 
     if direct:
         moved = [flip(pieces[away], "dp", away) for away in range(1, dp_size)]
-        stacks = [[pieces[0]] + moved[:1], moved[1:]]
-
-        def all_shares(stack):
-            stack = jnp.concatenate(stack, axis=1) if len(stack) > 1 else stack[0]
-            return [stack] + [flip(stack, "mp", mask) for mask in range(1, mp_size)]
-
-        def both_cores(nears):
-            return [array for near in nears for array in (near, flip(near, "segment", 1))]
-
-        swap = flip(jnp.where(first, scored, rows), "segment", 1)
-        near_x = jnp.where(first, rows, scored)
-        whole = parts.reshape(2 * dp_size * keep, 1)
-        where = jnp.stack([flag, dp_at, mp_at])
-
-        def gradients(aways, spots, groups, inputs, given, mebibytes):
-            tokens = 2 * len(aways) * keep
-            dense = [own_lout, gram, *given]
+        soon = min(3, mp_size)
+        own = [pieces[0]] + [flip(pieces[0], "mp", mask) for mask in range(1, soon)]
+        moved, own, diagonal = lax.optimization_barrier((moved, own, pieces[0]))
+        own += [flip(diagonal, "mp", mask) for mask in range(soon, mp_size)]
+        rest = jnp.concatenate(moved, axis=1) if moved else None
+        places_at = jnp.stack([flag, dp_at, mp_at])
+
+        def gradients(aways, spots, groups, inputs, other, kind):
+            tokens = len(aways) * keep
             return call(
-                functools.partial(gradient_kernel, share, mp_size, aways, spots, dp_size),
-                [jax.ShapeDtypeStruct((block, width), F32)] * 2,
-                [SMEM] + [HBM] * (len(groups) + 2 + len(dense)) + [VMEM],
+                functools.partial(gradient_kernel, share, mp_size, aways, spots, other),
+                [jax.ShapeDtypeStruct((block, width), kind)] * 2,
+                [SMEM] + [HBM] * (len(groups) + 4),
                 [
                     pltpu.VMEM((tokens, inner + block + SIDE), BF),
                     pltpu.VMEM((tokens, width), BF),
                     pltpu.VMEM((tokens, width), BF),
                     pltpu.VMEM((tokens, width), BF),
                     pltpu.VMEM((tokens, block), BF),
-                    pltpu.VMEM((tokens, 1), F32),
                     pltpu.VMEM(own_lout.shape, BF),
                     pltpu.VMEM(gram.shape, BF),
-                    pltpu.SemaphoreType.DMA((2 * len(aways) * (mp_size + 1) + len(dense),)),
+                    pltpu.SemaphoreType.DMA((len(aways) * (mp_size + 1) + 2,)),
                 ],
-                mebibytes=mebibytes,
-            )(where, *placed(*groups, *inputs, *dense), whole)
-
-        early = all_shares(stacks[0])
-        early[1:] = lax.optimization_barrier(early[1:])
-        groups = both_cores(early)
-        grads = gradients((0,), ((0, 0),), groups, (near_x, swap), (), 14)
+                mebibytes=16,
+            )(places_at, *placed(*groups, *inputs, other_lout if other else own_lout, gram))
+
+        groups, spots = own, ((0, 0),)
         if dp_size > 1:
-            spots = ((0, 1),)
-            if dp_size > 2:
-                *stack, _ = lax.optimization_barrier((*stacks[1], early[1:]))
-                late = all_shares(stack)
-                last, grads = lax.optimization_barrier((late[-1], grads))
-                groups = groups + both_cores(late[:-1] + [last])
-                spots += tuple((1, place) for place in range(dp_size - 2))
-            tokens = 2 * dp_size * keep
-            inputs = (
-                every_row.reshape(tokens, width + SIDE),
-                every_scored.reshape(tokens, width),
-            )
-            grads = gradients(tuple(range(1, dp_size)), spots, groups, inputs, grads, 22)
+            groups = own + [rest] + [flip(rest, "mp", mask) for mask in range(1, mp_size)]
+            spots += tuple((1, place) for place in range(dp_size - 1))
+        inputs = (every_row, every_scored)
+        aways = tuple(range(dp_size))
+        far = gradients(aways, spots, groups, inputs, True, BF)
+        near = gradients(aways, spots, groups, inputs, False, F32)
     else:
         ring = [(source, (source + 1) % dp_size) for source in range(dp_size)]
 
@@ -569,11 +576,19 @@
             grads, full = carry
             cross = lax.dynamic_slice_in_dim(full, inner + column, block, 1)
             piece = jnp.concatenate([full[:, :inner], cross, full[:, 2 * inner :]], axis=1)
-            grads = add(grads, [spread(piece)], [(dp_at - step) % dp_size])
+            grads = add(grads, spread(piece), (dp_at - step) % dp_size)
             return grads, lax.ppermute(full, "dp", ring)
 
-        grads = (jnp.zeros((block, width), F32), jnp.zeros((block, width), F32))
+        grads = [jnp.zeros((block, width), F32)] * 4
         grads, _ = lax.fori_loop(0, dp_size, turn, (grads, pieces[0]))
+        near, far = grads[:2], [grad.astype(BF) for grad in grads[2:]]
+    got = [flip(sent, "segment", 1) for sent in far]
+    grads = call(
+        add_kernel,
+        [jax.ShapeDtypeStruct((block, width), F32)] * 2,
+        [VMEM] * 4,
+        mebibytes=10,
+    )(*near, *got)
     return (grads[0][None], grads[1][None])
 
 

time: 127 us -> 114 us (0.90); the launches traced: 126 us -> 114 us
  between operations: 15 us -> 1.6 us
  local copies, waits for them, and re-layouts: 10.5 us -> 1.01 us
  waiting for transfers between devices: 23 us -> 31.1 us
  starting transfers between devices: 36.7 us -> 44.1 us
  other arithmetic: 4.56 us -> 1.21 us
    all_to_all x0 -> x2, starting transfers between devices: none -> 9.63 us  [the longest x1 4.86 us: on_device(): every_scored = lax.all_to_all(repeated, 'dp', 0, 0, tiled=True)]
    ppermute x35 -> x28, waiting for transfers between devices: 22.9 us -> 31.1 us  [flip(): return lax.ppermute(value, axis, pairs)]
    unnamed x49 -> x28, local copies, waits for them, and re-layouts: 8.47 us -> 0.83 us
    ppermute x35 -> x28, starting transfers between devices: 36.7 us -> 34.4 us  [flip(): return lax.ppermute(value, axis, pairs)]
    select_n x1 -> x0, other arithmetic: 1.69 us -> none  [on_device(): swap = flip(jnp.where(first, scored, rows), 'segment', 1)]
    slice x1 -> x0, local copies, waits for them, and re-layouts: 1.67 us -> none  [on_device(): part, goals = lax.optimization_barrier((part, every_row[:, :, width]))]
    pallas_call x2 -> x4, Pallas kernels: 13.1 us -> 13.7 us  [the longest x2 11.2 us: gradients(): call(functools.partial(gradient_kernel, share, mp_size, aways, spots, oth...]
  transfers between devices with their start and end apart: 37 -> 30, of which waited for: 12 -> 13; matrix products, arithmetic and copies ran while one was open for 9% -> 4% of each run, Pallas kernels for 16% -> 20%
where the time goes in v4:
time: 114 us
  starting transfers between devices  44.1 us (39%)
  Pallas kernels  32.1 us (28%)
  waiting for transfers between devices  31.1 us (27%)
  matrix products  2.79 us (2%)
  between operations  1.6 us (1%)
  other arithmetic  1.21 us (1%)
    ppermute x28, starting transfers between devices, flip(): return lax.ppermute(value, axis, pairs)  34.4 us
    ppermute x28, waiting for transfers between devices, flip(): return lax.ppermute(value, axis, pairs)  31.1 us
    pallas_call x2, Pallas kernels, gradients(): call(functools.partial(gradient_kernel, share, mp_size, aways, spots, oth...  11.2 us
    all_to_all x1, starting transfers between devices, on_device(): every_scored = lax.all_to_all(repeated, 'dp', 0, 0, tiled=True)  4.86 us
    all_to_all x1, starting transfers between devices, on_device(): every_row = lax.all_to_all(repeat(rows_wide), 'dp', 0, 0, tiled=True)  4.77 us
    pallas_call x1, Pallas kernels, on_device(): call(functools.partial(share_kernel, share), [jax.ShapeDtypeStruct((share...  4.41 us
    pallas_call x1, Pallas kernels, on_device(): call(functools.partial(score_kernel, scorer_width), [hidden_type, sums[1]...  3.7 us
    pallas_call x1, Pallas kernels, on_device(): call(learn_kernel, [jax.ShapeDtypeStruct((keep, 2 * inner), F32)], [SMEM,...  3.61 us
  transfers between devices with their start and end apart: 30, of which 13 were waited for; matrix products, arithmetic and copies ran while one was open for 4% of the time, Pallas kernels for 20%

profile of v4, /device:TPU:11, one launch (start us, length us, event | category | flops | bytes accessed | tf_op | source)
XLA Modules:
  0.0 113.9 jit_solution(11073095887865585514)
XLA Ops:
  1.4 2.5 %fusion = f32[256,1024]{0,1:T(8,128)S(1)} fusion(bf16[1,1024,1024]{2,1,0:T(8,128)(2,1)} %param.12, s32[]{:T(128)S(6)} %select_n.25), kind=kOutput, calls=%fused_computation.2 | convolution fusion | flops 536870912 | bytes 3670020 | tf_op jit(solution)/shard_map/dot_general | solution.py:26
  5.6 2.7 %shard_map.95 = (f32[128,1024]{1,0:T(8,128)S(1)}, f32[128,1]{1,0:T(8,128)S(1)}, bf16[64,2176]{1,0:T(8,128)(2,1)S(1)}, bf16[64,2176]{1,0:T(8,128)(2,1)S(1)}, f32[512,256]{1,0:T(8,128)S(1)}) custom-call(s32[3]{0:T(128)S(1)} %pad_add_fusion.1.where, bf16[128,1024]{1,0:T(8,128)(2,1)S(1)} %convolution_convert_fusion.rows.refs_4_, bf16[1024,1024]{1,0:T(8,128)(2,1)} %bitcast.37, ...), custom_call_target="tpu_custom_call" | custom-call | tf_op jit(solution)/shard_map/pallas_call | solution.py:400
  10.4 4.8 %all-to-all-start = ((bf16[4,128,1152]{2,1,0:T(8,128)(2,1)}), bf16[4,128,1152]{2,1,0:T(8,128)(2,1)S(1)}, u32[]{:S(2)}, u32[]{:S(2)}) async-start(bf16[4,128,1152]{2,1,0:T(8,128)(2,1)} %bitcast.39), calls=%async_computation | async-start | bytes 2359296 | tf_op jit(solution)/shard_map/all_to_all | solution.py:408
  15.4 1.2 %collective-permute-start.3 = (bf16[64,2176]{1,0:T(8,128)(2,1)S(1)}, bf16[64,2176]{1,0:T(8,128)(2,1)S(1)}, u32[]{:S(2)}, u32[]{:S(2)}) collective-permute-start(bf16[64,2176]{1,0:T(8,128)(2,1)S(1)} %get-tuple-element.82), channel_id=1, source_target_pairs={{0,2},{1,3},{2,0},{3,1},{4,6},{5,7},{6,4},{7,5},{8,10},{9,11},{10,... | collective-permute-start | bytes 835592 | tf_op jit(solution)/shard_map/ppermute | solution.py:18
  16.6 6.2 %collective-permute-done.2.got_top = bf16[64,2176]{1,0:T(8,128)(2,1)S(1)} collective-permute-done((bf16[64,2176]{1,0:T(8,128)(2,1)}, bf16[64,2176]{1,0:T(8,128)(2,1)S(1)}, u32[]{:S(2)}, u32[]{:S(2)}) %collective-permute-start.2) | collective-permute-done | bytes 278560 | tf_op jit(solution)/shard_map/ppermute | solution.py:18
  23.1 1.3 %collective-permute-start.4 = (bf16[64,2176]{1,0:T(8,128)(2,1)S(1)}, bf16[64,2176]{1,0:T(8,128)(2,1)S(1)}, u32[]{:S(2)}, u32[]{:S(2)}) collective-permute-start(bf16[64,2176]{1,0:T(8,128)(2,1)S(1)} %get-tuple-element.90), channel_id=1, source_target_pairs={{0,2},{1,3},{2,0},{3,1},{4,6},{5,7},{6,4},{7,5},{8,10},{9,11},{10,... | collective-permute-start | bytes 835592 | tf_op jit(solution)/shard_map/ppermute | solution.py:18
  25.4 4.3 %collective-permute-done.4.refs_2_ = bf16[64,2176]{1,0:T(8,128)(2,1)S(1)} collective-permute-done((bf16[64,2176]{1,0:T(8,128)(2,1)S(1)}, bf16[64,2176]{1,0:T(8,128)(2,1)S(1)}, u32[]{:S(2)}, u32[]{:S(2)}) %collective-permute-start.4) | collective-permute-done | bytes 278560 | tf_op jit(solution)/shard_map/ppermute | solution.py:18
  30.7 3.3 %shard_map.97 = (bf16[128,1024]{1,0:T(8,128)(2,1)S(1)}, f32[128,1024]{1,0:T(8,128)S(1)}, f32[128,1]{1,0:T(8,128)S(1)}, bf16[64,1152]{1,0:T(8,128)(2,1)S(1)}, bf1...) custom-call(s32[3]{0:T(128)S(1)} %pad_add_fusion.1.where, f32[128,1024]{1,0:T(8,128)S(1)} %get-tuple-element.86.refs_0_, ...), custom_call_target="tpu_custom_call" | custom-call | tf_op jit(solution)/shard_map/pallas_call | solution.py:421
  35.0 3.6 %shard_map.99.given = f32[128,2048]{1,0:T(8,128)S(1)} custom-call(s32[3]{0:T(128)S(1)} %pad_add_fusion.1.where, bf16[128,1024]{1,0:T(8,128)(2,1)S(1)} %convolution_convert_fusion.rows.refs_4_, bf16[1024,1024]{1,0:T(8,128)(2,1)} %bitcast.11.value_a, bf16[1024,1024]{1,0:T(8,128)(2,1)} %collective-permute-done.9.value_b, ...), custom_call_target="tpu_custom_call" | custom-call | tf_op jit(solution)/shard_map/pallas_call | solution.py:431
  40.9 3.2 %collective-permute-done.11.refs_2_ = bf16[64,1152]{1,0:T(8,128)(2,1)S(1)} collective-permute-done((bf16[64,1152]{1,0:T(8,128)(2,1)S(1)}, bf16[64,1152]{1,0:T(8,128)(2,1)S(1)}, u32[]{:S(2)}, u32[]{:S(2)}) %collective-permute-start.11) | collective-permute-done | bytes 147488 | tf_op jit(solution)/shard_map/ppermute | solution.py:18
  44.1 3.7 %shard_map.100 = (bf16[128,1024]{1,0:T(8,128)(2,1)S(1)}, f32[128,1]{1,0:T(8,128)S(1)}, bf16[512,1024]{1,0:T(8,128)(2,1)}) custom-call(s32[3]{0:T(128)S(1)} %pad_add_fusion.1.where, f32[128,1024]{1,0:T(8,128)S(1)} %get-tuple-element.104.refs_0_, f32[128,1]{1,0:T(8,128)S(1)} %get-tuple-element.105.refs_1_, ...), custom_call_target="tpu_custom_call" | custom-call | tf_op jit(solution)/shard_map/pallas_call | solution.py:445
  47.8 4.9 %all-to-all-start.1 = ((bf16[4,128,1024]{2,1,0:T(8,128)(2,1)}), bf16[4,128,1024]{2,1,0:T(8,128)(2,1)}, u32[]{:S(2)}, u32[]{:S(2)}) async-start(bf16[4,128,1024]{2,1,0:T(8,128)(2,1)} %bitcast.40), calls=%async_computation.1 | async-start | bytes 2097152 | tf_op jit(solution)/shard_map/all_to_all | solution.py:461
  52.7 4.4 %shard_map.102 = (f32[32,2048]{1,0:T(8,128)S(1)}, f32[32,1]{1,0:T(8,128)S(1)}, f32[32,1]{1,0:T(8,128)S(1)}, bf16[32,2176]{1,0:T(8,128)(2,1)}, bf16[32,2176]{1,0:T(8,128)(2,1)}, /*index=5*/bf16[32,2176]{1,0:T(8,128)(2,1)}) custom-call(s32[3]{0:T(128)S(1)} %pad_add_fusion.1.where, bf16[128,1024]{1,0:T(8,128)(2,1)S(1)} %get-tuple-element.117.scored, ...), custom_call_target="tpu_custom_call" | custom-call | tf_op jit(solution)/shard_map/pallas_call | solution.py:462
  59.8 1.9 %collective-permute-done.13.refs_0_ = bf16[32,2176]{1,0:T(8,128)(2,1)S(1)} collective-permute-done((bf16[32,2176]{1,0:T(8,128)(2,1)}, bf16[32,2176]{1,0:T(8,128)(2,1)S(1)}, u32[]{:S(2)}, u32[]{:S(2)}) %collective-permute-start.13) | collective-permute-done | bytes 139296 | tf_op jit(solution)/shard_map/ppermute | solution.py:18
  64.6 1.7 %collective-permute-start.17 = (bf16[32,1408]{1,0:T(8,128)(2,1)S(1)}, bf16[32,1408]{1,0:T(8,128)(2,1)S(1)}, u32[]{:S(2)}, u32[]{:S(2)}) collective-permute-start(bf16[32,1408]{1,0:T(8,128)(2,1)S(1)} %get-tuple-element.130), channel_id=1, source_target_pairs={{0,8},{4,12},{8,0},{12,4},{1,9},{5,13},{9,1},{13,5},{2,10},{6,14},... | collective-permute-start | bytes 270344 | tf_op jit(solution)/shard_map/ppermute | solution.py:18
  68.8 9.1 %collective-permute-start.25 = (bf16[512,256]{1,0:T(8,128)(2,1)S(1)}, bf16[512,256]{1,0:T(8,128)(2,1)S(1)}, u32[]{:S(2)}, u32[]{:S(2)}) collective-permute-start(bf16[512,256]{1,0:T(8,128)(2,1)S(1)} %get-tuple-element.141), channel_id=1, source_target_pairs={{0,16},{16,0},{1,17},{17,1},{2,18},{18,2},{3,19},{19,3},{4,20},{20... | collective-permute-start | bytes 786440 | tf_op jit(solution)/shard_map/ppermute | solution.py:18
  77.9 4.2 %collective-permute-done.18 = bf16[32,1408]{1,0:T(8,128)(2,1)S(1)} collective-permute-done((bf16[32,1408]{1,0:T(8,128)(2,1)S(1)}, bf16[32,1408]{1,0:T(8,128)(2,1)S(1)}, u32[]{:S(2)}, u32[]{:S(2)}) %collective-permute-start.18) | collective-permute-done | bytes 90144 | tf_op jit(solution)/shard_map/ppermute | solution.py:18
  82.2 1.5 %collective-permute-start.22 = (bf16[32,4224]{1,0:T(8,128)(2,1)S(1)}, bf16[32,4224]{1,0:T(8,128)(2,1)S(1)}, u32[]{:S(2)}, u32[]{:S(2)}) collective-permute-start(bf16[32,4224]{1,0:T(8,128)(2,1)S(1)} %constant_dynamic-update-slice_fusion.refs_4_), channel_id=1, source_target_pairs={{0,1},{1,0},{2,3},{3,2},{4,5},{5,4},{6,7},{7,6},{8,9},{9,8},{10,11... | collective-permute-start | bytes 811016 | tf_op jit(solution)/shard_map/ppermute | solution.py:18
  83.6 1.3 %collective-permute-start.24 = (bf16[32,4224]{1,0:T(8,128)(2,1)S(1)}, bf16[32,4224]{1,0:T(8,128)(2,1)S(1)}, u32[]{:S(2)}, u32[]{:S(2)}) collective-permute-start(bf16[32,4224]{1,0:T(8,128)(2,1)S(1)} %constant_dynamic-update-slice_fusion.refs_4_), channel_id=1, source_target_pairs={{0,3},{1,2},{2,1},{3,0},{4,7},{5,6},{6,5},{7,4},{8,11},{9,10},{10,... | collective-permute-start | bytes 811016 | tf_op jit(solution)/shard_map/ppermute | solution.py:18
  87.1 6.8 %collective-permute-done.21.refs_3_ = bf16[32,1408]{1,0:T(8,128)(2,1)S(1)} collective-permute-done((bf16[32,1408]{1,0:T(8,128)(2,1)S(1)}, bf16[32,1408]{1,0:T(8,128)(2,1)S(1)}, u32[]{:S(2)}, u32[]{:S(2)}) %collective-permute-start.21) | collective-permute-done | bytes 90144 | tf_op jit(solution)/shard_map/ppermute | solution.py:18
  95.2 5.6 %shard_map.105 = (bf16[256,1024]{1,0:T(8,128)(2,1)S(1)}, bf16[256,1024]{1,0:T(8,128)(2,1)S(1)}) custom-call(s32[3]{0:T(128)S(1)} %pad_add_fusion.where, bf16[32,1408]{1,0:T(8,128)(2,1)} %copy-done.2, bf16[32,1408]{1,0:T(8,128)(2,1)} %copy-done.8, bf16[32,1408]{1,0:T(8,128)(2,1)} %copy-done.9, bf16[32,1408]{1,0:T(8,128)(2,1)} %copy-done.10, ...), custom_call_target="tpu_custom_call" | custom-call | tf_op jit(solution)/shard_map/pallas_call | solution.py:547
  100.8 5.9 %collective-permute-start.26 = (bf16[256,1024]{1,0:T(8,128)(2,1)S(1)}, bf16[256,1024]{1,0:T(8,128)(2,1)S(1)}, u32[]{:S(2)}, u32[]{:S(2)}) collective-permute-start(bf16[256,1024]{1,0:T(8,128)(2,1)S(1)} %get-tuple-element.144), channel_id=1, source_target_pairs={{0,16},{16,0},{1,17},{17,1},{2,18},{18,2},{3,19},{19,3},{4,20},{20... | collective-permute-start | bytes 1572872 | tf_op jit(solution)/shard_map/ppermute | solution.py:18
  106.8 5.6 %shard_map.104 = (f32[256,1024]{1,0:T(8,128)S(1)}, f32[256,1024]{1,0:T(8,128)S(1)}) custom-call(s32[3]{0:T(128)S(1)} %pad_add_fusion.where, bf16[32,1408]{1,0:T(8,128)(2,1)} %copy-done.2, bf16[32,1408]{1,0:T(8,128)(2,1)} %copy-done.8, bf16[32,1408]{1,0:T(8,128)(2,1)} %copy-done.9, bf16[32,1408]{1,0:T(8,128)(2,1)} %copy-done.10, bf16[32,4224]{1,0:T(8,128)(2,1)} %copy-done.4, ...), custom_call_target="tpu_custom_call" | custom-call | tf_op jit(solution)/shard_map/pallas_call | solution.py:547
  112.4 1.5 %shard_map.106 = (f32[256,1024]{1,0:T(8,128)}, f32[256,1024]{1,0:T(8,128)}) custom-call(f32[256,1024]{1,0:T(8,128)S(1)} %get-tuple-element.142.value_near, f32[256,1024]{1,0:T(8,128)S(1)} %get-tuple-element.143.out_near, bf16[256,1024]{1,0:T(8,128)(2,1)S(1)} %collective-permute-done.26.value_far, bf16[256,1024]{1,0:T(8,128)(2,1)S(1)} %collective-permute-done.27.out_far), custom_call_target="tpu_custom_call" | custom-call | tf_op jit(solution)/shard_map/pallas_call | solution.py:586
  (88 shorter events, 21.3 us)
Async XLA Ops:
  0.6 4.9 %collective-permute-start = (bf16[1024,1024]{1,0:T(8,128)(2,1)}, bf16[1024,1024]{1,0:T(8,128)(2,1)}, u32[]{:S(2)}, u32[]{:S(2)}) collective-permute-start(bf16[1024,1024]{1,0:T(8,128)(2,1)} %bitcast.36), channel_id=1, source_target_pairs={{0,16},{16,0},{1,17},{17,1},{2,18},{18,2},{3,19},{19,3},{4,20},{20... | collective-permute-start | bytes 6291464 | tf_op jit(solution)/shard_map/ppermute | solution.py:18
  8.3 22.4 %collective-permute-start.6 = (bf16[1024,1024]{1,0:T(8,128)(2,1)}, bf16[1024,1024]{1,0:T(8,128)(2,1)}, u32[]{:S(2)}, u32[]{:S(2)}) collective-permute-start(bf16[1024,1024]{1,0:T(8,128)(2,1)} %bitcast.10.refs_5_.refs_6_), channel_id=1, source_target_pairs={{0,16},{16,0},{1,17},{17,1},{2,18},{18,2},{3,19},{19,3},{4,20},{20... | collective-permute-start | bytes 6291464 | tf_op jit(solution)/shard_map/ppermute | solution.py:18
  8.7 26.3 %collective-permute-start.9 = (bf16[1024,1024]{1,0:T(8,128)(2,1)}, bf16[1024,1024]{1,0:T(8,128)(2,1)}, u32[]{:S(2)}, u32[]{:S(2)}) collective-permute-start(bf16[1024,1024]{1,0:T(8,128)(2,1)} %bitcast.11.value_a), channel_id=1, source_target_pairs={{0,16},{16,0},{1,17},{17,1},{2,18},{18,2},{3,19},{19,3},{4,20},{20... | collective-permute-start | bytes 6291464 | tf_op jit(solution)/shard_map/ppermute | solution.py:18
  8.8 26.1 %collective-permute-start.10 = (bf16[1024,1024]{1,0:T(8,128)(2,1)}, bf16[1024,1024]{1,0:T(8,128)(2,1)}, u32[]{:S(2)}, u32[]{:S(2)}) collective-permute-start(bf16[1024,1024]{1,0:T(8,128)(2,1)} %bitcast.7.lout_a.refs_10_), channel_id=1, source_target_pairs={{0,16},{16,0},{1,17},{17,1},{2,18},{18,2},{3,19},{19,3},{4,20},{20... | collective-permute-start | bytes 6291464 | tf_op jit(solution)/shard_map/ppermute | solution.py:18
  10.4 37.4 %all-to-all-start = ((bf16[4,128,1152]{2,1,0:T(8,128)(2,1)}), bf16[4,128,1152]{2,1,0:T(8,128)(2,1)S(1)}, u32[]{:S(2)}, u32[]{:S(2)}) async-start(bf16[4,128,1152]{2,1,0:T(8,128)(2,1)} %bitcast.39), calls=%async_computation | async-start | bytes 2359296 | tf_op jit(solution)/shard_map/all_to_all | solution.py:408
  15.2 7.7 %collective-permute-start.2 = (bf16[64,2176]{1,0:T(8,128)(2,1)}, bf16[64,2176]{1,0:T(8,128)(2,1)S(1)}, u32[]{:S(2)}, u32[]{:S(2)}) collective-permute-start(bf16[64,2176]{1,0:T(8,128)(2,1)} %copy-done.3), channel_id=1, source_target_pairs={{0,1},{1,0},{2,3},{3,2},{4,5},{5,4},{6,7},{7,6},{8,9},{9,8},{10,11... | collective-permute-start | bytes 835592 | tf_op jit(solution)/shard_map/ppermute | solution.py:18
  15.4 7.4 %collective-permute-start.3 = (bf16[64,2176]{1,0:T(8,128)(2,1)S(1)}, bf16[64,2176]{1,0:T(8,128)(2,1)S(1)}, u32[]{:S(2)}, u32[]{:S(2)}) collective-permute-start(bf16[64,2176]{1,0:T(8,128)(2,1)S(1)} %get-tuple-element.82), channel_id=1, source_target_pairs={{0,2},{1,3},{2,0},{3,1},{4,6},{5,7},{6,4},{7,5},{8,10},{9,11},{10,... | collective-permute-start | bytes 835592 | tf_op jit(solution)/shard_map/ppermute | solution.py:18
  23.1 6.6 %collective-permute-start.4 = (bf16[64,2176]{1,0:T(8,128)(2,1)S(1)}, bf16[64,2176]{1,0:T(8,128)(2,1)S(1)}, u32[]{:S(2)}, u32[]{:S(2)}) collective-permute-start(bf16[64,2176]{1,0:T(8,128)(2,1)S(1)} %get-tuple-element.90), channel_id=1, source_target_pairs={{0,2},{1,3},{2,0},{3,1},{4,6},{5,7},{6,4},{7,5},{8,10},{9,11},{10,... | collective-permute-start | bytes 835592 | tf_op jit(solution)/shard_map/ppermute | solution.py:18
  24.4 6.2 %collective-permute-start.5 = (bf16[64,2176]{1,0:T(8,128)(2,1)S(1)}, bf16[64,2176]{1,0:T(8,128)(2,1)S(1)}, u32[]{:S(2)}, u32[]{:S(2)}) collective-permute-start(bf16[64,2176]{1,0:T(8,128)(2,1)S(1)} %get-tuple-element.91), channel_id=1, source_target_pairs={{0,1},{1,0},{2,3},{3,2},{4,5},{5,4},{6,7},{7,6},{8,9},{9,8},{10,11... | collective-permute-start | bytes 835592 | tf_op jit(solution)/shard_map/ppermute | solution.py:18
  38.9 5.2 %collective-permute-start.11 = (bf16[64,1152]{1,0:T(8,128)(2,1)S(1)}, bf16[64,1152]{1,0:T(8,128)(2,1)S(1)}, u32[]{:S(2)}, u32[]{:S(2)}) collective-permute-start(bf16[64,1152]{1,0:T(8,128)(2,1)S(1)} %get-tuple-element.112), channel_id=1, source_target_pairs={{0,2},{1,3},{2,0},{3,1},{4,6},{5,7},{6,4},{7,5},{8,10},{9,11},{10,... | collective-permute-start | bytes 442376 | tf_op jit(solution)/shard_map/ppermute | solution.py:18
  47.8 46.6 %all-to-all-start.1 = ((bf16[4,128,1024]{2,1,0:T(8,128)(2,1)}), bf16[4,128,1024]{2,1,0:T(8,128)(2,1)}, u32[]{:S(2)}, u32[]{:S(2)}) async-start(bf16[4,128,1024]{2,1,0:T(8,128)(2,1)} %bitcast.40), calls=%async_computation.1 | async-start | bytes 2097152 | tf_op jit(solution)/shard_map/all_to_all | solution.py:461
  58.6 5.0 %collective-permute-start.15 = (bf16[32,2176]{1,0:T(8,128)(2,1)}, bf16[32,2176]{1,0:T(8,128)(2,1)S(1)}, u32[]{:S(2)}, u32[]{:S(2)}) collective-permute-start(bf16[32,2176]{1,0:T(8,128)(2,1)} %get-tuple-element.125), channel_id=1, source_target_pairs={{0,3},{1,2},{2,1},{3,0},{4,7},{5,6},{6,5},{7,4},{8,11},{9,10},{10,... | collective-permute-start | bytes 417800 | tf_op jit(solution)/shard_map/ppermute | solution.py:18
  63.9 4.9 %collective-permute-start.16 = (bf16[32,1408]{1,0:T(8,128)(2,1)S(1)}, bf16[32,1408]{1,0:T(8,128)(2,1)S(1)}, u32[]{:S(2)}, u32[]{:S(2)}) collective-permute-start(bf16[32,1408]{1,0:T(8,128)(2,1)S(1)} %get-tuple-element.129), channel_id=1, source_target_pairs={{0,4},{4,0},{8,12},{12,8},{1,5},{5,1},{9,13},{13,9},{2,6},{6,2},{1... | collective-permute-start | bytes 270344 | tf_op jit(solution)/shard_map/ppermute | solution.py:18
  64.6 13.3 %collective-permute-start.17 = (bf16[32,1408]{1,0:T(8,128)(2,1)S(1)}, bf16[32,1408]{1,0:T(8,128)(2,1)S(1)}, u32[]{:S(2)}, u32[]{:S(2)}) collective-permute-start(bf16[32,1408]{1,0:T(8,128)(2,1)S(1)} %get-tuple-element.130), channel_id=1, source_target_pairs={{0,8},{4,12},{8,0},{12,4},{1,9},{5,13},{9,1},{13,5},{2,10},{6,14},... | collective-permute-start | bytes 270344 | tf_op jit(solution)/shard_map/ppermute | solution.py:18
  66.3 15.7 %collective-permute-start.18 = (bf16[32,1408]{1,0:T(8,128)(2,1)S(1)}, bf16[32,1408]{1,0:T(8,128)(2,1)S(1)}, u32[]{:S(2)}, u32[]{:S(2)}) collective-permute-start(bf16[32,1408]{1,0:T(8,128)(2,1)S(1)} %get-tuple-element.131), channel_id=1, source_target_pairs={{0,12},{4,8},{8,4},{12,0},{1,13},{5,9},{9,5},{13,1},{2,14},{6,10},... | collective-permute-start | bytes 270344 | tf_op jit(solution)/shard_map/ppermute | solution.py:18
  66.6 15.5 %collective-permute-start.19 = (bf16[32,1408]{1,0:T(8,128)(2,1)S(1)}, bf16[32,1408]{1,0:T(8,128)(2,1)S(1)}, u32[]{:S(2)}, u32[]{:S(2)}) collective-permute-start(bf16[32,1408]{1,0:T(8,128)(2,1)S(1)} %get-tuple-element.136.refs_0_), channel_id=1, source_target_pairs={{0,1},{1,0},{2,3},{3,2},{4,5},{5,4},{6,7},{7,6},{8,9},{9,8},{10,11... | collective-permute-start | bytes 270344 | tf_op jit(solution)/shard_map/ppermute | solution.py:18
  67.4 14.7 %collective-permute-start.20 = (bf16[32,1408]{1,0:T(8,128)(2,1)S(1)}, bf16[32,1408]{1,0:T(8,128)(2,1)S(1)}, u32[]{:S(2)}, u32[]{:S(2)}) collective-permute-start(bf16[32,1408]{1,0:T(8,128)(2,1)S(1)} %get-tuple-element.136.refs_0_), channel_id=1, source_target_pairs={{0,2},{1,3},{2,0},{3,1},{4,6},{5,7},{6,4},{7,5},{8,10},{9,11},{10,... | collective-permute-start | bytes 270344 | tf_op jit(solution)/shard_map/ppermute | solution.py:18
  68.8 17.3 %collective-permute-start.25 = (bf16[512,256]{1,0:T(8,128)(2,1)S(1)}, bf16[512,256]{1,0:T(8,128)(2,1)S(1)}, u32[]{:S(2)}, u32[]{:S(2)}) collective-permute-start(bf16[512,256]{1,0:T(8,128)(2,1)S(1)} %get-tuple-element.141), channel_id=1, source_target_pairs={{0,16},{16,0},{1,17},{17,1},{2,18},{18,2},{3,19},{19,3},{4,20},{20... | collective-permute-start | bytes 786440 | tf_op jit(solution)/shard_map/ppermute | solution.py:18
  82.2 11.7 %collective-permute-start.22 = (bf16[32,4224]{1,0:T(8,128)(2,1)S(1)}, bf16[32,4224]{1,0:T(8,128)(2,1)S(1)}, u32[]{:S(2)}, u32[]{:S(2)}) collective-permute-start(bf16[32,4224]{1,0:T(8,128)(2,1)S(1)} %constant_dynamic-update-slice_fusion.refs_4_), channel_id=1, source_target_pairs={{0,1},{1,0},{2,3},{3,2},{4,5},{5,4},{6,7},{7,6},{8,9},{9,8},{10,11... | collective-permute-start | bytes 811016 | tf_op jit(solution)/shard_map/ppermute | solution.py:18
  83.6 10.8 %collective-permute-start.23 = (bf16[32,4224]{1,0:T(8,128)(2,1)S(1)}, bf16[32,4224]{1,0:T(8,128)(2,1)S(1)}, u32[]{:S(2)}, u32[]{:S(2)}) collective-permute-start(bf16[32,4224]{1,0:T(8,128)(2,1)S(1)} %constant_dynamic-update-slice_fusion.refs_4_), channel_id=1, source_target_pairs={{0,2},{1,3},{2,0},{3,1},{4,6},{5,7},{6,4},{7,5},{8,10},{9,11},{10,... | collective-permute-start | bytes 811016 | tf_op jit(solution)/shard_map/ppermute | solution.py:18
  83.6 10.8 %collective-permute-start.24 = (bf16[32,4224]{1,0:T(8,128)(2,1)S(1)}, bf16[32,4224]{1,0:T(8,128)(2,1)S(1)}, u32[]{:S(2)}, u32[]{:S(2)}) collective-permute-start(bf16[32,4224]{1,0:T(8,128)(2,1)S(1)} %constant_dynamic-update-slice_fusion.refs_4_), channel_id=1, source_target_pairs={{0,3},{1,2},{2,1},{3,0},{4,7},{5,6},{6,5},{7,4},{8,11},{9,10},{10,... | collective-permute-start | bytes 811016 | tf_op jit(solution)/shard_map/ppermute | solution.py:18
  85.0 8.9 %collective-permute-start.21 = (bf16[32,1408]{1,0:T(8,128)(2,1)S(1)}, bf16[32,1408]{1,0:T(8,128)(2,1)S(1)}, u32[]{:S(2)}, u32[]{:S(2)}) collective-permute-start(bf16[32,1408]{1,0:T(8,128)(2,1)S(1)} %get-tuple-element.136.refs_0_), channel_id=1, source_target_pairs={{0,3},{1,2},{2,1},{3,0},{4,7},{5,6},{6,5},{7,4},{8,11},{9,10},{10,... | collective-permute-start | bytes 270344 | tf_op jit(solution)/shard_map/ppermute | solution.py:18
  100.8 11.6 %collective-permute-start.26 = (bf16[256,1024]{1,0:T(8,128)(2,1)S(1)}, bf16[256,1024]{1,0:T(8,128)(2,1)S(1)}, u32[]{:S(2)}, u32[]{:S(2)}) collective-permute-start(bf16[256,1024]{1,0:T(8,128)(2,1)S(1)} %get-tuple-element.144), channel_id=1, source_target_pairs={{0,16},{16,0},{1,17},{17,1},{2,18},{18,2},{3,19},{19,3},{4,20},{20... | collective-permute-start | bytes 1572872 | tf_op jit(solution)/shard_map/ppermute | solution.py:18
  106.7 5.7 %collective-permute-start.27 = (bf16[256,1024]{1,0:T(8,128)(2,1)S(1)}, bf16[256,1024]{1,0:T(8,128)(2,1)S(1)}, u32[]{:S(2)}, u32[]{:S(2)}) collective-permute-start(bf16[256,1024]{1,0:T(8,128)(2,1)S(1)} %get-tuple-element.145), channel_id=1, source_target_pairs={{0,16},{16,0},{1,17},{17,1},{2,18},{18,2},{3,19},{19,3},{4,20},{20... | collective-permute-start | bytes 1572872 | tf_op jit(solution)/shard_map/ppermute | solution.py:18
  (19 other events, 115.8 us)

commit v5 on v4

--- a/solution.py
+++ b/solution.py
@@ -276,8 +276,6 @@
     def begin(source, target):
         copies.append(start_copy(source, target, sems.at[len(copies)]))
 
-    begin(lout_in, lout)
-    begin(gram_in, gram)
     ready = []
     for number, (away, (group, place)) in enumerate(zip(aways, spots)):
         start = number * keep
@@ -291,20 +289,30 @@
             source = sources[group * peers + mask].at[:, pl.ds(place * piece, piece)]
             begin(source, tokens.at[pl.ds(at, share), :])
         ready.append(len(copies))
-    done = 0
-    for number, until in enumerate(ready):
-        for copy in copies[done:until]:
-            copy.wait()
+        if number == min(1, len(aways) - 1):
+            maps = len(copies)
+            begin(gram_in, gram)
+            begin(lout_in, lout)
+    done, step = 0, 2 if len(aways) % 2 == 0 else 1
+    for number in range(0, len(aways), step):
+        until = ready[number + step - 1]
+        for index in range(done, until):
+            if index not in (maps, maps + 1):
+                copies[index].wait()
         done = until
-        here = pl.ds(keep * number, keep)
+        here = pl.ds(keep * number, keep * step)
         wide = x[here, :].astype(F32)
-        values = tokens[here, :inner]
         side = tokens[here, inner + block :]
         portion = 1.0 / from_side(side, 1)
+        normed[here, :] = (wide * from_side(side)).astype(BF)
+        values = tokens[here, :inner]
+        crossed = tokens[here, inner : inner + block].astype(F32)
+        if number == 0:
+            copies[maps].wait()
+        back[here, :] = ((crossed + matmul(values, gram[...])) * portion).astype(BF)
+        if number == 0:
+            copies[maps + 1].wait()
         slopes[here, :] = ((wide + matmul(values, lout[...])) * portion).astype(BF)
-        normed[here, :] = (wide * from_side(side)).astype(BF)
-        crossed = tokens[here, inner : inner + block].astype(F32)
-        back[here, :] = ((crossed + matmul(values, gram[...])) * portion).astype(BF)
     column = pl.ds(pl.multiple_of(dp_at * block, block), block)
     grad_value[...] = matmul_tn(back[...], normed[...]).astype(grad_value.dtype)
     grad_out[...] = matmul_tn(tokens[:, column], slopes[...]).astype(grad_out.dtype)
@@ -367,7 +375,6 @@
             [VMEM],
             [pltpu.SemaphoreType.DMA((dp_size,))],
             out_specs=[HBM],
-
         )(array)[0]
 
     gram = matmul_nt(own_lout, lax.dynamic_slice_in_dim(own_lout, dp_at * block, block, 0))

time: 114 us -> 114 us (level)
  transfers between devices with their start and end apart: 30 -> 30, of which waited for: 13 -> 13; matrix products, arithmetic and copies ran while one was open for 4% -> 4% of each run, Pallas kernels for 20% -> 19%
where the time goes in v5:
time: 114 us; the launch traced here: 113 us
  starting transfers between devices  44.1 us (39%)
  Pallas kernels  31.4 us (28%)
  waiting for transfers between devices  31.1 us (27%)
  matrix products  2.79 us (2%)
  between operations  1.6 us (1%)
  other arithmetic  1.21 us (1%)
    ppermute x28, starting transfers between devices, flip(): return lax.ppermute(value, axis, pairs)  34.4 us
    ppermute x28, waiting for transfers between devices, flip(): return lax.ppermute(value, axis, pairs)  31.1 us
    pallas_call x2, Pallas kernels, gradients(): call(functools.partial(gradient_kernel, share, mp_size, aways, spots, oth...  10.5 us
    all_to_all x1, starting transfers between devices, on_device(): every_scored = lax.all_to_all(repeated, 'dp', 0, 0, tiled=True)  4.86 us
    all_to_all x1, starting transfers between devices, on_device(): every_row = lax.all_to_all(repeat(rows_wide), 'dp', 0, 0, tiled=True)  4.77 us
    pallas_call x1, Pallas kernels, on_device(): call(functools.partial(share_kernel, share), [jax.ShapeDtypeStruct((share...  4.41 us
    pallas_call x1, Pallas kernels, on_device(): call(functools.partial(score_kernel, scorer_width), [hidden_type, sums[1]...  3.7 us
    pallas_call x1, Pallas kernels, on_device(): call(learn_kernel, [jax.ShapeDtypeStruct((keep, 2 * inner), F32)], [SMEM,...  3.61 us
  transfers between devices with their start and end apart: 30, of which 13 were waited for; matrix products, arithmetic and copies ran while one was open for 4% of the time, Pallas kernels for 19%

profile of v5, /device:TPU:11, one launch (start us, length us, event | category | flops | bytes accessed | tf_op | source)
XLA Modules:
  0.0 113.2 jit_solution(12872835707662029391)
XLA Ops:
  1.4 2.5 %fusion = f32[256,1024]{0,1:T(8,128)S(1)} fusion(bf16[1,1024,1024]{2,1,0:T(8,128)(2,1)} %param.12, s32[]{:T(128)S(6)} %select_n.25), kind=kOutput, calls=%fused_computation.2 | convolution fusion | flops 536870912 | bytes 3670020 | tf_op jit(solution)/shard_map/dot_general | solution.py:26
  5.6 2.7 %shard_map.95 = (f32[128,1024]{1,0:T(8,128)S(1)}, f32[128,1]{1,0:T(8,128)S(1)}, bf16[64,2176]{1,0:T(8,128)(2,1)S(1)}, bf16[64,2176]{1,0:T(8,128)(2,1)S(1)}, f32[512,256]{1,0:T(8,128)S(1)}) custom-call(s32[3]{0:T(128)S(1)} %pad_add_fusion.1.where, bf16[128,1024]{1,0:T(8,128)(2,1)S(1)} %convolution_convert_fusion.rows.refs_4_, bf16[1024,1024]{1,0:T(8,128)(2,1)} %bitcast.37, ...), custom_call_target="tpu_custom_call" | custom-call | tf_op jit(solution)/shard_map/pallas_call | solution.py:407
  10.4 4.8 %all-to-all-start = ((bf16[4,128,1152]{2,1,0:T(8,128)(2,1)}), bf16[4,128,1152]{2,1,0:T(8,128)(2,1)S(1)}, u32[]{:S(2)}, u32[]{:S(2)}) async-start(bf16[4,128,1152]{2,1,0:T(8,128)(2,1)} %bitcast.39), calls=%async_computation | async-start | bytes 2359296 | tf_op jit(solution)/shard_map/all_to_all | solution.py:415
  15.4 1.2 %collective-permute-start.3 = (bf16[64,2176]{1,0:T(8,128)(2,1)S(1)}, bf16[64,2176]{1,0:T(8,128)(2,1)S(1)}, u32[]{:S(2)}, u32[]{:S(2)}) collective-permute-start(bf16[64,2176]{1,0:T(8,128)(2,1)S(1)} %get-tuple-element.82), channel_id=1, source_target_pairs={{0,2},{1,3},{2,0},{3,1},{4,6},{5,7},{6,4},{7,5},{8,10},{9,11},{10,... | collective-permute-start | bytes 835592 | tf_op jit(solution)/shard_map/ppermute | solution.py:18
  16.6 6.2 %collective-permute-done.2.got_top = bf16[64,2176]{1,0:T(8,128)(2,1)S(1)} collective-permute-done((bf16[64,2176]{1,0:T(8,128)(2,1)}, bf16[64,2176]{1,0:T(8,128)(2,1)S(1)}, u32[]{:S(2)}, u32[]{:S(2)}) %collective-permute-start.2) | collective-permute-done | bytes 278560 | tf_op jit(solution)/shard_map/ppermute | solution.py:18
  23.1 1.3 %collective-permute-start.4 = (bf16[64,2176]{1,0:T(8,128)(2,1)S(1)}, bf16[64,2176]{1,0:T(8,128)(2,1)S(1)}, u32[]{:S(2)}, u32[]{:S(2)}) collective-permute-start(bf16[64,2176]{1,0:T(8,128)(2,1)S(1)} %get-tuple-element.90), channel_id=1, source_target_pairs={{0,2},{1,3},{2,0},{3,1},{4,6},{5,7},{6,4},{7,5},{8,10},{9,11},{10,... | collective-permute-start | bytes 835592 | tf_op jit(solution)/shard_map/ppermute | solution.py:18
  25.4 4.3 %collective-permute-done.4.refs_2_ = bf16[64,2176]{1,0:T(8,128)(2,1)S(1)} collective-permute-done((bf16[64,2176]{1,0:T(8,128)(2,1)S(1)}, bf16[64,2176]{1,0:T(8,128)(2,1)S(1)}, u32[]{:S(2)}, u32[]{:S(2)}) %collective-permute-start.4) | collective-permute-done | bytes 278560 | tf_op jit(solution)/shard_map/ppermute | solution.py:18
  30.7 3.3 %shard_map.97 = (bf16[128,1024]{1,0:T(8,128)(2,1)S(1)}, f32[128,1024]{1,0:T(8,128)S(1)}, f32[128,1]{1,0:T(8,128)S(1)}, bf16[64,1152]{1,0:T(8,128)(2,1)S(1)}, bf1...) custom-call(s32[3]{0:T(128)S(1)} %pad_add_fusion.1.where, f32[128,1024]{1,0:T(8,128)S(1)} %get-tuple-element.86.refs_0_, ...), custom_call_target="tpu_custom_call" | custom-call | tf_op jit(solution)/shard_map/pallas_call | solution.py:428
  35.0 3.6 %shard_map.99.given = f32[128,2048]{1,0:T(8,128)S(1)} custom-call(s32[3]{0:T(128)S(1)} %pad_add_fusion.1.where, bf16[128,1024]{1,0:T(8,128)(2,1)S(1)} %convolution_convert_fusion.rows.refs_4_, bf16[1024,1024]{1,0:T(8,128)(2,1)} %bitcast.11.value_a, bf16[1024,1024]{1,0:T(8,128)(2,1)} %collective-permute-done.9.value_b, ...), custom_call_target="tpu_custom_call" | custom-call | tf_op jit(solution)/shard_map/pallas_call | solution.py:438
  40.9 3.2 %collective-permute-done.11.refs_2_ = bf16[64,1152]{1,0:T(8,128)(2,1)S(1)} collective-permute-done((bf16[64,1152]{1,0:T(8,128)(2,1)S(1)}, bf16[64,1152]{1,0:T(8,128)(2,1)S(1)}, u32[]{:S(2)}, u32[]{:S(2)}) %collective-permute-start.11) | collective-permute-done | bytes 147488 | tf_op jit(solution)/shard_map/ppermute | solution.py:18
  44.1 3.7 %shard_map.100 = (bf16[128,1024]{1,0:T(8,128)(2,1)S(1)}, f32[128,1]{1,0:T(8,128)S(1)}, bf16[512,1024]{1,0:T(8,128)(2,1)}) custom-call(s32[3]{0:T(128)S(1)} %pad_add_fusion.1.where, f32[128,1024]{1,0:T(8,128)S(1)} %get-tuple-element.104.refs_0_, f32[128,1]{1,0:T(8,128)S(1)} %get-tuple-element.105.refs_1_, ...), custom_call_target="tpu_custom_call" | custom-call | tf_op jit(solution)/shard_map/pallas_call | solution.py:452
  47.8 4.9 %all-to-all-start.1 = ((bf16[4,128,1024]{2,1,0:T(8,128)(2,1)}), bf16[4,128,1024]{2,1,0:T(8,128)(2,1)}, u32[]{:S(2)}, u32[]{:S(2)}) async-start(bf16[4,128,1024]{2,1,0:T(8,128)(2,1)} %bitcast.40), calls=%async_computation.1 | async-start | bytes 2097152 | tf_op jit(solution)/shard_map/all_to_all | solution.py:468
  52.7 4.4 %shard_map.102 = (f32[32,2048]{1,0:T(8,128)S(1)}, f32[32,1]{1,0:T(8,128)S(1)}, f32[32,1]{1,0:T(8,128)S(1)}, bf16[32,2176]{1,0:T(8,128)(2,1)}, bf16[32,2176]{1,0:T(8,128)(2,1)}, /*index=5*/bf16[32,2176]{1,0:T(8,128)(2,1)}) custom-call(s32[3]{0:T(128)S(1)} %pad_add_fusion.1.where, bf16[128,1024]{1,0:T(8,128)(2,1)S(1)} %get-tuple-element.117.scored, ...), custom_call_target="tpu_custom_call" | custom-call | tf_op jit(solution)/shard_map/pallas_call | solution.py:469
  59.8 1.9 %collective-permute-done.13.refs_0_ = bf16[32,2176]{1,0:T(8,128)(2,1)S(1)} collective-permute-done((bf16[32,2176]{1,0:T(8,128)(2,1)}, bf16[32,2176]{1,0:T(8,128)(2,1)S(1)}, u32[]{:S(2)}, u32[]{:S(2)}) %collective-permute-start.13) | collective-permute-done | bytes 139296 | tf_op jit(solution)/shard_map/ppermute | solution.py:18
  64.6 1.7 %collective-permute-start.17 = (bf16[32,1408]{1,0:T(8,128)(2,1)S(1)}, bf16[32,1408]{1,0:T(8,128)(2,1)S(1)}, u32[]{:S(2)}, u32[]{:S(2)}) collective-permute-start(bf16[32,1408]{1,0:T(8,128)(2,1)S(1)} %get-tuple-element.130), channel_id=1, source_target_pairs={{0,8},{4,12},{8,0},{12,4},{1,9},{5,13},{9,1},{13,5},{2,10},{6,14},... | collective-permute-start | bytes 270344 | tf_op jit(solution)/shard_map/ppermute | solution.py:18
  68.8 9.1 %collective-permute-start.25 = (bf16[512,256]{1,0:T(8,128)(2,1)S(1)}, bf16[512,256]{1,0:T(8,128)(2,1)S(1)}, u32[]{:S(2)}, u32[]{:S(2)}) collective-permute-start(bf16[512,256]{1,0:T(8,128)(2,1)S(1)} %get-tuple-element.141), channel_id=1, source_target_pairs={{0,16},{16,0},{1,17},{17,1},{2,18},{18,2},{3,19},{19,3},{4,20},{20... | collective-permute-start | bytes 786440 | tf_op jit(solution)/shard_map/ppermute | solution.py:18
  77.9 4.2 %collective-permute-done.18 = bf16[32,1408]{1,0:T(8,128)(2,1)S(1)} collective-permute-done((bf16[32,1408]{1,0:T(8,128)(2,1)S(1)}, bf16[32,1408]{1,0:T(8,128)(2,1)S(1)}, u32[]{:S(2)}, u32[]{:S(2)}) %collective-permute-start.18) | collective-permute-done | bytes 90144 | tf_op jit(solution)/shard_map/ppermute | solution.py:18
  82.2 1.5 %collective-permute-start.22 = (bf16[32,4224]{1,0:T(8,128)(2,1)S(1)}, bf16[32,4224]{1,0:T(8,128)(2,1)S(1)}, u32[]{:S(2)}, u32[]{:S(2)}) collective-permute-start(bf16[32,4224]{1,0:T(8,128)(2,1)S(1)} %constant_dynamic-update-slice_fusion.refs_4_), channel_id=1, source_target_pairs={{0,1},{1,0},{2,3},{3,2},{4,5},{5,4},{6,7},{7,6},{8,9},{9,8},{10,11... | collective-permute-start | bytes 811016 | tf_op jit(solution)/shard_map/ppermute | solution.py:18
  83.6 1.3 %collective-permute-start.24 = (bf16[32,4224]{1,0:T(8,128)(2,1)S(1)}, bf16[32,4224]{1,0:T(8,128)(2,1)S(1)}, u32[]{:S(2)}, u32[]{:S(2)}) collective-permute-start(bf16[32,4224]{1,0:T(8,128)(2,1)S(1)} %constant_dynamic-update-slice_fusion.refs_4_), channel_id=1, source_target_pairs={{0,3},{1,2},{2,1},{3,0},{4,7},{5,6},{6,5},{7,4},{8,11},{9,10},{10,... | collective-permute-start | bytes 811016 | tf_op jit(solution)/shard_map/ppermute | solution.py:18
  87.1 6.8 %collective-permute-done.21.refs_3_ = bf16[32,1408]{1,0:T(8,128)(2,1)S(1)} collective-permute-done((bf16[32,1408]{1,0:T(8,128)(2,1)S(1)}, bf16[32,1408]{1,0:T(8,128)(2,1)S(1)}, u32[]{:S(2)}, u32[]{:S(2)}) %collective-permute-start.21) | collective-permute-done | bytes 90144 | tf_op jit(solution)/shard_map/ppermute | solution.py:18
  95.2 5.2 %shard_map.105 = (bf16[256,1024]{1,0:T(8,128)(2,1)S(1)}, bf16[256,1024]{1,0:T(8,128)(2,1)S(1)}) custom-call(s32[3]{0:T(128)S(1)} %pad_add_fusion.where, bf16[32,1408]{1,0:T(8,128)(2,1)} %copy-done.2, bf16[32,1408]{1,0:T(8,128)(2,1)} %copy-done.8, bf16[32,1408]{1,0:T(8,128)(2,1)} %copy-done.9, bf16[32,1408]{1,0:T(8,128)(2,1)} %copy-done.10, ...), custom_call_target="tpu_custom_call" | custom-call | tf_op jit(solution)/shard_map/pallas_call | solution.py:554
  100.5 5.9 %collective-permute-start.26 = (bf16[256,1024]{1,0:T(8,128)(2,1)S(1)}, bf16[256,1024]{1,0:T(8,128)(2,1)S(1)}, u32[]{:S(2)}, u32[]{:S(2)}) collective-permute-start(bf16[256,1024]{1,0:T(8,128)(2,1)S(1)} %get-tuple-element.144), channel_id=1, source_target_pairs={{0,16},{16,0},{1,17},{17,1},{2,18},{18,2},{3,19},{19,3},{4,20},{20... | collective-permute-start | bytes 1572872 | tf_op jit(solution)/shard_map/ppermute | solution.py:18
  106.5 5.2 %shard_map.104 = (f32[256,1024]{1,0:T(8,128)S(1)}, f32[256,1024]{1,0:T(8,128)S(1)}) custom-call(s32[3]{0:T(128)S(1)} %pad_add_fusion.where, bf16[32,1408]{1,0:T(8,128)(2,1)} %copy-done.2, bf16[32,1408]{1,0:T(8,128)(2,1)} %copy-done.8, bf16[32,1408]{1,0:T(8,128)(2,1)} %copy-done.9, bf16[32,1408]{1,0:T(8,128)(2,1)} %copy-done.10, bf16[32,4224]{1,0:T(8,128)(2,1)} %copy-done.4, ...), custom_call_target="tpu_custom_call" | custom-call | tf_op jit(solution)/shard_map/pallas_call | solution.py:554
  111.7 1.5 %shard_map.106 = (f32[256,1024]{1,0:T(8,128)}, f32[256,1024]{1,0:T(8,128)}) custom-call(f32[256,1024]{1,0:T(8,128)S(1)} %get-tuple-element.142.value_near, f32[256,1024]{1,0:T(8,128)S(1)} %get-tuple-element.143.out_near, bf16[256,1024]{1,0:T(8,128)(2,1)S(1)} %collective-permute-done.26.value_far, bf16[256,1024]{1,0:T(8,128)(2,1)S(1)} %collective-permute-done.27.out_far), custom_call_target="tpu_custom_call" | custom-call | tf_op jit(solution)/shard_map/pallas_call | solution.py:593
  (88 shorter events, 21.3 us)
Async XLA Ops:
  0.6 4.9 %collective-permute-start = (bf16[1024,1024]{1,0:T(8,128)(2,1)}, bf16[1024,1024]{1,0:T(8,128)(2,1)}, u32[]{:S(2)}, u32[]{:S(2)}) collective-permute-start(bf16[1024,1024]{1,0:T(8,128)(2,1)} %bitcast.36), channel_id=1, source_target_pairs={{0,16},{16,0},{1,17},{17,1},{2,18},{18,2},{3,19},{19,3},{4,20},{20... | collective-permute-start | bytes 6291464 | tf_op jit(solution)/shard_map/ppermute | solution.py:18
  8.3 22.4 %collective-permute-start.6 = (bf16[1024,1024]{1,0:T(8,128)(2,1)}, bf16[1024,1024]{1,0:T(8,128)(2,1)}, u32[]{:S(2)}, u32[]{:S(2)}) collective-permute-start(bf16[1024,1024]{1,0:T(8,128)(2,1)} %bitcast.10.refs_5_.refs_6_), channel_id=1, source_target_pairs={{0,16},{16,0},{1,17},{17,1},{2,18},{18,2},{3,19},{19,3},{4,20},{20... | collective-permute-start | bytes 6291464 | tf_op jit(solution)/shard_map/ppermute | solution.py:18
  8.7 26.3 %collective-permute-start.9 = (bf16[1024,1024]{1,0:T(8,128)(2,1)}, bf16[1024,1024]{1,0:T(8,128)(2,1)}, u32[]{:S(2)}, u32[]{:S(2)}) collective-permute-start(bf16[1024,1024]{1,0:T(8,128)(2,1)} %bitcast.11.value_a), channel_id=1, source_target_pairs={{0,16},{16,0},{1,17},{17,1},{2,18},{18,2},{3,19},{19,3},{4,20},{20... | collective-permute-start | bytes 6291464 | tf_op jit(solution)/shard_map/ppermute | solution.py:18
  8.8 26.1 %collective-permute-start.10 = (bf16[1024,1024]{1,0:T(8,128)(2,1)}, bf16[1024,1024]{1,0:T(8,128)(2,1)}, u32[]{:S(2)}, u32[]{:S(2)}) collective-permute-start(bf16[1024,1024]{1,0:T(8,128)(2,1)} %bitcast.7.lout_a.refs_10_), channel_id=1, source_target_pairs={{0,16},{16,0},{1,17},{17,1},{2,18},{18,2},{3,19},{19,3},{4,20},{20... | collective-permute-start | bytes 6291464 | tf_op jit(solution)/shard_map/ppermute | solution.py:18
  10.4 37.4 %all-to-all-start = ((bf16[4,128,1152]{2,1,0:T(8,128)(2,1)}), bf16[4,128,1152]{2,1,0:T(8,128)(2,1)S(1)}, u32[]{:S(2)}, u32[]{:S(2)}) async-start(bf16[4,128,1152]{2,1,0:T(8,128)(2,1)} %bitcast.39), calls=%async_computation | async-start | bytes 2359296 | tf_op jit(solution)/shard_map/all_to_all | solution.py:415
  15.2 7.7 %collective-permute-start.2 = (bf16[64,2176]{1,0:T(8,128)(2,1)}, bf16[64,2176]{1,0:T(8,128)(2,1)S(1)}, u32[]{:S(2)}, u32[]{:S(2)}) collective-permute-start(bf16[64,2176]{1,0:T(8,128)(2,1)} %copy-done.3), channel_id=1, source_target_pairs={{0,1},{1,0},{2,3},{3,2},{4,5},{5,4},{6,7},{7,6},{8,9},{9,8},{10,11... | collective-permute-start | bytes 835592 | tf_op jit(solution)/shard_map/ppermute | solution.py:18
  15.4 7.4 %collective-permute-start.3 = (bf16[64,2176]{1,0:T(8,128)(2,1)S(1)}, bf16[64,2176]{1,0:T(8,128)(2,1)S(1)}, u32[]{:S(2)}, u32[]{:S(2)}) collective-permute-start(bf16[64,2176]{1,0:T(8,128)(2,1)S(1)} %get-tuple-element.82), channel_id=1, source_target_pairs={{0,2},{1,3},{2,0},{3,1},{4,6},{5,7},{6,4},{7,5},{8,10},{9,11},{10,... | collective-permute-start | bytes 835592 | tf_op jit(solution)/shard_map/ppermute | solution.py:18
  23.1 6.6 %collective-permute-start.4 = (bf16[64,2176]{1,0:T(8,128)(2,1)S(1)}, bf16[64,2176]{1,0:T(8,128)(2,1)S(1)}, u32[]{:S(2)}, u32[]{:S(2)}) collective-permute-start(bf16[64,2176]{1,0:T(8,128)(2,1)S(1)} %get-tuple-element.90), channel_id=1, source_target_pairs={{0,2},{1,3},{2,0},{3,1},{4,6},{5,7},{6,4},{7,5},{8,10},{9,11},{10,... | collective-permute-start | bytes 835592 | tf_op jit(solution)/shard_map/ppermute | solution.py:18
  24.4 6.2 %collective-permute-start.5 = (bf16[64,2176]{1,0:T(8,128)(2,1)S(1)}, bf16[64,2176]{1,0:T(8,128)(2,1)S(1)}, u32[]{:S(2)}, u32[]{:S(2)}) collective-permute-start(bf16[64,2176]{1,0:T(8,128)(2,1)S(1)} %get-tuple-element.91), channel_id=1, source_target_pairs={{0,1},{1,0},{2,3},{3,2},{4,5},{5,4},{6,7},{7,6},{8,9},{9,8},{10,11... | collective-permute-start | bytes 835592 | tf_op jit(solution)/shard_map/ppermute | solution.py:18
  38.9 5.2 %collective-permute-start.11 = (bf16[64,1152]{1,0:T(8,128)(2,1)S(1)}, bf16[64,1152]{1,0:T(8,128)(2,1)S(1)}, u32[]{:S(2)}, u32[]{:S(2)}) collective-permute-start(bf16[64,1152]{1,0:T(8,128)(2,1)S(1)} %get-tuple-element.112), channel_id=1, source_target_pairs={{0,2},{1,3},{2,0},{3,1},{4,6},{5,7},{6,4},{7,5},{8,10},{9,11},{10,... | collective-permute-start | bytes 442376 | tf_op jit(solution)/shard_map/ppermute | solution.py:18
  47.8 46.6 %all-to-all-start.1 = ((bf16[4,128,1024]{2,1,0:T(8,128)(2,1)}), bf16[4,128,1024]{2,1,0:T(8,128)(2,1)}, u32[]{:S(2)}, u32[]{:S(2)}) async-start(bf16[4,128,1024]{2,1,0:T(8,128)(2,1)} %bitcast.40), calls=%async_computation.1 | async-start | bytes 2097152 | tf_op jit(solution)/shard_map/all_to_all | solution.py:468
  58.6 5.0 %collective-permute-start.15 = (bf16[32,2176]{1,0:T(8,128)(2,1)}, bf16[32,2176]{1,0:T(8,128)(2,1)S(1)}, u32[]{:S(2)}, u32[]{:S(2)}) collective-permute-start(bf16[32,2176]{1,0:T(8,128)(2,1)} %get-tuple-element.125), channel_id=1, source_target_pairs={{0,3},{1,2},{2,1},{3,0},{4,7},{5,6},{6,5},{7,4},{8,11},{9,10},{10,... | collective-permute-start | bytes 417800 | tf_op jit(solution)/shard_map/ppermute | solution.py:18
  63.9 4.9 %collective-permute-start.16 = (bf16[32,1408]{1,0:T(8,128)(2,1)S(1)}, bf16[32,1408]{1,0:T(8,128)(2,1)S(1)}, u32[]{:S(2)}, u32[]{:S(2)}) collective-permute-start(bf16[32,1408]{1,0:T(8,128)(2,1)S(1)} %get-tuple-element.129), channel_id=1, source_target_pairs={{0,4},{4,0},{8,12},{12,8},{1,5},{5,1},{9,13},{13,9},{2,6},{6,2},{1... | collective-permute-start | bytes 270344 | tf_op jit(solution)/shard_map/ppermute | solution.py:18
  64.6 13.3 %collective-permute-start.17 = (bf16[32,1408]{1,0:T(8,128)(2,1)S(1)}, bf16[32,1408]{1,0:T(8,128)(2,1)S(1)}, u32[]{:S(2)}, u32[]{:S(2)}) collective-permute-start(bf16[32,1408]{1,0:T(8,128)(2,1)S(1)} %get-tuple-element.130), channel_id=1, source_target_pairs={{0,8},{4,12},{8,0},{12,4},{1,9},{5,13},{9,1},{13,5},{2,10},{6,14},... | collective-permute-start | bytes 270344 | tf_op jit(solution)/shard_map/ppermute | solution.py:18
  66.3 15.7 %collective-permute-start.18 = (bf16[32,1408]{1,0:T(8,128)(2,1)S(1)}, bf16[32,1408]{1,0:T(8,128)(2,1)S(1)}, u32[]{:S(2)}, u32[]{:S(2)}) collective-permute-start(bf16[32,1408]{1,0:T(8,128)(2,1)S(1)} %get-tuple-element.131), channel_id=1, source_target_pairs={{0,12},{4,8},{8,4},{12,0},{1,13},{5,9},{9,5},{13,1},{2,14},{6,10},... | collective-permute-start | bytes 270344 | tf_op jit(solution)/shard_map/ppermute | solution.py:18
  66.6 15.5 %collective-permute-start.19 = (bf16[32,1408]{1,0:T(8,128)(2,1)S(1)}, bf16[32,1408]{1,0:T(8,128)(2,1)S(1)}, u32[]{:S(2)}, u32[]{:S(2)}) collective-permute-start(bf16[32,1408]{1,0:T(8,128)(2,1)S(1)} %get-tuple-element.136.refs_0_), channel_id=1, source_target_pairs={{0,1},{1,0},{2,3},{3,2},{4,5},{5,4},{6,7},{7,6},{8,9},{9,8},{10,11... | collective-permute-start | bytes 270344 | tf_op jit(solution)/shard_map/ppermute | solution.py:18
  67.4 14.7 %collective-permute-start.20 = (bf16[32,1408]{1,0:T(8,128)(2,1)S(1)}, bf16[32,1408]{1,0:T(8,128)(2,1)S(1)}, u32[]{:S(2)}, u32[]{:S(2)}) collective-permute-start(bf16[32,1408]{1,0:T(8,128)(2,1)S(1)} %get-tuple-element.136.refs_0_), channel_id=1, source_target_pairs={{0,2},{1,3},{2,0},{3,1},{4,6},{5,7},{6,4},{7,5},{8,10},{9,11},{10,... | collective-permute-start | bytes 270344 | tf_op jit(solution)/shard_map/ppermute | solution.py:18
  68.8 17.3 %collective-permute-start.25 = (bf16[512,256]{1,0:T(8,128)(2,1)S(1)}, bf16[512,256]{1,0:T(8,128)(2,1)S(1)}, u32[]{:S(2)}, u32[]{:S(2)}) collective-permute-start(bf16[512,256]{1,0:T(8,128)(2,1)S(1)} %get-tuple-element.141), channel_id=1, source_target_pairs={{0,16},{16,0},{1,17},{17,1},{2,18},{18,2},{3,19},{19,3},{4,20},{20... | collective-permute-start | bytes 786440 | tf_op jit(solution)/shard_map/ppermute | solution.py:18
  82.2 11.7 %collective-permute-start.22 = (bf16[32,4224]{1,0:T(8,128)(2,1)S(1)}, bf16[32,4224]{1,0:T(8,128)(2,1)S(1)}, u32[]{:S(2)}, u32[]{:S(2)}) collective-permute-start(bf16[32,4224]{1,0:T(8,128)(2,1)S(1)} %constant_dynamic-update-slice_fusion.refs_4_), channel_id=1, source_target_pairs={{0,1},{1,0},{2,3},{3,2},{4,5},{5,4},{6,7},{7,6},{8,9},{9,8},{10,11... | collective-permute-start | bytes 811016 | tf_op jit(solution)/shard_map/ppermute | solution.py:18
  83.6 10.8 %collective-permute-start.23 = (bf16[32,4224]{1,0:T(8,128)(2,1)S(1)}, bf16[32,4224]{1,0:T(8,128)(2,1)S(1)}, u32[]{:S(2)}, u32[]{:S(2)}) collective-permute-start(bf16[32,4224]{1,0:T(8,128)(2,1)S(1)} %constant_dynamic-update-slice_fusion.refs_4_), channel_id=1, source_target_pairs={{0,2},{1,3},{2,0},{3,1},{4,6},{5,7},{6,4},{7,5},{8,10},{9,11},{10,... | collective-permute-start | bytes 811016 | tf_op jit(solution)/shard_map/ppermute | solution.py:18
  83.6 10.8 %collective-permute-start.24 = (bf16[32,4224]{1,0:T(8,128)(2,1)S(1)}, bf16[32,4224]{1,0:T(8,128)(2,1)S(1)}, u32[]{:S(2)}, u32[]{:S(2)}) collective-permute-start(bf16[32,4224]{1,0:T(8,128)(2,1)S(1)} %constant_dynamic-update-slice_fusion.refs_4_), channel_id=1, source_target_pairs={{0,3},{1,2},{2,1},{3,0},{4,7},{5,6},{6,5},{7,4},{8,11},{9,10},{10,... | collective-permute-start | bytes 811016 | tf_op jit(solution)/shard_map/ppermute | solution.py:18
  85.0 8.9 %collective-permute-start.21 = (bf16[32,1408]{1,0:T(8,128)(2,1)S(1)}, bf16[32,1408]{1,0:T(8,128)(2,1)S(1)}, u32[]{:S(2)}, u32[]{:S(2)}) collective-permute-start(bf16[32,1408]{1,0:T(8,128)(2,1)S(1)} %get-tuple-element.136.refs_0_), channel_id=1, source_target_pairs={{0,3},{1,2},{2,1},{3,0},{4,7},{5,6},{6,5},{7,4},{8,11},{9,10},{10,... | collective-permute-start | bytes 270344 | tf_op jit(solution)/shard_map/ppermute | solution.py:18
  100.5 11.2 %collective-permute-start.26 = (bf16[256,1024]{1,0:T(8,128)(2,1)S(1)}, bf16[256,1024]{1,0:T(8,128)(2,1)S(1)}, u32[]{:S(2)}, u32[]{:S(2)}) collective-permute-start(bf16[256,1024]{1,0:T(8,128)(2,1)S(1)} %get-tuple-element.144), channel_id=1, source_target_pairs={{0,16},{16,0},{1,17},{17,1},{2,18},{18,2},{3,19},{19,3},{4,20},{20... | collective-permute-start | bytes 1572872 | tf_op jit(solution)/shard_map/ppermute | solution.py:18
  106.4 5.3 %collective-permute-start.27 = (bf16[256,1024]{1,0:T(8,128)(2,1)S(1)}, bf16[256,1024]{1,0:T(8,128)(2,1)S(1)}, u32[]{:S(2)}, u32[]{:S(2)}) collective-permute-start(bf16[256,1024]{1,0:T(8,128)(2,1)S(1)} %get-tuple-element.145), channel_id=1, source_target_pairs={{0,16},{16,0},{1,17},{17,1},{2,18},{18,2},{3,19},{19,3},{4,20},{20... | collective-permute-start | bytes 1572872 | tf_op jit(solution)/shard_map/ppermute | solution.py:18
  (19 other events, 115.8 us)

commit v6 on v5

--- a/solution.py
+++ b/solution.py
@@ -40,7 +40,7 @@
 HBM = pl.BlockSpec(memory_space=pltpu.HBM)
 
 
-def call(body, outs, in_specs, scratch=(), mebibytes=4, out_specs=None, cost=None):
+def call(body, outs, in_specs, scratch=(), mebibytes=12, out_specs=None, cost=None):
     return pl.pallas_call(
         body,
         out_shape=outs,
@@ -566,7 +566,7 @@
                     pltpu.SemaphoreType.DMA((len(aways) * (mp_size + 1) + 2,)),
                 ],
                 mebibytes=16,
-            )(places_at, *placed(*groups, *inputs, other_lout if other else own_lout, gram))
+            )(places_at, *groups, *placed(*inputs, other_lout if other else own_lout, gram))
 
         groups, spots = own, ((0, 0),)
         if dp_size > 1:

time: 114 us -> 113 us (level)
  transfers between devices with their start and end apart: 30 -> 30, of which waited for: 13 -> 13; matrix products, arithmetic and copies ran while one was open for 4% -> 4% of each run, Pallas kernels for 19% -> 20%
where the time goes in v6:
time: 113 us
  starting transfers between devices  44.1 us (39%)
  Pallas kernels  31.8 us (28%)
  waiting for transfers between devices  31.1 us (28%)
  matrix products  2.79 us (2%)
  between operations  1.53 us (1%)
  other arithmetic  1.21 us (1%)
    ppermute x28, starting transfers between devices, flip(): return lax.ppermute(value, axis, pairs)  34.5 us
    ppermute x28, waiting for transfers between devices, flip(): return lax.ppermute(value, axis, pairs)  31.1 us
    pallas_call x2, Pallas kernels, gradients(): call(functools.partial(gradient_kernel, share, mp_size, aways, spots, oth...  10.8 us
    all_to_all x1, starting transfers between devices, on_device(): every_scored = lax.all_to_all(repeated, 'dp', 0, 0, tiled=True)  4.84 us
    all_to_all x1, starting transfers between devices, on_device(): every_row = lax.all_to_all(repeat(rows_wide), 'dp', 0, 0, tiled=True)  4.77 us
    pallas_call x1, Pallas kernels, on_device(): call(functools.partial(share_kernel, share), [jax.ShapeDtypeStruct((share...  4.41 us
    pallas_call x1, Pallas kernels, on_device(): call(functools.partial(score_kernel, scorer_width), [hidden_type, sums[1]...  3.7 us
    pallas_call x1, Pallas kernels, on_device(): call(learn_kernel, [jax.ShapeDtypeStruct((keep, 2 * inner), F32)], [SMEM,...  3.61 us
  transfers between devices with their start and end apart: 30, of which 13 were waited for; matrix products, arithmetic and copies ran while one was open for 4% of the time, Pallas kernels for 20%

profile of v6, /device:TPU:11, one launch (start us, length us, event | category | flops | bytes accessed | tf_op | source)
XLA Modules:
  0.0 112.7 jit_solution(5103735227679268134)
XLA Ops:
  1.4 2.5 %fusion = f32[256,1024]{0,1:T(8,128)S(1)} fusion(bf16[1,1024,1024]{2,1,0:T(8,128)(2,1)} %param.12, s32[]{:T(128)S(6)} %select_n.25), kind=kOutput, calls=%fused_computation.2 | convolution fusion | flops 536870912 | bytes 3670020 | tf_op jit(solution)/shard_map/dot_general | solution.py:26
  5.6 2.7 %shard_map.95 = (f32[128,1024]{1,0:T(8,128)S(1)}, f32[128,1]{1,0:T(8,128)S(1)}, bf16[64,2176]{1,0:T(8,128)(2,1)S(1)}, bf16[64,2176]{1,0:T(8,128)(2,1)S(1)}, f32[512,256]{1,0:T(8,128)S(1)}) custom-call(s32[3]{0:T(128)S(1)} %pad_add_fusion.1.where, bf16[128,1024]{1,0:T(8,128)(2,1)S(1)} %convolution_convert_fusion.rows.refs_4_, bf16[1024,1024]{1,0:T(8,128)(2,1)} %bitcast.37, ...), custom_call_target="tpu_custom_call" | custom-call | tf_op jit(solution)/shard_map/pallas_call | solution.py:407
  10.4 4.8 %all-to-all-start = ((bf16[4,128,1152]{2,1,0:T(8,128)(2,1)}), bf16[4,128,1152]{2,1,0:T(8,128)(2,1)S(1)}, u32[]{:S(2)}, u32[]{:S(2)}) async-start(bf16[4,128,1152]{2,1,0:T(8,128)(2,1)} %bitcast.39), calls=%async_computation | async-start | bytes 2359296 | tf_op jit(solution)/shard_map/all_to_all | solution.py:415
  15.4 1.2 %collective-permute-start.3 = (bf16[64,2176]{1,0:T(8,128)(2,1)S(1)}, bf16[64,2176]{1,0:T(8,128)(2,1)S(1)}, u32[]{:S(2)}, u32[]{:S(2)}) collective-permute-start(bf16[64,2176]{1,0:T(8,128)(2,1)S(1)} %get-tuple-element.82), channel_id=1, source_target_pairs={{0,2},{1,3},{2,0},{3,1},{4,6},{5,7},{6,4},{7,5},{8,10},{9,11},{10,... | collective-permute-start | bytes 835592 | tf_op jit(solution)/shard_map/ppermute | solution.py:18
  16.6 6.2 %collective-permute-done.2.got_top = bf16[64,2176]{1,0:T(8,128)(2,1)S(1)} collective-permute-done((bf16[64,2176]{1,0:T(8,128)(2,1)}, bf16[64,2176]{1,0:T(8,128)(2,1)S(1)}, u32[]{:S(2)}, u32[]{:S(2)}) %collective-permute-start.2) | collective-permute-done | bytes 278560 | tf_op jit(solution)/shard_map/ppermute | solution.py:18
  23.1 1.3 %collective-permute-start.4 = (bf16[64,2176]{1,0:T(8,128)(2,1)S(1)}, bf16[64,2176]{1,0:T(8,128)(2,1)S(1)}, u32[]{:S(2)}, u32[]{:S(2)}) collective-permute-start(bf16[64,2176]{1,0:T(8,128)(2,1)S(1)} %get-tuple-element.90), channel_id=1, source_target_pairs={{0,2},{1,3},{2,0},{3,1},{4,6},{5,7},{6,4},{7,5},{8,10},{9,11},{10,... | collective-permute-start | bytes 835592 | tf_op jit(solution)/shard_map/ppermute | solution.py:18
  25.4 4.3 %collective-permute-done.4.refs_2_ = bf16[64,2176]{1,0:T(8,128)(2,1)S(1)} collective-permute-done((bf16[64,2176]{1,0:T(8,128)(2,1)S(1)}, bf16[64,2176]{1,0:T(8,128)(2,1)S(1)}, u32[]{:S(2)}, u32[]{:S(2)}) %collective-permute-start.4) | collective-permute-done | bytes 278560 | tf_op jit(solution)/shard_map/ppermute | solution.py:18
  30.7 3.3 %shard_map.97 = (bf16[128,1024]{1,0:T(8,128)(2,1)S(1)}, f32[128,1024]{1,0:T(8,128)S(1)}, f32[128,1]{1,0:T(8,128)S(1)}, bf16[64,1152]{1,0:T(8,128)(2,1)S(1)}, bf1...) custom-call(s32[3]{0:T(128)S(1)} %pad_add_fusion.1.where, f32[128,1024]{1,0:T(8,128)S(1)} %get-tuple-element.86.refs_0_, ...), custom_call_target="tpu_custom_call" | custom-call | tf_op jit(solution)/shard_map/pallas_call | solution.py:428
  35.0 3.6 %shard_map.99.given = f32[128,2048]{1,0:T(8,128)S(1)} custom-call(s32[3]{0:T(128)S(1)} %pad_add_fusion.1.where, bf16[128,1024]{1,0:T(8,128)(2,1)S(1)} %convolution_convert_fusion.rows.refs_4_, bf16[1024,1024]{1,0:T(8,128)(2,1)} %bitcast.11.value_a, bf16[1024,1024]{1,0:T(8,128)(2,1)} %collective-permute-done.9.value_b, ...), custom_call_target="tpu_custom_call" | custom-call | tf_op jit(solution)/shard_map/pallas_call | solution.py:438
  40.9 3.2 %collective-permute-done.11.refs_2_ = bf16[64,1152]{1,0:T(8,128)(2,1)S(1)} collective-permute-done((bf16[64,1152]{1,0:T(8,128)(2,1)S(1)}, bf16[64,1152]{1,0:T(8,128)(2,1)S(1)}, u32[]{:S(2)}, u32[]{:S(2)}) %collective-permute-start.11) | collective-permute-done | bytes 147488 | tf_op jit(solution)/shard_map/ppermute | solution.py:18
  44.1 3.7 %shard_map.100 = (bf16[128,1024]{1,0:T(8,128)(2,1)S(1)}, f32[128,1]{1,0:T(8,128)S(1)}, bf16[512,1024]{1,0:T(8,128)(2,1)}) custom-call(s32[3]{0:T(128)S(1)} %pad_add_fusion.1.where, f32[128,1024]{1,0:T(8,128)S(1)} %get-tuple-element.104.refs_0_, f32[128,1]{1,0:T(8,128)S(1)} %get-tuple-element.105.refs_1_, ...), custom_call_target="tpu_custom_call" | custom-call | tf_op jit(solution)/shard_map/pallas_call | solution.py:452
  47.8 4.8 %all-to-all-start.1 = ((bf16[4,128,1024]{2,1,0:T(8,128)(2,1)}), bf16[4,128,1024]{2,1,0:T(8,128)(2,1)}, u32[]{:S(2)}, u32[]{:S(2)}) async-start(bf16[4,128,1024]{2,1,0:T(8,128)(2,1)} %bitcast.40), calls=%async_computation.1 | async-start | bytes 2097152 | tf_op jit(solution)/shard_map/all_to_all | solution.py:468
  52.7 4.4 %shard_map.102 = (f32[32,2048]{1,0:T(8,128)S(1)}, f32[32,1]{1,0:T(8,128)S(1)}, f32[32,1]{1,0:T(8,128)S(1)}, bf16[32,2176]{1,0:T(8,128)(2,1)}, bf16[32,2176]{1,0:T(8,128)(2,1)}, /*index=5*/bf16[32,2176]{1,0:T(8,128)(2,1)}) custom-call(s32[3]{0:T(128)S(1)} %pad_add_fusion.1.where, bf16[128,1024]{1,0:T(8,128)(2,1)S(1)} %get-tuple-element.117.scored, ...), custom_call_target="tpu_custom_call" | custom-call | tf_op jit(solution)/shard_map/pallas_call | solution.py:469
  59.8 1.9 %collective-permute-done.13.refs_0_ = bf16[32,2176]{1,0:T(8,128)(2,1)S(1)} collective-permute-done((bf16[32,2176]{1,0:T(8,128)(2,1)}, bf16[32,2176]{1,0:T(8,128)(2,1)S(1)}, u32[]{:S(2)}, u32[]{:S(2)}) %collective-permute-start.13) | collective-permute-done | bytes 139296 | tf_op jit(solution)/shard_map/ppermute | solution.py:18
  64.6 1.7 %collective-permute-start.17 = (bf16[32,1408]{1,0:T(8,128)(2,1)S(1)}, bf16[32,1408]{1,0:T(8,128)(2,1)S(1)}, u32[]{:S(2)}, u32[]{:S(2)}) collective-permute-start(bf16[32,1408]{1,0:T(8,128)(2,1)S(1)} %get-tuple-element.130), channel_id=1, source_target_pairs={{0,8},{4,12},{8,0},{12,4},{1,9},{5,13},{9,1},{13,5},{2,10},{6,14},... | collective-permute-start | bytes 270344 | tf_op jit(solution)/shard_map/ppermute | solution.py:18
  68.7 9.2 %collective-permute-start.25 = (bf16[512,256]{1,0:T(8,128)(2,1)S(1)}, bf16[512,256]{1,0:T(8,128)(2,1)S(1)}, u32[]{:S(2)}, u32[]{:S(2)}) collective-permute-start(bf16[512,256]{1,0:T(8,128)(2,1)S(1)} %get-tuple-element.141), channel_id=1, source_target_pairs={{0,16},{16,0},{1,17},{17,1},{2,18},{18,2},{3,19},{19,3},{4,20},{20... | collective-permute-start | bytes 786440 | tf_op jit(solution)/shard_map/ppermute | solution.py:18
  77.9 4.2 %collective-permute-done.18 = bf16[32,1408]{1,0:T(8,128)(2,1)S(1)} collective-permute-done((bf16[32,1408]{1,0:T(8,128)(2,1)S(1)}, bf16[32,1408]{1,0:T(8,128)(2,1)S(1)}, u32[]{:S(2)}, u32[]{:S(2)}) %collective-permute-start.18) | collective-permute-done | bytes 90144 | tf_op jit(solution)/shard_map/ppermute | solution.py:18
  82.1 1.4 %collective-permute-start.22 = (bf16[32,4224]{1,0:T(8,128)(2,1)S(1)}, bf16[32,4224]{1,0:T(8,128)(2,1)S(1)}, u32[]{:S(2)}, u32[]{:S(2)}) collective-permute-start(bf16[32,4224]{1,0:T(8,128)(2,1)S(1)} %constant_dynamic-update-slice_fusion.refs_4_), channel_id=1, source_target_pairs={{0,1},{1,0},{2,3},{3,2},{4,5},{5,4},{6,7},{7,6},{8,9},{9,8},{10,11... | collective-permute-start | bytes 811016 | tf_op jit(solution)/shard_map/ppermute | solution.py:18
  83.5 1.3 %collective-permute-start.24 = (bf16[32,4224]{1,0:T(8,128)(2,1)S(1)}, bf16[32,4224]{1,0:T(8,128)(2,1)S(1)}, u32[]{:S(2)}, u32[]{:S(2)}) collective-permute-start(bf16[32,4224]{1,0:T(8,128)(2,1)S(1)} %constant_dynamic-update-slice_fusion.refs_4_), channel_id=1, source_target_pairs={{0,3},{1,2},{2,1},{3,0},{4,7},{5,6},{6,5},{7,4},{8,11},{9,10},{10,... | collective-permute-start | bytes 811016 | tf_op jit(solution)/shard_map/ppermute | solution.py:18
  87.0 6.7 %collective-permute-done.21.refs_3_ = bf16[32,1408]{1,0:T(8,128)(2,1)S(1)} collective-permute-done((bf16[32,1408]{1,0:T(8,128)(2,1)S(1)}, bf16[32,1408]{1,0:T(8,128)(2,1)S(1)}, u32[]{:S(2)}, u32[]{:S(2)}) %collective-permute-start.21) | collective-permute-done | bytes 90144 | tf_op jit(solution)/shard_map/ppermute | solution.py:18
  94.3 5.4 %shard_map.105 = (bf16[256,1024]{1,0:T(8,128)(2,1)S(1)}, bf16[256,1024]{1,0:T(8,128)(2,1)S(1)}) custom-call(s32[3]{0:T(128)S(1)} %pad_add_fusion.where, bf16[32,1408]{1,0:T(8,128)(2,1)S(1)} %get-tuple-element.136.refs_0_, bf16[32,1408]{1,0:T(8,128)(2,1)S(1)} %collective-permute-done.19.refs_1_, bf16[32,1408]{1,0:T(8,128)(2,1)S(1)} %collective-permute-done.20.refs_2_, ...), custom_call_target="tpu_custom_call" | custom-call | tf_op jit(solution)/shard_map/pallas_call | solution.py:554
  99.7 6.0 %collective-permute-start.26 = (bf16[256,1024]{1,0:T(8,128)(2,1)S(1)}, bf16[256,1024]{1,0:T(8,128)(2,1)S(1)}, u32[]{:S(2)}, u32[]{:S(2)}) collective-permute-start(bf16[256,1024]{1,0:T(8,128)(2,1)S(1)} %get-tuple-element.144), channel_id=1, source_target_pairs={{0,16},{16,0},{1,17},{17,1},{2,18},{18,2},{3,19},{19,3},{4,20},{20... | collective-permute-start | bytes 1572872 | tf_op jit(solution)/shard_map/ppermute | solution.py:18
  105.8 5.4 %shard_map.104 = (f32[256,1024]{1,0:T(8,128)S(1)}, f32[256,1024]{1,0:T(8,128)S(1)}) custom-call(s32[3]{0:T(128)S(1)} %pad_add_fusion.where, bf16[32,1408]{1,0:T(8,128)(2,1)S(1)} %get-tuple-element.136.refs_0_, bf16[32,1408]{1,0:T(8,128)(2,1)S(1)} %collective-permute-done.19.refs_1_, bf16[32,1408]{1,0:T(8,128)(2,1)S(1)} %collective-permute-done.20.refs_2_, ...), custom_call_target="tpu_custom_call" | custom-call | tf_op jit(solution)/shard_map/pallas_call | solution.py:554
  111.2 1.5 %shard_map.106 = (f32[256,1024]{1,0:T(8,128)}, f32[256,1024]{1,0:T(8,128)}) custom-call(f32[256,1024]{1,0:T(8,128)S(1)} %get-tuple-element.142.value_near, f32[256,1024]{1,0:T(8,128)S(1)} %get-tuple-element.143.out_near, bf16[256,1024]{1,0:T(8,128)(2,1)S(1)} %collective-permute-done.26.value_far, bf16[256,1024]{1,0:T(8,128)(2,1)S(1)} %collective-permute-done.27.out_far), custom_call_target="tpu_custom_call" | custom-call | tf_op jit(solution)/shard_map/pallas_call | solution.py:593
  (72 shorter events, 20.5 us)
Async XLA Ops:
  0.6 4.9 %collective-permute-start = (bf16[1024,1024]{1,0:T(8,128)(2,1)}, bf16[1024,1024]{1,0:T(8,128)(2,1)}, u32[]{:S(2)}, u32[]{:S(2)}) collective-permute-start(bf16[1024,1024]{1,0:T(8,128)(2,1)} %bitcast.36), channel_id=1, source_target_pairs={{0,16},{16,0},{1,17},{17,1},{2,18},{18,2},{3,19},{19,3},{4,20},{20... | collective-permute-start | bytes 6291464 | tf_op jit(solution)/shard_map/ppermute | solution.py:18
  8.3 22.4 %collective-permute-start.6 = (bf16[1024,1024]{1,0:T(8,128)(2,1)}, bf16[1024,1024]{1,0:T(8,128)(2,1)}, u32[]{:S(2)}, u32[]{:S(2)}) collective-permute-start(bf16[1024,1024]{1,0:T(8,128)(2,1)} %bitcast.10.refs_5_.refs_6_), channel_id=1, source_target_pairs={{0,16},{16,0},{1,17},{17,1},{2,18},{18,2},{3,19},{19,3},{4,20},{20... | collective-permute-start | bytes 6291464 | tf_op jit(solution)/shard_map/ppermute | solution.py:18
  8.7 26.3 %collective-permute-start.9 = (bf16[1024,1024]{1,0:T(8,128)(2,1)}, bf16[1024,1024]{1,0:T(8,128)(2,1)}, u32[]{:S(2)}, u32[]{:S(2)}) collective-permute-start(bf16[1024,1024]{1,0:T(8,128)(2,1)} %bitcast.11.value_a), channel_id=1, source_target_pairs={{0,16},{16,0},{1,17},{17,1},{2,18},{18,2},{3,19},{19,3},{4,20},{20... | collective-permute-start | bytes 6291464 | tf_op jit(solution)/shard_map/ppermute | solution.py:18
  8.8 26.1 %collective-permute-start.10 = (bf16[1024,1024]{1,0:T(8,128)(2,1)}, bf16[1024,1024]{1,0:T(8,128)(2,1)}, u32[]{:S(2)}, u32[]{:S(2)}) collective-permute-start(bf16[1024,1024]{1,0:T(8,128)(2,1)} %bitcast.7.lout_a.refs_10_), channel_id=1, source_target_pairs={{0,16},{16,0},{1,17},{17,1},{2,18},{18,2},{3,19},{19,3},{4,20},{20... | collective-permute-start | bytes 6291464 | tf_op jit(solution)/shard_map/ppermute | solution.py:18
  10.4 37.4 %all-to-all-start = ((bf16[4,128,1152]{2,1,0:T(8,128)(2,1)}), bf16[4,128,1152]{2,1,0:T(8,128)(2,1)S(1)}, u32[]{:S(2)}, u32[]{:S(2)}) async-start(bf16[4,128,1152]{2,1,0:T(8,128)(2,1)} %bitcast.39), calls=%async_computation | async-start | bytes 2359296 | tf_op jit(solution)/shard_map/all_to_all | solution.py:415
  15.1 7.7 %collective-permute-start.2 = (bf16[64,2176]{1,0:T(8,128)(2,1)}, bf16[64,2176]{1,0:T(8,128)(2,1)S(1)}, u32[]{:S(2)}, u32[]{:S(2)}) collective-permute-start(bf16[64,2176]{1,0:T(8,128)(2,1)} %copy-done.2), channel_id=1, source_target_pairs={{0,1},{1,0},{2,3},{3,2},{4,5},{5,4},{6,7},{7,6},{8,9},{9,8},{10,11... | collective-permute-start | bytes 835592 | tf_op jit(solution)/shard_map/ppermute | solution.py:18
  15.4 7.4 %collective-permute-start.3 = (bf16[64,2176]{1,0:T(8,128)(2,1)S(1)}, bf16[64,2176]{1,0:T(8,128)(2,1)S(1)}, u32[]{:S(2)}, u32[]{:S(2)}) collective-permute-start(bf16[64,2176]{1,0:T(8,128)(2,1)S(1)} %get-tuple-element.82), channel_id=1, source_target_pairs={{0,2},{1,3},{2,0},{3,1},{4,6},{5,7},{6,4},{7,5},{8,10},{9,11},{10,... | collective-permute-start | bytes 835592 | tf_op jit(solution)/shard_map/ppermute | solution.py:18
  23.1 6.6 %collective-permute-start.4 = (bf16[64,2176]{1,0:T(8,128)(2,1)S(1)}, bf16[64,2176]{1,0:T(8,128)(2,1)S(1)}, u32[]{:S(2)}, u32[]{:S(2)}) collective-permute-start(bf16[64,2176]{1,0:T(8,128)(2,1)S(1)} %get-tuple-element.90), channel_id=1, source_target_pairs={{0,2},{1,3},{2,0},{3,1},{4,6},{5,7},{6,4},{7,5},{8,10},{9,11},{10,... | collective-permute-start | bytes 835592 | tf_op jit(solution)/shard_map/ppermute | solution.py:18
  24.4 6.2 %collective-permute-start.5 = (bf16[64,2176]{1,0:T(8,128)(2,1)S(1)}, bf16[64,2176]{1,0:T(8,128)(2,1)S(1)}, u32[]{:S(2)}, u32[]{:S(2)}) collective-permute-start(bf16[64,2176]{1,0:T(8,128)(2,1)S(1)} %get-tuple-element.91), channel_id=1, source_target_pairs={{0,1},{1,0},{2,3},{3,2},{4,5},{5,4},{6,7},{7,6},{8,9},{9,8},{10,11... | collective-permute-start | bytes 835592 | tf_op jit(solution)/shard_map/ppermute | solution.py:18
  38.9 5.2 %collective-permute-start.11 = (bf16[64,1152]{1,0:T(8,128)(2,1)S(1)}, bf16[64,1152]{1,0:T(8,128)(2,1)S(1)}, u32[]{:S(2)}, u32[]{:S(2)}) collective-permute-start(bf16[64,1152]{1,0:T(8,128)(2,1)S(1)} %get-tuple-element.112), channel_id=1, source_target_pairs={{0,2},{1,3},{2,0},{3,1},{4,6},{5,7},{6,4},{7,5},{8,10},{9,11},{10,... | collective-permute-start | bytes 442376 | tf_op jit(solution)/shard_map/ppermute | solution.py:18
  47.8 46.4 %all-to-all-start.1 = ((bf16[4,128,1024]{2,1,0:T(8,128)(2,1)}), bf16[4,128,1024]{2,1,0:T(8,128)(2,1)}, u32[]{:S(2)}, u32[]{:S(2)}) async-start(bf16[4,128,1024]{2,1,0:T(8,128)(2,1)} %bitcast.40), calls=%async_computation.1 | async-start | bytes 2097152 | tf_op jit(solution)/shard_map/all_to_all | solution.py:468
  58.6 5.0 %collective-permute-start.15 = (bf16[32,2176]{1,0:T(8,128)(2,1)}, bf16[32,2176]{1,0:T(8,128)(2,1)S(1)}, u32[]{:S(2)}, u32[]{:S(2)}) collective-permute-start(bf16[32,2176]{1,0:T(8,128)(2,1)} %get-tuple-element.125), channel_id=1, source_target_pairs={{0,3},{1,2},{2,1},{3,0},{4,7},{5,6},{6,5},{7,4},{8,11},{9,10},{10,... | collective-permute-start | bytes 417800 | tf_op jit(solution)/shard_map/ppermute | solution.py:18
  63.8 4.9 %collective-permute-start.16 = (bf16[32,1408]{1,0:T(8,128)(2,1)S(1)}, bf16[32,1408]{1,0:T(8,128)(2,1)S(1)}, u32[]{:S(2)}, u32[]{:S(2)}) collective-permute-start(bf16[32,1408]{1,0:T(8,128)(2,1)S(1)} %get-tuple-element.129), channel_id=1, source_target_pairs={{0,4},{4,0},{8,12},{12,8},{1,5},{5,1},{9,13},{13,9},{2,6},{6,2},{1... | collective-permute-start | bytes 270344 | tf_op jit(solution)/shard_map/ppermute | solution.py:18
  64.6 13.3 %collective-permute-start.17 = (bf16[32,1408]{1,0:T(8,128)(2,1)S(1)}, bf16[32,1408]{1,0:T(8,128)(2,1)S(1)}, u32[]{:S(2)}, u32[]{:S(2)}) collective-permute-start(bf16[32,1408]{1,0:T(8,128)(2,1)S(1)} %get-tuple-element.130), channel_id=1, source_target_pairs={{0,8},{4,12},{8,0},{12,4},{1,9},{5,13},{9,1},{13,5},{2,10},{6,14},... | collective-permute-start | bytes 270344 | tf_op jit(solution)/shard_map/ppermute | solution.py:18
  66.3 15.8 %collective-permute-start.18 = (bf16[32,1408]{1,0:T(8,128)(2,1)S(1)}, bf16[32,1408]{1,0:T(8,128)(2,1)S(1)}, u32[]{:S(2)}, u32[]{:S(2)}) collective-permute-start(bf16[32,1408]{1,0:T(8,128)(2,1)S(1)} %get-tuple-element.131), channel_id=1, source_target_pairs={{0,12},{4,8},{8,4},{12,0},{1,13},{5,9},{9,5},{13,1},{2,14},{6,10},... | collective-permute-start | bytes 270344 | tf_op jit(solution)/shard_map/ppermute | solution.py:18
  66.6 15.5 %collective-permute-start.19 = (bf16[32,1408]{1,0:T(8,128)(2,1)S(1)}, bf16[32,1408]{1,0:T(8,128)(2,1)S(1)}, u32[]{:S(2)}, u32[]{:S(2)}) collective-permute-start(bf16[32,1408]{1,0:T(8,128)(2,1)S(1)} %get-tuple-element.136.refs_0_), channel_id=1, source_target_pairs={{0,1},{1,0},{2,3},{3,2},{4,5},{5,4},{6,7},{7,6},{8,9},{9,8},{10,11... | collective-permute-start | bytes 270344 | tf_op jit(solution)/shard_map/ppermute | solution.py:18
  67.3 14.7 %collective-permute-start.20 = (bf16[32,1408]{1,0:T(8,128)(2,1)S(1)}, bf16[32,1408]{1,0:T(8,128)(2,1)S(1)}, u32[]{:S(2)}, u32[]{:S(2)}) collective-permute-start(bf16[32,1408]{1,0:T(8,128)(2,1)S(1)} %get-tuple-element.136.refs_0_), channel_id=1, source_target_pairs={{0,2},{1,3},{2,0},{3,1},{4,6},{5,7},{6,4},{7,5},{8,10},{9,11},{10,... | collective-permute-start | bytes 270344 | tf_op jit(solution)/shard_map/ppermute | solution.py:18
  68.7 17.3 %collective-permute-start.25 = (bf16[512,256]{1,0:T(8,128)(2,1)S(1)}, bf16[512,256]{1,0:T(8,128)(2,1)S(1)}, u32[]{:S(2)}, u32[]{:S(2)}) collective-permute-start(bf16[512,256]{1,0:T(8,128)(2,1)S(1)} %get-tuple-element.141), channel_id=1, source_target_pairs={{0,16},{16,0},{1,17},{17,1},{2,18},{18,2},{3,19},{19,3},{4,20},{20... | collective-permute-start | bytes 786440 | tf_op jit(solution)/shard_map/ppermute | solution.py:18
  82.1 11.7 %collective-permute-start.22 = (bf16[32,4224]{1,0:T(8,128)(2,1)S(1)}, bf16[32,4224]{1,0:T(8,128)(2,1)S(1)}, u32[]{:S(2)}, u32[]{:S(2)}) collective-permute-start(bf16[32,4224]{1,0:T(8,128)(2,1)S(1)} %constant_dynamic-update-slice_fusion.refs_4_), channel_id=1, source_target_pairs={{0,1},{1,0},{2,3},{3,2},{4,5},{5,4},{6,7},{7,6},{8,9},{9,8},{10,11... | collective-permute-start | bytes 811016 | tf_op jit(solution)/shard_map/ppermute | solution.py:18
  83.5 10.7 %collective-permute-start.23 = (bf16[32,4224]{1,0:T(8,128)(2,1)S(1)}, bf16[32,4224]{1,0:T(8,128)(2,1)S(1)}, u32[]{:S(2)}, u32[]{:S(2)}) collective-permute-start(bf16[32,4224]{1,0:T(8,128)(2,1)S(1)} %constant_dynamic-update-slice_fusion.refs_4_), channel_id=1, source_target_pairs={{0,2},{1,3},{2,0},{3,1},{4,6},{5,7},{6,4},{7,5},{8,10},{9,11},{10,... | collective-permute-start | bytes 811016 | tf_op jit(solution)/shard_map/ppermute | solution.py:18
  83.5 10.7 %collective-permute-start.24 = (bf16[32,4224]{1,0:T(8,128)(2,1)S(1)}, bf16[32,4224]{1,0:T(8,128)(2,1)S(1)}, u32[]{:S(2)}, u32[]{:S(2)}) collective-permute-start(bf16[32,4224]{1,0:T(8,128)(2,1)S(1)} %constant_dynamic-update-slice_fusion.refs_4_), channel_id=1, source_target_pairs={{0,3},{1,2},{2,1},{3,0},{4,7},{5,6},{6,5},{7,4},{8,11},{9,10},{10,... | collective-permute-start | bytes 811016 | tf_op jit(solution)/shard_map/ppermute | solution.py:18
  84.9 8.9 %collective-permute-start.21 = (bf16[32,1408]{1,0:T(8,128)(2,1)S(1)}, bf16[32,1408]{1,0:T(8,128)(2,1)S(1)}, u32[]{:S(2)}, u32[]{:S(2)}) collective-permute-start(bf16[32,1408]{1,0:T(8,128)(2,1)S(1)} %get-tuple-element.136.refs_0_), channel_id=1, source_target_pairs={{0,3},{1,2},{2,1},{3,0},{4,7},{5,6},{6,5},{7,4},{8,11},{9,10},{10,... | collective-permute-start | bytes 270344 | tf_op jit(solution)/shard_map/ppermute | solution.py:18
  99.7 11.5 %collective-permute-start.26 = (bf16[256,1024]{1,0:T(8,128)(2,1)S(1)}, bf16[256,1024]{1,0:T(8,128)(2,1)S(1)}, u32[]{:S(2)}, u32[]{:S(2)}) collective-permute-start(bf16[256,1024]{1,0:T(8,128)(2,1)S(1)} %get-tuple-element.144), channel_id=1, source_target_pairs={{0,16},{16,0},{1,17},{17,1},{2,18},{18,2},{3,19},{19,3},{4,20},{20... | collective-permute-start | bytes 1572872 | tf_op jit(solution)/shard_map/ppermute | solution.py:18
  105.7 5.5 %collective-permute-start.27 = (bf16[256,1024]{1,0:T(8,128)(2,1)S(1)}, bf16[256,1024]{1,0:T(8,128)(2,1)S(1)}, u32[]{:S(2)}, u32[]{:S(2)}) collective-permute-start(bf16[256,1024]{1,0:T(8,128)(2,1)S(1)} %get-tuple-element.145), channel_id=1, source_target_pairs={{0,16},{16,0},{1,17},{17,1},{2,18},{18,2},{3,19},{19,3},{4,20},{20... | collective-permute-start | bytes 1572872 | tf_op jit(solution)/shard_map/ppermute | solution.py:18
  (11 other events, 45.3 us)

commit v7 on v6

--- a/solution.py
+++ b/solution.py
@@ -119,29 +119,26 @@
     return jnp.concatenate(parts, axis=0), jnp.concatenate(norms, axis=0)
 
 
-def repeat_kernel(array, repeated, sems):
-    rows = array.shape[0]
-    copies = [
-        start_copy(array, repeated.at[pl.ds(place * rows, rows), :], sems.at[place])
-        for place in range(repeated.shape[0] // rows)
-    ]
-    for copy in copies:
-        copy.wait()
-
-
 def start_kernel(with_gram, where, rows, value_a, value_b, *refs):
     gram_a, gram_b = refs[:2] if with_gram else (None, None)
     refs = refs[2:] if with_gram else refs
     part, norm, top, low = refs[:4]
-    gram, (weight, sem) = refs[4] if with_gram else None, refs[-2:]
+    gram, (repeated, weight, sem, sems) = refs[4] if with_gram else None, refs[-4:]
     fetch(where[0] == 1, value_a, value_b, weight, sem)
-    row = rows[...]
+    keep = rows.shape[0]
+    copies = [
+        start_copy(rows, repeated.at[pl.ds(place * keep, keep), :], sems.at[place])
+        for place in range(repeated.shape[0] // keep)
+    ]
+    row = rows[:, : weight.shape[0]]
     norm[...] = square_sum(row)
     if with_gram:
         gram[...] = gram_a[...] + gram_b[...].astype(F32)
     pltpu.make_async_copy(value_a, weight, sem).wait()
     part[...] = matmul(row, weight[...])
     emit(part, norm, (top, low), gram)
+    for copy in copies:
+        copy.wait()
 
 
 def between_kernel(with_gram, part_in, norm_in, got_top, got_low, *refs):
@@ -368,15 +365,6 @@
     goal = jnp.where(is_live, keep_dest[0] + 1, 0).astype(F32)[:, None]
     rows_wide = jnp.concatenate([rows, jnp.broadcast_to(goal, (keep, SIDE)).astype(BF)], axis=1)
 
-    def repeat(array):
-        return call(
-            repeat_kernel,
-            [pltpu.HBM((dp_size * keep, array.shape[1]), BF)],
-            [VMEM],
-            [pltpu.SemaphoreType.DMA((dp_size,))],
-            out_specs=[HBM],
-        )(array)[0]
-
     gram = matmul_nt(own_lout, lax.dynamic_slice_in_dim(own_lout, dp_at * block, block, 0))
     half = inner // 2
     at = lax.axis_index("segment")
@@ -404,15 +392,21 @@
     def halves(outs):
         return outs[0], outs[1], outs[2:4], list(outs[4:])
 
-    outs = call(
+    *outs, repeated = call(
         functools.partial(start_kernel, direct),
-        wide_state,
+        wide_state + [pltpu.HBM((dp_size * keep, width + SIDE), BF)],
         [SMEM, VMEM, HBM, HBM] + [VMEM] * (2 * direct),
-        [weight, pltpu.SemaphoreType.DMA],
+        [weight, pltpu.SemaphoreType.DMA, pltpu.SemaphoreType.DMA((dp_size,))],
         mebibytes=12,
-    )(where, rows, *placed(own_value, other_value), *((kept_half, got_half) if direct else ()))
+        out_specs=[VMEM] * len(wide_state) + [HBM],
+    )(
+        where,
+        rows_wide,
+        *placed(own_value, other_value),
+        *((kept_half, got_half) if direct else ()),
+    )
     part, rows_squares, sents, gram_sum = halves(outs)
-    every_row = lax.all_to_all(repeat(rows_wide), "dp", 0, 0, tiled=True)
+    every_row = lax.all_to_all(repeated, "dp", 0, 0, tiled=True)
     own_out, own_lvalue, own_lout, sents = lax.optimization_barrier(
         (own_out, own_lvalue, own_lout, sents)
     )

time: 113 us -> 113 us (level)
    pallas_call x2 -> x1, Pallas kernels: 3.71 us -> 3.09 us  [on_device(): call(functools.partial(start_kernel, direct), wide_state + [pltpu.HBM((dp...]
  transfers between devices with their start and end apart: 30 -> 30, of which waited for: 13 -> 13; matrix products, arithmetic and copies ran while one was open for 4% -> 4% of each run, Pallas kernels for 20% -> 19%
where the time goes in v7:
time: 113 us
  starting transfers between devices  44 us (39%)
  Pallas kernels  31.2 us (28%)
  waiting for transfers between devices  30.9 us (27%)
  matrix products  2.79 us (2%)
  between operations  1.54 us (1%)
  other arithmetic  1.21 us (1%)
    ppermute x28, starting transfers between devices, flip(): return lax.ppermute(value, axis, pairs)  34.4 us
    ppermute x28, waiting for transfers between devices, flip(): return lax.ppermute(value, axis, pairs)  30.9 us
    pallas_call x2, Pallas kernels, gradients(): call(functools.partial(gradient_kernel, share, mp_size, aways, spots, oth...  10.8 us
    all_to_all x1, starting transfers between devices, on_device(): every_scored = lax.all_to_all(repeated, 'dp', 0, 0, tiled=True)  4.84 us
    all_to_all x1, starting transfers between devices, on_device(): every_row = lax.all_to_all(repeated, 'dp', 0, 0, tiled=True)  4.76 us
    pallas_call x1, Pallas kernels, on_device(): call(functools.partial(share_kernel, share), [jax.ShapeDtypeStruct((share...  4.41 us
    pallas_call x1, Pallas kernels, on_device(): call(functools.partial(score_kernel, scorer_width), [hidden_type, sums[1]...  3.7 us
    pallas_call x1, Pallas kernels, on_device(): call(learn_kernel, [jax.ShapeDtypeStruct((keep, 2 * inner), F32)], [SMEM,...  3.61 us
  transfers between devices with their start and end apart: 30, of which 13 were waited for; matrix products, arithmetic and copies ran while one was open for 4% of the time, Pallas kernels for 19%

profile of v7, /device:TPU:11, one launch (start us, length us, event | category | flops | bytes accessed | tf_op | source)
XLA Modules:
  0.0 112.5 jit_solution(1260164987027456745)
XLA Ops:
  1.4 2.5 %fusion = f32[256,1024]{0,1:T(8,128)S(1)} fusion(bf16[1,1024,1024]{2,1,0:T(8,128)(2,1)} %param.12, s32[]{:T(128)S(6)} %select_n.26), kind=kOutput, calls=%fused_computation.2 | convolution fusion | flops 536870912 | bytes 3670020 | tf_op jit(solution)/shard_map/dot_general | solution.py:26
  5.6 3.1 %shard_map.95 = (f32[128,1024]{1,0:T(8,128)S(1)}, f32[128,1]{1,0:T(8,128)S(1)}, bf16[64,2176]{1,0:T(8,128)(2,1)S(1)}, bf16[64,2176]{1,0:T(8,128)(2,1)S(1)}, f32[...) custom-call(s32[3]{0:T(128)S(1)} %pad_add_fusion.1.where, bf16[128,1152]{1,0:T(8,128)(2,1)S(1)} %pad_maximum_fusion.rows, ...), custom_call_target="tpu_custom_call" | custom-call | tf_op jit(solution)/shard_map/pallas_call | solution.py:395
  10.2 4.8 %all-to-all-start = ((bf16[4,128,1152]{2,1,0:T(8,128)(2,1)}), bf16[4,128,1152]{2,1,0:T(8,128)(2,1)S(1)}, u32[]{:S(2)}, u32[]{:S(2)}) async-start(bf16[4,128,1152]{2,1,0:T(8,128)(2,1)} %bitcast.39), calls=%async_computation | async-start | bytes 2359296 | tf_op jit(solution)/shard_map/all_to_all | solution.py:409
  15.3 1.2 %collective-permute-start.3 = (bf16[64,2176]{1,0:T(8,128)(2,1)S(1)}, bf16[64,2176]{1,0:T(8,128)(2,1)S(1)}, u32[]{:S(2)}, u32[]{:S(2)}) collective-permute-start(bf16[64,2176]{1,0:T(8,128)(2,1)S(1)} %get-tuple-element.83), channel_id=1, source_target_pairs={{0,2},{1,3},{2,0},{3,1},{4,6},{5,7},{6,4},{7,5},{8,10},{9,11},{10,... | collective-permute-start | bytes 835592 | tf_op jit(solution)/shard_map/ppermute | solution.py:18
  16.5 6.2 %collective-permute-done.2.got_top = bf16[64,2176]{1,0:T(8,128)(2,1)S(1)} collective-permute-done((bf16[64,2176]{1,0:T(8,128)(2,1)}, bf16[64,2176]{1,0:T(8,128)(2,1)S(1)}, u32[]{:S(2)}, u32[]{:S(2)}) %collective-permute-start.2) | collective-permute-done | bytes 278560 | tf_op jit(solution)/shard_map/ppermute | solution.py:18
  23.0 1.3 %collective-permute-start.4 = (bf16[64,2176]{1,0:T(8,128)(2,1)S(1)}, bf16[64,2176]{1,0:T(8,128)(2,1)S(1)}, u32[]{:S(2)}, u32[]{:S(2)}) collective-permute-start(bf16[64,2176]{1,0:T(8,128)(2,1)S(1)} %get-tuple-element.91), channel_id=1, source_target_pairs={{0,2},{1,3},{2,0},{3,1},{4,6},{5,7},{6,4},{7,5},{8,10},{9,11},{10,... | collective-permute-start | bytes 835592 | tf_op jit(solution)/shard_map/ppermute | solution.py:18
  25.2 4.3 %collective-permute-done.4.refs_2_ = bf16[64,2176]{1,0:T(8,128)(2,1)S(1)} collective-permute-done((bf16[64,2176]{1,0:T(8,128)(2,1)S(1)}, bf16[64,2176]{1,0:T(8,128)(2,1)S(1)}, u32[]{:S(2)}, u32[]{:S(2)}) %collective-permute-start.4) | collective-permute-done | bytes 278560 | tf_op jit(solution)/shard_map/ppermute | solution.py:18
  30.5 3.3 %shard_map.97 = (bf16[128,1024]{1,0:T(8,128)(2,1)S(1)}, f32[128,1024]{1,0:T(8,128)S(1)}, f32[128,1]{1,0:T(8,128)S(1)}, bf16[64,1152]{1,0:T(8,128)(2,1)S(1)}, bf1...) custom-call(s32[3]{0:T(128)S(1)} %pad_add_fusion.1.where, f32[128,1024]{1,0:T(8,128)S(1)} %get-tuple-element.87.refs_0_, ...), custom_call_target="tpu_custom_call" | custom-call | tf_op jit(solution)/shard_map/pallas_call | solution.py:422
  34.8 3.6 %shard_map.99.given = f32[128,2048]{1,0:T(8,128)S(1)} custom-call(s32[3]{0:T(128)S(1)} %pad_add_fusion.1.where, bf16[128,1024]{1,0:T(8,128)(2,1)S(1)} %convolution_convert_fusion.refs_4_.rows, bf16[1024,1024]{1,0:T(8,128)(2,1)} %bitcast.12.value_a, bf16[1024,1024]{1,0:T(8,128)(2,1)} %collective-permute-done.9.value_b, ...), custom_call_target="tpu_custom_call" | custom-call | tf_op jit(solution)/shard_map/pallas_call | solution.py:432
  40.8 3.2 %collective-permute-done.11.refs_2_ = bf16[64,1152]{1,0:T(8,128)(2,1)S(1)} collective-permute-done((bf16[64,1152]{1,0:T(8,128)(2,1)S(1)}, bf16[64,1152]{1,0:T(8,128)(2,1)S(1)}, u32[]{:S(2)}, u32[]{:S(2)}) %collective-permute-start.11) | collective-permute-done | bytes 147488 | tf_op jit(solution)/shard_map/ppermute | solution.py:18
  44.0 3.7 %shard_map.100 = (bf16[128,1024]{1,0:T(8,128)(2,1)S(1)}, f32[128,1]{1,0:T(8,128)S(1)}, bf16[512,1024]{1,0:T(8,128)(2,1)}) custom-call(s32[3]{0:T(128)S(1)} %pad_add_fusion.1.where, f32[128,1024]{1,0:T(8,128)S(1)} %get-tuple-element.105.refs_0_, f32[128,1]{1,0:T(8,128)S(1)} %get-tuple-element.106.refs_1_, ...), custom_call_target="tpu_custom_call" | custom-call | tf_op jit(solution)/shard_map/pallas_call | solution.py:446
  47.7 4.8 %all-to-all-start.1 = ((bf16[4,128,1024]{2,1,0:T(8,128)(2,1)}), bf16[4,128,1024]{2,1,0:T(8,128)(2,1)}, u32[]{:S(2)}, u32[]{:S(2)}) async-start(bf16[4,128,1024]{2,1,0:T(8,128)(2,1)} %bitcast.40), calls=%async_computation.1 | async-start | bytes 2097152 | tf_op jit(solution)/shard_map/all_to_all | solution.py:462
  52.5 4.4 %shard_map.101 = (f32[32,2048]{1,0:T(8,128)S(1)}, f32[32,1]{1,0:T(8,128)S(1)}, f32[32,1]{1,0:T(8,128)S(1)}, bf16[32,2176]{1,0:T(8,128)(2,1)}, bf16[32,2176]{1,0:T(8,128)(2,1)}, /*index=5*/bf16[32,2176]{1,0:T(8,128)(2,1)}) custom-call(s32[3]{0:T(128)S(1)} %pad_add_fusion.1.where, bf16[128,1024]{1,0:T(8,128)(2,1)S(1)} %get-tuple-element.118.scored, ...), custom_call_target="tpu_custom_call" | custom-call | tf_op jit(solution)/shard_map/pallas_call | solution.py:463
  59.7 1.9 %collective-permute-done.13.refs_0_ = bf16[32,2176]{1,0:T(8,128)(2,1)S(1)} collective-permute-done((bf16[32,2176]{1,0:T(8,128)(2,1)}, bf16[32,2176]{1,0:T(8,128)(2,1)S(1)}, u32[]{:S(2)}, u32[]{:S(2)}) %collective-permute-start.13) | collective-permute-done | bytes 139296 | tf_op jit(solution)/shard_map/ppermute | solution.py:18
  64.4 1.7 %collective-permute-start.17 = (bf16[32,1408]{1,0:T(8,128)(2,1)S(1)}, bf16[32,1408]{1,0:T(8,128)(2,1)S(1)}, u32[]{:S(2)}, u32[]{:S(2)}) collective-permute-start(bf16[32,1408]{1,0:T(8,128)(2,1)S(1)} %get-tuple-element.132), channel_id=1, source_target_pairs={{0,8},{4,12},{8,0},{12,4},{1,9},{5,13},{9,1},{13,5},{2,10},{6,14},... | collective-permute-start | bytes 270344 | tf_op jit(solution)/shard_map/ppermute | solution.py:18
  68.6 9.2 %collective-permute-start.25 = (bf16[512,256]{1,0:T(8,128)(2,1)S(1)}, bf16[512,256]{1,0:T(8,128)(2,1)S(1)}, u32[]{:S(2)}, u32[]{:S(2)}) collective-permute-start(bf16[512,256]{1,0:T(8,128)(2,1)S(1)} %get-tuple-element.143), channel_id=1, source_target_pairs={{0,16},{16,0},{1,17},{17,1},{2,18},{18,2},{3,19},{19,3},{4,20},{20... | collective-permute-start | bytes 786440 | tf_op jit(solution)/shard_map/ppermute | solution.py:18
  77.7 4.1 %collective-permute-done.18 = bf16[32,1408]{1,0:T(8,128)(2,1)S(1)} collective-permute-done((bf16[32,1408]{1,0:T(8,128)(2,1)S(1)}, bf16[32,1408]{1,0:T(8,128)(2,1)S(1)}, u32[]{:S(2)}, u32[]{:S(2)}) %collective-permute-start.18) | collective-permute-done | bytes 90144 | tf_op jit(solution)/shard_map/ppermute | solution.py:18
  81.9 1.5 %collective-permute-start.22 = (bf16[32,4224]{1,0:T(8,128)(2,1)S(1)}, bf16[32,4224]{1,0:T(8,128)(2,1)S(1)}, u32[]{:S(2)}, u32[]{:S(2)}) collective-permute-start(bf16[32,4224]{1,0:T(8,128)(2,1)S(1)} %constant_dynamic-update-slice_fusion.refs_4_), channel_id=1, source_target_pairs={{0,1},{1,0},{2,3},{3,2},{4,5},{5,4},{6,7},{7,6},{8,9},{9,8},{10,11... | collective-permute-start | bytes 811016 | tf_op jit(solution)/shard_map/ppermute | solution.py:18
  83.4 1.3 %collective-permute-start.24 = (bf16[32,4224]{1,0:T(8,128)(2,1)S(1)}, bf16[32,4224]{1,0:T(8,128)(2,1)S(1)}, u32[]{:S(2)}, u32[]{:S(2)}) collective-permute-start(bf16[32,4224]{1,0:T(8,128)(2,1)S(1)} %constant_dynamic-update-slice_fusion.refs_4_), channel_id=1, source_target_pairs={{0,3},{1,2},{2,1},{3,0},{4,7},{5,6},{6,5},{7,4},{8,11},{9,10},{10,... | collective-permute-start | bytes 811016 | tf_op jit(solution)/shard_map/ppermute | solution.py:18
  86.9 6.7 %collective-permute-done.21.refs_3_ = bf16[32,1408]{1,0:T(8,128)(2,1)S(1)} collective-permute-done((bf16[32,1408]{1,0:T(8,128)(2,1)S(1)}, bf16[32,1408]{1,0:T(8,128)(2,1)S(1)}, u32[]{:S(2)}, u32[]{:S(2)}) %collective-permute-start.21) | collective-permute-done | bytes 90144 | tf_op jit(solution)/shard_map/ppermute | solution.py:18
  94.1 5.4 %shard_map.104 = (bf16[256,1024]{1,0:T(8,128)(2,1)S(1)}, bf16[256,1024]{1,0:T(8,128)(2,1)S(1)}) custom-call(s32[3]{0:T(128)S(1)} %pad_add_fusion.where, bf16[32,1408]{1,0:T(8,128)(2,1)S(1)} %get-tuple-element.138.refs_0_, bf16[32,1408]{1,0:T(8,128)(2,1)S(1)} %collective-permute-done.19.refs_1_, bf16[32,1408]{1,0:T(8,128)(2,1)S(1)} %collective-permute-done.20.refs_2_, ...), custom_call_target="tpu_custom_call" | custom-call | tf_op jit(solution)/shard_map/pallas_call | solution.py:548
  99.6 6.0 %collective-permute-start.26 = (bf16[256,1024]{1,0:T(8,128)(2,1)S(1)}, bf16[256,1024]{1,0:T(8,128)(2,1)S(1)}, u32[]{:S(2)}, u32[]{:S(2)}) collective-permute-start(bf16[256,1024]{1,0:T(8,128)(2,1)S(1)} %get-tuple-element.146), channel_id=1, source_target_pairs={{0,16},{16,0},{1,17},{17,1},{2,18},{18,2},{3,19},{19,3},{4,20},{20... | collective-permute-start | bytes 1572872 | tf_op jit(solution)/shard_map/ppermute | solution.py:18
  105.6 5.4 %shard_map.103 = (f32[256,1024]{1,0:T(8,128)S(1)}, f32[256,1024]{1,0:T(8,128)S(1)}) custom-call(s32[3]{0:T(128)S(1)} %pad_add_fusion.where, bf16[32,1408]{1,0:T(8,128)(2,1)S(1)} %get-tuple-element.138.refs_0_, bf16[32,1408]{1,0:T(8,128)(2,1)S(1)} %collective-permute-done.19.refs_1_, bf16[32,1408]{1,0:T(8,128)(2,1)S(1)} %collective-permute-done.20.refs_2_, ...), custom_call_target="tpu_custom_call" | custom-call | tf_op jit(solution)/shard_map/pallas_call | solution.py:548
  111.1 1.5 %shard_map.105 = (f32[256,1024]{1,0:T(8,128)}, f32[256,1024]{1,0:T(8,128)}) custom-call(f32[256,1024]{1,0:T(8,128)S(1)} %get-tuple-element.144.value_near, f32[256,1024]{1,0:T(8,128)S(1)} %get-tuple-element.145.out_near, bf16[256,1024]{1,0:T(8,128)(2,1)S(1)} %collective-permute-done.26.value_far, bf16[256,1024]{1,0:T(8,128)(2,1)S(1)} %collective-permute-done.27.out_far), custom_call_target="tpu_custom_call" | custom-call | tf_op jit(solution)/shard_map/pallas_call | solution.py:587
  (71 shorter events, 19.9 us)
Async XLA Ops:
  0.6 4.9 %collective-permute-start = (bf16[1024,1024]{1,0:T(8,128)(2,1)}, bf16[1024,1024]{1,0:T(8,128)(2,1)}, u32[]{:S(2)}, u32[]{:S(2)}) collective-permute-start(bf16[1024,1024]{1,0:T(8,128)(2,1)} %bitcast.36), channel_id=1, source_target_pairs={{0,16},{16,0},{1,17},{17,1},{2,18},{18,2},{3,19},{19,3},{4,20},{20... | collective-permute-start | bytes 6291464 | tf_op jit(solution)/shard_map/ppermute | solution.py:18
  9.4 21.1 %collective-permute-start.6 = (bf16[1024,1024]{1,0:T(8,128)(2,1)}, bf16[1024,1024]{1,0:T(8,128)(2,1)}, u32[]{:S(2)}, u32[]{:S(2)}) collective-permute-start(bf16[1024,1024]{1,0:T(8,128)(2,1)} %bitcast.11.refs_5_.refs_6_), channel_id=1, source_target_pairs={{0,16},{16,0},{1,17},{17,1},{2,18},{18,2},{3,19},{19,3},{4,20},{20... | collective-permute-start | bytes 6291464 | tf_op jit(solution)/shard_map/ppermute | solution.py:18
  9.7 25.1 %collective-permute-start.9 = (bf16[1024,1024]{1,0:T(8,128)(2,1)}, bf16[1024,1024]{1,0:T(8,128)(2,1)}, u32[]{:S(2)}, u32[]{:S(2)}) collective-permute-start(bf16[1024,1024]{1,0:T(8,128)(2,1)} %bitcast.12.value_a), channel_id=1, source_target_pairs={{0,16},{16,0},{1,17},{17,1},{2,18},{18,2},{3,19},{19,3},{4,20},{20... | collective-permute-start | bytes 6291464 | tf_op jit(solution)/shard_map/ppermute | solution.py:18
  9.9 24.9 %collective-permute-start.10 = (bf16[1024,1024]{1,0:T(8,128)(2,1)}, bf16[1024,1024]{1,0:T(8,128)(2,1)}, u32[]{:S(2)}, u32[]{:S(2)}) collective-permute-start(bf16[1024,1024]{1,0:T(8,128)(2,1)} %bitcast.8.lout_a.refs_10_), channel_id=1, source_target_pairs={{0,16},{16,0},{1,17},{17,1},{2,18},{18,2},{3,19},{19,3},{4,20},{20... | collective-permute-start | bytes 6291464 | tf_op jit(solution)/shard_map/ppermute | solution.py:18
  10.2 37.4 %all-to-all-start = ((bf16[4,128,1152]{2,1,0:T(8,128)(2,1)}), bf16[4,128,1152]{2,1,0:T(8,128)(2,1)S(1)}, u32[]{:S(2)}, u32[]{:S(2)}) async-start(bf16[4,128,1152]{2,1,0:T(8,128)(2,1)} %bitcast.39), calls=%async_computation | async-start | bytes 2359296 | tf_op jit(solution)/shard_map/all_to_all | solution.py:409
  15.0 7.7 %collective-permute-start.2 = (bf16[64,2176]{1,0:T(8,128)(2,1)}, bf16[64,2176]{1,0:T(8,128)(2,1)S(1)}, u32[]{:S(2)}, u32[]{:S(2)}) collective-permute-start(bf16[64,2176]{1,0:T(8,128)(2,1)} %copy-done.2), channel_id=1, source_target_pairs={{0,1},{1,0},{2,3},{3,2},{4,5},{5,4},{6,7},{7,6},{8,9},{9,8},{10,11... | collective-permute-start | bytes 835592 | tf_op jit(solution)/shard_map/ppermute | solution.py:18
  15.3 7.4 %collective-permute-start.3 = (bf16[64,2176]{1,0:T(8,128)(2,1)S(1)}, bf16[64,2176]{1,0:T(8,128)(2,1)S(1)}, u32[]{:S(2)}, u32[]{:S(2)}) collective-permute-start(bf16[64,2176]{1,0:T(8,128)(2,1)S(1)} %get-tuple-element.83), channel_id=1, source_target_pairs={{0,2},{1,3},{2,0},{3,1},{4,6},{5,7},{6,4},{7,5},{8,10},{9,11},{10,... | collective-permute-start | bytes 835592 | tf_op jit(solution)/shard_map/ppermute | solution.py:18
  23.0 6.6 %collective-permute-start.4 = (bf16[64,2176]{1,0:T(8,128)(2,1)S(1)}, bf16[64,2176]{1,0:T(8,128)(2,1)S(1)}, u32[]{:S(2)}, u32[]{:S(2)}) collective-permute-start(bf16[64,2176]{1,0:T(8,128)(2,1)S(1)} %get-tuple-element.91), channel_id=1, source_target_pairs={{0,2},{1,3},{2,0},{3,1},{4,6},{5,7},{6,4},{7,5},{8,10},{9,11},{10,... | collective-permute-start | bytes 835592 | tf_op jit(solution)/shard_map/ppermute | solution.py:18
  24.3 6.2 %collective-permute-start.5 = (bf16[64,2176]{1,0:T(8,128)(2,1)S(1)}, bf16[64,2176]{1,0:T(8,128)(2,1)S(1)}, u32[]{:S(2)}, u32[]{:S(2)}) collective-permute-start(bf16[64,2176]{1,0:T(8,128)(2,1)S(1)} %get-tuple-element.92), channel_id=1, source_target_pairs={{0,1},{1,0},{2,3},{3,2},{4,5},{5,4},{6,7},{7,6},{8,9},{9,8},{10,11... | collective-permute-start | bytes 835592 | tf_op jit(solution)/shard_map/ppermute | solution.py:18
  38.8 5.2 %collective-permute-start.11 = (bf16[64,1152]{1,0:T(8,128)(2,1)S(1)}, bf16[64,1152]{1,0:T(8,128)(2,1)S(1)}, u32[]{:S(2)}, u32[]{:S(2)}) collective-permute-start(bf16[64,1152]{1,0:T(8,128)(2,1)S(1)} %get-tuple-element.113), channel_id=1, source_target_pairs={{0,2},{1,3},{2,0},{3,1},{4,6},{5,7},{6,4},{7,5},{8,10},{9,11},{10,... | collective-permute-start | bytes 442376 | tf_op jit(solution)/shard_map/ppermute | solution.py:18
  47.7 46.5 %all-to-all-start.1 = ((bf16[4,128,1024]{2,1,0:T(8,128)(2,1)}), bf16[4,128,1024]{2,1,0:T(8,128)(2,1)}, u32[]{:S(2)}, u32[]{:S(2)}) async-start(bf16[4,128,1024]{2,1,0:T(8,128)(2,1)} %bitcast.40), calls=%async_computation.1 | async-start | bytes 2097152 | tf_op jit(solution)/shard_map/all_to_all | solution.py:462
  58.5 5.0 %collective-permute-start.15 = (bf16[32,2176]{1,0:T(8,128)(2,1)}, bf16[32,2176]{1,0:T(8,128)(2,1)S(1)}, u32[]{:S(2)}, u32[]{:S(2)}) collective-permute-start(bf16[32,2176]{1,0:T(8,128)(2,1)} %get-tuple-element.127), channel_id=1, source_target_pairs={{0,3},{1,2},{2,1},{3,0},{4,7},{5,6},{6,5},{7,4},{8,11},{9,10},{10,... | collective-permute-start | bytes 417800 | tf_op jit(solution)/shard_map/ppermute | solution.py:18
  63.7 4.9 %collective-permute-start.16 = (bf16[32,1408]{1,0:T(8,128)(2,1)S(1)}, bf16[32,1408]{1,0:T(8,128)(2,1)S(1)}, u32[]{:S(2)}, u32[]{:S(2)}) collective-permute-start(bf16[32,1408]{1,0:T(8,128)(2,1)S(1)} %get-tuple-element.131), channel_id=1, source_target_pairs={{0,4},{4,0},{8,12},{12,8},{1,5},{5,1},{9,13},{13,9},{2,6},{6,2},{1... | collective-permute-start | bytes 270344 | tf_op jit(solution)/shard_map/ppermute | solution.py:18
  64.4 13.3 %collective-permute-start.17 = (bf16[32,1408]{1,0:T(8,128)(2,1)S(1)}, bf16[32,1408]{1,0:T(8,128)(2,1)S(1)}, u32[]{:S(2)}, u32[]{:S(2)}) collective-permute-start(bf16[32,1408]{1,0:T(8,128)(2,1)S(1)} %get-tuple-element.132), channel_id=1, source_target_pairs={{0,8},{4,12},{8,0},{12,4},{1,9},{5,13},{9,1},{13,5},{2,10},{6,14},... | collective-permute-start | bytes 270344 | tf_op jit(solution)/shard_map/ppermute | solution.py:18
  66.1 15.7 %collective-permute-start.18 = (bf16[32,1408]{1,0:T(8,128)(2,1)S(1)}, bf16[32,1408]{1,0:T(8,128)(2,1)S(1)}, u32[]{:S(2)}, u32[]{:S(2)}) collective-permute-start(bf16[32,1408]{1,0:T(8,128)(2,1)S(1)} %get-tuple-element.133), channel_id=1, source_target_pairs={{0,12},{4,8},{8,4},{12,0},{1,13},{5,9},{9,5},{13,1},{2,14},{6,10},... | collective-permute-start | bytes 270344 | tf_op jit(solution)/shard_map/ppermute | solution.py:18
  66.4 15.5 %collective-permute-start.19 = (bf16[32,1408]{1,0:T(8,128)(2,1)S(1)}, bf16[32,1408]{1,0:T(8,128)(2,1)S(1)}, u32[]{:S(2)}, u32[]{:S(2)}) collective-permute-start(bf16[32,1408]{1,0:T(8,128)(2,1)S(1)} %get-tuple-element.138.refs_0_), channel_id=1, source_target_pairs={{0,1},{1,0},{2,3},{3,2},{4,5},{5,4},{6,7},{7,6},{8,9},{9,8},{10,11... | collective-permute-start | bytes 270344 | tf_op jit(solution)/shard_map/ppermute | solution.py:18
  67.2 14.7 %collective-permute-start.20 = (bf16[32,1408]{1,0:T(8,128)(2,1)S(1)}, bf16[32,1408]{1,0:T(8,128)(2,1)S(1)}, u32[]{:S(2)}, u32[]{:S(2)}) collective-permute-start(bf16[32,1408]{1,0:T(8,128)(2,1)S(1)} %get-tuple-element.138.refs_0_), channel_id=1, source_target_pairs={{0,2},{1,3},{2,0},{3,1},{4,6},{5,7},{6,4},{7,5},{8,10},{9,11},{10,... | collective-permute-start | bytes 270344 | tf_op jit(solution)/shard_map/ppermute | solution.py:18
  68.6 17.3 %collective-permute-start.25 = (bf16[512,256]{1,0:T(8,128)(2,1)S(1)}, bf16[512,256]{1,0:T(8,128)(2,1)S(1)}, u32[]{:S(2)}, u32[]{:S(2)}) collective-permute-start(bf16[512,256]{1,0:T(8,128)(2,1)S(1)} %get-tuple-element.143), channel_id=1, source_target_pairs={{0,16},{16,0},{1,17},{17,1},{2,18},{18,2},{3,19},{19,3},{4,20},{20... | collective-permute-start | bytes 786440 | tf_op jit(solution)/shard_map/ppermute | solution.py:18
  81.9 11.7 %collective-permute-start.22 = (bf16[32,4224]{1,0:T(8,128)(2,1)S(1)}, bf16[32,4224]{1,0:T(8,128)(2,1)S(1)}, u32[]{:S(2)}, u32[]{:S(2)}) collective-permute-start(bf16[32,4224]{1,0:T(8,128)(2,1)S(1)} %constant_dynamic-update-slice_fusion.refs_4_), channel_id=1, source_target_pairs={{0,1},{1,0},{2,3},{3,2},{4,5},{5,4},{6,7},{7,6},{8,9},{9,8},{10,11... | collective-permute-start | bytes 811016 | tf_op jit(solution)/shard_map/ppermute | solution.py:18
  83.4 10.7 %collective-permute-start.23 = (bf16[32,4224]{1,0:T(8,128)(2,1)S(1)}, bf16[32,4224]{1,0:T(8,128)(2,1)S(1)}, u32[]{:S(2)}, u32[]{:S(2)}) collective-permute-start(bf16[32,4224]{1,0:T(8,128)(2,1)S(1)} %constant_dynamic-update-slice_fusion.refs_4_), channel_id=1, source_target_pairs={{0,2},{1,3},{2,0},{3,1},{4,6},{5,7},{6,4},{7,5},{8,10},{9,11},{10,... | collective-permute-start | bytes 811016 | tf_op jit(solution)/shard_map/ppermute | solution.py:18
  83.4 10.7 %collective-permute-start.24 = (bf16[32,4224]{1,0:T(8,128)(2,1)S(1)}, bf16[32,4224]{1,0:T(8,128)(2,1)S(1)}, u32[]{:S(2)}, u32[]{:S(2)}) collective-permute-start(bf16[32,4224]{1,0:T(8,128)(2,1)S(1)} %constant_dynamic-update-slice_fusion.refs_4_), channel_id=1, source_target_pairs={{0,3},{1,2},{2,1},{3,0},{4,7},{5,6},{6,5},{7,4},{8,11},{9,10},{10,... | collective-permute-start | bytes 811016 | tf_op jit(solution)/shard_map/ppermute | solution.py:18
  84.7 8.9 %collective-permute-start.21 = (bf16[32,1408]{1,0:T(8,128)(2,1)S(1)}, bf16[32,1408]{1,0:T(8,128)(2,1)S(1)}, u32[]{:S(2)}, u32[]{:S(2)}) collective-permute-start(bf16[32,1408]{1,0:T(8,128)(2,1)S(1)} %get-tuple-element.138.refs_0_), channel_id=1, source_target_pairs={{0,3},{1,2},{2,1},{3,0},{4,7},{5,6},{6,5},{7,4},{8,11},{9,10},{10,... | collective-permute-start | bytes 270344 | tf_op jit(solution)/shard_map/ppermute | solution.py:18
  99.6 11.5 %collective-permute-start.26 = (bf16[256,1024]{1,0:T(8,128)(2,1)S(1)}, bf16[256,1024]{1,0:T(8,128)(2,1)S(1)}, u32[]{:S(2)}, u32[]{:S(2)}) collective-permute-start(bf16[256,1024]{1,0:T(8,128)(2,1)S(1)} %get-tuple-element.146), channel_id=1, source_target_pairs={{0,16},{16,0},{1,17},{17,1},{2,18},{18,2},{3,19},{19,3},{4,20},{20... | collective-permute-start | bytes 1572872 | tf_op jit(solution)/shard_map/ppermute | solution.py:18
  105.5 5.5 %collective-permute-start.27 = (bf16[256,1024]{1,0:T(8,128)(2,1)S(1)}, bf16[256,1024]{1,0:T(8,128)(2,1)S(1)}, u32[]{:S(2)}, u32[]{:S(2)}) collective-permute-start(bf16[256,1024]{1,0:T(8,128)(2,1)S(1)} %get-tuple-element.147), channel_id=1, source_target_pairs={{0,16},{16,0},{1,17},{17,1},{2,18},{18,2},{3,19},{19,3},{4,20},{20... | collective-permute-start | bytes 1572872 | tf_op jit(solution)/shard_map/ppermute | solution.py:18
  (11 other events, 44.4 us)

commit v8 on v7

--- a/solution.py
+++ b/solution.py
@@ -201,11 +201,11 @@
 def share_kernel(share, where, scored, norm, given, value_a, value_b, lout_a, lout_b, *refs):
     every_row, kept, kept_norm, kept_count = refs[:4]
     peers, (value, lout, part, sent, goals, sems) = refs[4:-6], refs[-6:]
-    sides = every_row.at[:, pl.ds(scored.shape[1], SIDE)]
-    goal_copy = start_copy(sides, goals, sems.at[sems.shape[0] - 1])
     first, at = where[0] == 1, where[1]
     fetch(first, value_b, value_a, value, sems.at[0])
     fetch(first, lout_b, lout_a, lout, sems.at[1])
+    sides = every_row.at[:, pl.ds(scored.shape[1], SIDE)]
+    goal_copy = start_copy(sides, goals, sems.at[sems.shape[0] - 1])
     inner = value.shape[1]
     score = scored[...]
     sent[:, 2 * inner :] = side_of(norm[...])

time: 113 us -> 113 us (level)
  no operation moved by 1% of the time
where the time goes in v8:
time: 113 us
  starting transfers between devices  44 us (39%)
  Pallas kernels  31.1 us (28%)
  waiting for transfers between devices  30.9 us (27%)
  matrix products  2.79 us (2%)
  between operations  1.54 us (1%)
  other arithmetic  1.21 us (1%)
    ppermute x28, starting transfers between devices, flip(): return lax.ppermute(value, axis, pairs)  34.4 us
    ppermute x28, waiting for transfers between devices, flip(): return lax.ppermute(value, axis, pairs)  30.9 us
    pallas_call x2, Pallas kernels, gradients(): call(functools.partial(gradient_kernel, share, mp_size, aways, spots, oth...  10.8 us
    all_to_all x1, starting transfers between devices, on_device(): every_scored = lax.all_to_all(repeated, 'dp', 0, 0, tiled=True)  4.84 us
    all_to_all x1, starting transfers between devices, on_device(): every_row = lax.all_to_all(repeated, 'dp', 0, 0, tiled=True)  4.76 us
    pallas_call x1, Pallas kernels, on_device(): call(functools.partial(share_kernel, share), [jax.ShapeDtypeStruct((share...  4.39 us
    pallas_call x1, Pallas kernels, on_device(): call(functools.partial(score_kernel, scorer_width), [hidden_type, sums[1]...  3.7 us
    pallas_call x1, Pallas kernels, on_device(): call(learn_kernel, [jax.ShapeDtypeStruct((keep, 2 * inner), F32)], [SMEM,...  3.61 us
  transfers between devices with their start and end apart: 30, of which 13 were waited for; matrix products, arithmetic and copies ran while one was open for 4% of the time, Pallas kernels for 19%

profile of v8, /device:TPU:11, one launch (start us, length us, event | category | flops | bytes accessed | tf_op | source)
XLA Modules:
  0.0 112.5 jit_solution(10028584706859056385)
XLA Ops:
  1.4 2.5 %fusion = f32[256,1024]{0,1:T(8,128)S(1)} fusion(bf16[1,1024,1024]{2,1,0:T(8,128)(2,1)} %param.12, s32[]{:T(128)S(6)} %select_n.26), kind=kOutput, calls=%fused_computation.2 | convolution fusion | flops 536870912 | bytes 3670020 | tf_op jit(solution)/shard_map/dot_general | solution.py:26
  5.6 3.1 %shard_map.95 = (f32[128,1024]{1,0:T(8,128)S(1)}, f32[128,1]{1,0:T(8,128)S(1)}, bf16[64,2176]{1,0:T(8,128)(2,1)S(1)}, bf16[64,2176]{1,0:T(8,128)(2,1)S(1)}, f32[...) custom-call(s32[3]{0:T(128)S(1)} %pad_add_fusion.1.where, bf16[128,1152]{1,0:T(8,128)(2,1)S(1)} %pad_maximum_fusion.rows, ...), custom_call_target="tpu_custom_call" | custom-call | tf_op jit(solution)/shard_map/pallas_call | solution.py:395
  10.2 4.8 %all-to-all-start = ((bf16[4,128,1152]{2,1,0:T(8,128)(2,1)}), bf16[4,128,1152]{2,1,0:T(8,128)(2,1)S(1)}, u32[]{:S(2)}, u32[]{:S(2)}) async-start(bf16[4,128,1152]{2,1,0:T(8,128)(2,1)} %bitcast.39), calls=%async_computation | async-start | bytes 2359296 | tf_op jit(solution)/shard_map/all_to_all | solution.py:409
  15.3 1.2 %collective-permute-start.3 = (bf16[64,2176]{1,0:T(8,128)(2,1)S(1)}, bf16[64,2176]{1,0:T(8,128)(2,1)S(1)}, u32[]{:S(2)}, u32[]{:S(2)}) collective-permute-start(bf16[64,2176]{1,0:T(8,128)(2,1)S(1)} %get-tuple-element.83), channel_id=1, source_target_pairs={{0,2},{1,3},{2,0},{3,1},{4,6},{5,7},{6,4},{7,5},{8,10},{9,11},{10,... | collective-permute-start | bytes 835592 | tf_op jit(solution)/shard_map/ppermute | solution.py:18
  16.5 6.2 %collective-permute-done.2.got_top = bf16[64,2176]{1,0:T(8,128)(2,1)S(1)} collective-permute-done((bf16[64,2176]{1,0:T(8,128)(2,1)}, bf16[64,2176]{1,0:T(8,128)(2,1)S(1)}, u32[]{:S(2)}, u32[]{:S(2)}) %collective-permute-start.2) | collective-permute-done | bytes 278560 | tf_op jit(solution)/shard_map/ppermute | solution.py:18
  23.0 1.3 %collective-permute-start.4 = (bf16[64,2176]{1,0:T(8,128)(2,1)S(1)}, bf16[64,2176]{1,0:T(8,128)(2,1)S(1)}, u32[]{:S(2)}, u32[]{:S(2)}) collective-permute-start(bf16[64,2176]{1,0:T(8,128)(2,1)S(1)} %get-tuple-element.91), channel_id=1, source_target_pairs={{0,2},{1,3},{2,0},{3,1},{4,6},{5,7},{6,4},{7,5},{8,10},{9,11},{10,... | collective-permute-start | bytes 835592 | tf_op jit(solution)/shard_map/ppermute | solution.py:18
  25.2 4.3 %collective-permute-done.4.refs_2_ = bf16[64,2176]{1,0:T(8,128)(2,1)S(1)} collective-permute-done((bf16[64,2176]{1,0:T(8,128)(2,1)S(1)}, bf16[64,2176]{1,0:T(8,128)(2,1)S(1)}, u32[]{:S(2)}, u32[]{:S(2)}) %collective-permute-start.4) | collective-permute-done | bytes 278560 | tf_op jit(solution)/shard_map/ppermute | solution.py:18
  30.5 3.3 %shard_map.97 = (bf16[128,1024]{1,0:T(8,128)(2,1)S(1)}, f32[128,1024]{1,0:T(8,128)S(1)}, f32[128,1]{1,0:T(8,128)S(1)}, bf16[64,1152]{1,0:T(8,128)(2,1)S(1)}, bf1...) custom-call(s32[3]{0:T(128)S(1)} %pad_add_fusion.1.where, f32[128,1024]{1,0:T(8,128)S(1)} %get-tuple-element.87.refs_0_, ...), custom_call_target="tpu_custom_call" | custom-call | tf_op jit(solution)/shard_map/pallas_call | solution.py:422
  34.8 3.6 %shard_map.99.given = f32[128,2048]{1,0:T(8,128)S(1)} custom-call(s32[3]{0:T(128)S(1)} %pad_add_fusion.1.where, bf16[128,1024]{1,0:T(8,128)(2,1)S(1)} %convolution_convert_fusion.refs_4_.rows, bf16[1024,1024]{1,0:T(8,128)(2,1)} %bitcast.12.value_a, bf16[1024,1024]{1,0:T(8,128)(2,1)} %collective-permute-done.9.value_b, ...), custom_call_target="tpu_custom_call" | custom-call | tf_op jit(solution)/shard_map/pallas_call | solution.py:432
  40.8 3.2 %collective-permute-done.11.refs_2_ = bf16[64,1152]{1,0:T(8,128)(2,1)S(1)} collective-permute-done((bf16[64,1152]{1,0:T(8,128)(2,1)S(1)}, bf16[64,1152]{1,0:T(8,128)(2,1)S(1)}, u32[]{:S(2)}, u32[]{:S(2)}) %collective-permute-start.11) | collective-permute-done | bytes 147488 | tf_op jit(solution)/shard_map/ppermute | solution.py:18
  44.0 3.7 %shard_map.100 = (bf16[128,1024]{1,0:T(8,128)(2,1)S(1)}, f32[128,1]{1,0:T(8,128)S(1)}, bf16[512,1024]{1,0:T(8,128)(2,1)}) custom-call(s32[3]{0:T(128)S(1)} %pad_add_fusion.1.where, f32[128,1024]{1,0:T(8,128)S(1)} %get-tuple-element.105.refs_0_, f32[128,1]{1,0:T(8,128)S(1)} %get-tuple-element.106.refs_1_, ...), custom_call_target="tpu_custom_call" | custom-call | tf_op jit(solution)/shard_map/pallas_call | solution.py:446
  47.7 4.8 %all-to-all-start.1 = ((bf16[4,128,1024]{2,1,0:T(8,128)(2,1)}), bf16[4,128,1024]{2,1,0:T(8,128)(2,1)}, u32[]{:S(2)}, u32[]{:S(2)}) async-start(bf16[4,128,1024]{2,1,0:T(8,128)(2,1)} %bitcast.40), calls=%async_computation.1 | async-start | bytes 2097152 | tf_op jit(solution)/shard_map/all_to_all | solution.py:462
  52.5 4.4 %shard_map.101 = (f32[32,2048]{1,0:T(8,128)S(1)}, f32[32,1]{1,0:T(8,128)S(1)}, f32[32,1]{1,0:T(8,128)S(1)}, bf16[32,2176]{1,0:T(8,128)(2,1)}, bf16[32,2176]{1,0:T(8,128)(2,1)}, /*index=5*/bf16[32,2176]{1,0:T(8,128)(2,1)}) custom-call(s32[3]{0:T(128)S(1)} %pad_add_fusion.1.where, bf16[128,1024]{1,0:T(8,128)(2,1)S(1)} %get-tuple-element.118.scored, ...), custom_call_target="tpu_custom_call" | custom-call | tf_op jit(solution)/shard_map/pallas_call | solution.py:463
  59.6 1.9 %collective-permute-done.13.refs_0_ = bf16[32,2176]{1,0:T(8,128)(2,1)S(1)} collective-permute-done((bf16[32,2176]{1,0:T(8,128)(2,1)}, bf16[32,2176]{1,0:T(8,128)(2,1)S(1)}, u32[]{:S(2)}, u32[]{:S(2)}) %collective-permute-start.13) | collective-permute-done | bytes 139296 | tf_op jit(solution)/shard_map/ppermute | solution.py:18
  64.4 1.7 %collective-permute-start.17 = (bf16[32,1408]{1,0:T(8,128)(2,1)S(1)}, bf16[32,1408]{1,0:T(8,128)(2,1)S(1)}, u32[]{:S(2)}, u32[]{:S(2)}) collective-permute-start(bf16[32,1408]{1,0:T(8,128)(2,1)S(1)} %get-tuple-element.132), channel_id=1, source_target_pairs={{0,8},{4,12},{8,0},{12,4},{1,9},{5,13},{9,1},{13,5},{2,10},{6,14},... | collective-permute-start | bytes 270344 | tf_op jit(solution)/shard_map/ppermute | solution.py:18
  68.6 9.2 %collective-permute-start.25 = (bf16[512,256]{1,0:T(8,128)(2,1)S(1)}, bf16[512,256]{1,0:T(8,128)(2,1)S(1)}, u32[]{:S(2)}, u32[]{:S(2)}) collective-permute-start(bf16[512,256]{1,0:T(8,128)(2,1)S(1)} %get-tuple-element.143), channel_id=1, source_target_pairs={{0,16},{16,0},{1,17},{17,1},{2,18},{18,2},{3,19},{19,3},{4,20},{20... | collective-permute-start | bytes 786440 | tf_op jit(solution)/shard_map/ppermute | solution.py:18
  77.7 4.2 %collective-permute-done.18 = bf16[32,1408]{1,0:T(8,128)(2,1)S(1)} collective-permute-done((bf16[32,1408]{1,0:T(8,128)(2,1)S(1)}, bf16[32,1408]{1,0:T(8,128)(2,1)S(1)}, u32[]{:S(2)}, u32[]{:S(2)}) %collective-permute-start.18) | collective-permute-done | bytes 90144 | tf_op jit(solution)/shard_map/ppermute | solution.py:18
  81.9 1.5 %collective-permute-start.22 = (bf16[32,4224]{1,0:T(8,128)(2,1)S(1)}, bf16[32,4224]{1,0:T(8,128)(2,1)S(1)}, u32[]{:S(2)}, u32[]{:S(2)}) collective-permute-start(bf16[32,4224]{1,0:T(8,128)(2,1)S(1)} %constant_dynamic-update-slice_fusion.refs_4_), channel_id=1, source_target_pairs={{0,1},{1,0},{2,3},{3,2},{4,5},{5,4},{6,7},{7,6},{8,9},{9,8},{10,11... | collective-permute-start | bytes 811016 | tf_op jit(solution)/shard_map/ppermute | solution.py:18
  83.4 1.3 %collective-permute-start.24 = (bf16[32,4224]{1,0:T(8,128)(2,1)S(1)}, bf16[32,4224]{1,0:T(8,128)(2,1)S(1)}, u32[]{:S(2)}, u32[]{:S(2)}) collective-permute-start(bf16[32,4224]{1,0:T(8,128)(2,1)S(1)} %constant_dynamic-update-slice_fusion.refs_4_), channel_id=1, source_target_pairs={{0,3},{1,2},{2,1},{3,0},{4,7},{5,6},{6,5},{7,4},{8,11},{9,10},{10,... | collective-permute-start | bytes 811016 | tf_op jit(solution)/shard_map/ppermute | solution.py:18
  86.9 6.7 %collective-permute-done.21.refs_3_ = bf16[32,1408]{1,0:T(8,128)(2,1)S(1)} collective-permute-done((bf16[32,1408]{1,0:T(8,128)(2,1)S(1)}, bf16[32,1408]{1,0:T(8,128)(2,1)S(1)}, u32[]{:S(2)}, u32[]{:S(2)}) %collective-permute-start.21) | collective-permute-done | bytes 90144 | tf_op jit(solution)/shard_map/ppermute | solution.py:18
  94.1 5.4 %shard_map.104 = (bf16[256,1024]{1,0:T(8,128)(2,1)S(1)}, bf16[256,1024]{1,0:T(8,128)(2,1)S(1)}) custom-call(s32[3]{0:T(128)S(1)} %pad_add_fusion.where, bf16[32,1408]{1,0:T(8,128)(2,1)S(1)} %get-tuple-element.138.refs_0_, bf16[32,1408]{1,0:T(8,128)(2,1)S(1)} %collective-permute-done.19.refs_1_, bf16[32,1408]{1,0:T(8,128)(2,1)S(1)} %collective-permute-done.20.refs_2_, ...), custom_call_target="tpu_custom_call" | custom-call | tf_op jit(solution)/shard_map/pallas_call | solution.py:548
  99.6 6.0 %collective-permute-start.26 = (bf16[256,1024]{1,0:T(8,128)(2,1)S(1)}, bf16[256,1024]{1,0:T(8,128)(2,1)S(1)}, u32[]{:S(2)}, u32[]{:S(2)}) collective-permute-start(bf16[256,1024]{1,0:T(8,128)(2,1)S(1)} %get-tuple-element.146), channel_id=1, source_target_pairs={{0,16},{16,0},{1,17},{17,1},{2,18},{18,2},{3,19},{19,3},{4,20},{20... | collective-permute-start | bytes 1572872 | tf_op jit(solution)/shard_map/ppermute | solution.py:18
  105.6 5.4 %shard_map.103 = (f32[256,1024]{1,0:T(8,128)S(1)}, f32[256,1024]{1,0:T(8,128)S(1)}) custom-call(s32[3]{0:T(128)S(1)} %pad_add_fusion.where, bf16[32,1408]{1,0:T(8,128)(2,1)S(1)} %get-tuple-element.138.refs_0_, bf16[32,1408]{1,0:T(8,128)(2,1)S(1)} %collective-permute-done.19.refs_1_, bf16[32,1408]{1,0:T(8,128)(2,1)S(1)} %collective-permute-done.20.refs_2_, ...), custom_call_target="tpu_custom_call" | custom-call | tf_op jit(solution)/shard_map/pallas_call | solution.py:548
  111.1 1.5 %shard_map.105 = (f32[256,1024]{1,0:T(8,128)}, f32[256,1024]{1,0:T(8,128)}) custom-call(f32[256,1024]{1,0:T(8,128)S(1)} %get-tuple-element.144.value_near, f32[256,1024]{1,0:T(8,128)S(1)} %get-tuple-element.145.out_near, bf16[256,1024]{1,0:T(8,128)(2,1)S(1)} %collective-permute-done.26.value_far, bf16[256,1024]{1,0:T(8,128)(2,1)S(1)} %collective-permute-done.27.out_far), custom_call_target="tpu_custom_call" | custom-call | tf_op jit(solution)/shard_map/pallas_call | solution.py:587
  (71 shorter events, 19.9 us)
Async XLA Ops:
  0.6 4.9 %collective-permute-start = (bf16[1024,1024]{1,0:T(8,128)(2,1)}, bf16[1024,1024]{1,0:T(8,128)(2,1)}, u32[]{:S(2)}, u32[]{:S(2)}) collective-permute-start(bf16[1024,1024]{1,0:T(8,128)(2,1)} %bitcast.36), channel_id=1, source_target_pairs={{0,16},{16,0},{1,17},{17,1},{2,18},{18,2},{3,19},{19,3},{4,20},{20... | collective-permute-start | bytes 6291464 | tf_op jit(solution)/shard_map/ppermute | solution.py:18
  9.4 21.1 %collective-permute-start.6 = (bf16[1024,1024]{1,0:T(8,128)(2,1)}, bf16[1024,1024]{1,0:T(8,128)(2,1)}, u32[]{:S(2)}, u32[]{:S(2)}) collective-permute-start(bf16[1024,1024]{1,0:T(8,128)(2,1)} %bitcast.11.refs_5_.refs_6_), channel_id=1, source_target_pairs={{0,16},{16,0},{1,17},{17,1},{2,18},{18,2},{3,19},{19,3},{4,20},{20... | collective-permute-start | bytes 6291464 | tf_op jit(solution)/shard_map/ppermute | solution.py:18
  9.7 25.1 %collective-permute-start.9 = (bf16[1024,1024]{1,0:T(8,128)(2,1)}, bf16[1024,1024]{1,0:T(8,128)(2,1)}, u32[]{:S(2)}, u32[]{:S(2)}) collective-permute-start(bf16[1024,1024]{1,0:T(8,128)(2,1)} %bitcast.12.value_a), channel_id=1, source_target_pairs={{0,16},{16,0},{1,17},{17,1},{2,18},{18,2},{3,19},{19,3},{4,20},{20... | collective-permute-start | bytes 6291464 | tf_op jit(solution)/shard_map/ppermute | solution.py:18
  9.9 24.9 %collective-permute-start.10 = (bf16[1024,1024]{1,0:T(8,128)(2,1)}, bf16[1024,1024]{1,0:T(8,128)(2,1)}, u32[]{:S(2)}, u32[]{:S(2)}) collective-permute-start(bf16[1024,1024]{1,0:T(8,128)(2,1)} %bitcast.8.lout_a.refs_10_), channel_id=1, source_target_pairs={{0,16},{16,0},{1,17},{17,1},{2,18},{18,2},{3,19},{19,3},{4,20},{20... | collective-permute-start | bytes 6291464 | tf_op jit(solution)/shard_map/ppermute | solution.py:18
  10.2 37.4 %all-to-all-start = ((bf16[4,128,1152]{2,1,0:T(8,128)(2,1)}), bf16[4,128,1152]{2,1,0:T(8,128)(2,1)S(1)}, u32[]{:S(2)}, u32[]{:S(2)}) async-start(bf16[4,128,1152]{2,1,0:T(8,128)(2,1)} %bitcast.39), calls=%async_computation | async-start | bytes 2359296 | tf_op jit(solution)/shard_map/all_to_all | solution.py:409
  15.0 7.7 %collective-permute-start.2 = (bf16[64,2176]{1,0:T(8,128)(2,1)}, bf16[64,2176]{1,0:T(8,128)(2,1)S(1)}, u32[]{:S(2)}, u32[]{:S(2)}) collective-permute-start(bf16[64,2176]{1,0:T(8,128)(2,1)} %copy-done.2), channel_id=1, source_target_pairs={{0,1},{1,0},{2,3},{3,2},{4,5},{5,4},{6,7},{7,6},{8,9},{9,8},{10,11... | collective-permute-start | bytes 835592 | tf_op jit(solution)/shard_map/ppermute | solution.py:18
  15.3 7.4 %collective-permute-start.3 = (bf16[64,2176]{1,0:T(8,128)(2,1)S(1)}, bf16[64,2176]{1,0:T(8,128)(2,1)S(1)}, u32[]{:S(2)}, u32[]{:S(2)}) collective-permute-start(bf16[64,2176]{1,0:T(8,128)(2,1)S(1)} %get-tuple-element.83), channel_id=1, source_target_pairs={{0,2},{1,3},{2,0},{3,1},{4,6},{5,7},{6,4},{7,5},{8,10},{9,11},{10,... | collective-permute-start | bytes 835592 | tf_op jit(solution)/shard_map/ppermute | solution.py:18
  23.0 6.6 %collective-permute-start.4 = (bf16[64,2176]{1,0:T(8,128)(2,1)S(1)}, bf16[64,2176]{1,0:T(8,128)(2,1)S(1)}, u32[]{:S(2)}, u32[]{:S(2)}) collective-permute-start(bf16[64,2176]{1,0:T(8,128)(2,1)S(1)} %get-tuple-element.91), channel_id=1, source_target_pairs={{0,2},{1,3},{2,0},{3,1},{4,6},{5,7},{6,4},{7,5},{8,10},{9,11},{10,... | collective-permute-start | bytes 835592 | tf_op jit(solution)/shard_map/ppermute | solution.py:18
  24.3 6.2 %collective-permute-start.5 = (bf16[64,2176]{1,0:T(8,128)(2,1)S(1)}, bf16[64,2176]{1,0:T(8,128)(2,1)S(1)}, u32[]{:S(2)}, u32[]{:S(2)}) collective-permute-start(bf16[64,2176]{1,0:T(8,128)(2,1)S(1)} %get-tuple-element.92), channel_id=1, source_target_pairs={{0,1},{1,0},{2,3},{3,2},{4,5},{5,4},{6,7},{7,6},{8,9},{9,8},{10,11... | collective-permute-start | bytes 835592 | tf_op jit(solution)/shard_map/ppermute | solution.py:18
  38.8 5.2 %collective-permute-start.11 = (bf16[64,1152]{1,0:T(8,128)(2,1)S(1)}, bf16[64,1152]{1,0:T(8,128)(2,1)S(1)}, u32[]{:S(2)}, u32[]{:S(2)}) collective-permute-start(bf16[64,1152]{1,0:T(8,128)(2,1)S(1)} %get-tuple-element.113), channel_id=1, source_target_pairs={{0,2},{1,3},{2,0},{3,1},{4,6},{5,7},{6,4},{7,5},{8,10},{9,11},{10,... | collective-permute-start | bytes 442376 | tf_op jit(solution)/shard_map/ppermute | solution.py:18
  47.7 46.5 %all-to-all-start.1 = ((bf16[4,128,1024]{2,1,0:T(8,128)(2,1)}), bf16[4,128,1024]{2,1,0:T(8,128)(2,1)}, u32[]{:S(2)}, u32[]{:S(2)}) async-start(bf16[4,128,1024]{2,1,0:T(8,128)(2,1)} %bitcast.40), calls=%async_computation.1 | async-start | bytes 2097152 | tf_op jit(solution)/shard_map/all_to_all | solution.py:462
  58.4 5.0 %collective-permute-start.15 = (bf16[32,2176]{1,0:T(8,128)(2,1)}, bf16[32,2176]{1,0:T(8,128)(2,1)S(1)}, u32[]{:S(2)}, u32[]{:S(2)}) collective-permute-start(bf16[32,2176]{1,0:T(8,128)(2,1)} %get-tuple-element.127), channel_id=1, source_target_pairs={{0,3},{1,2},{2,1},{3,0},{4,7},{5,6},{6,5},{7,4},{8,11},{9,10},{10,... | collective-permute-start | bytes 417800 | tf_op jit(solution)/shard_map/ppermute | solution.py:18
  63.7 4.9 %collective-permute-start.16 = (bf16[32,1408]{1,0:T(8,128)(2,1)S(1)}, bf16[32,1408]{1,0:T(8,128)(2,1)S(1)}, u32[]{:S(2)}, u32[]{:S(2)}) collective-permute-start(bf16[32,1408]{1,0:T(8,128)(2,1)S(1)} %get-tuple-element.131), channel_id=1, source_target_pairs={{0,4},{4,0},{8,12},{12,8},{1,5},{5,1},{9,13},{13,9},{2,6},{6,2},{1... | collective-permute-start | bytes 270344 | tf_op jit(solution)/shard_map/ppermute | solution.py:18
  64.4 13.3 %collective-permute-start.17 = (bf16[32,1408]{1,0:T(8,128)(2,1)S(1)}, bf16[32,1408]{1,0:T(8,128)(2,1)S(1)}, u32[]{:S(2)}, u32[]{:S(2)}) collective-permute-start(bf16[32,1408]{1,0:T(8,128)(2,1)S(1)} %get-tuple-element.132), channel_id=1, source_target_pairs={{0,8},{4,12},{8,0},{12,4},{1,9},{5,13},{9,1},{13,5},{2,10},{6,14},... | collective-permute-start | bytes 270344 | tf_op jit(solution)/shard_map/ppermute | solution.py:18
  66.1 15.8 %collective-permute-start.18 = (bf16[32,1408]{1,0:T(8,128)(2,1)S(1)}, bf16[32,1408]{1,0:T(8,128)(2,1)S(1)}, u32[]{:S(2)}, u32[]{:S(2)}) collective-permute-start(bf16[32,1408]{1,0:T(8,128)(2,1)S(1)} %get-tuple-element.133), channel_id=1, source_target_pairs={{0,12},{4,8},{8,4},{12,0},{1,13},{5,9},{9,5},{13,1},{2,14},{6,10},... | collective-permute-start | bytes 270344 | tf_op jit(solution)/shard_map/ppermute | solution.py:18
  66.4 15.5 %collective-permute-start.19 = (bf16[32,1408]{1,0:T(8,128)(2,1)S(1)}, bf16[32,1408]{1,0:T(8,128)(2,1)S(1)}, u32[]{:S(2)}, u32[]{:S(2)}) collective-permute-start(bf16[32,1408]{1,0:T(8,128)(2,1)S(1)} %get-tuple-element.138.refs_0_), channel_id=1, source_target_pairs={{0,1},{1,0},{2,3},{3,2},{4,5},{5,4},{6,7},{7,6},{8,9},{9,8},{10,11... | collective-permute-start | bytes 270344 | tf_op jit(solution)/shard_map/ppermute | solution.py:18
  67.2 14.7 %collective-permute-start.20 = (bf16[32,1408]{1,0:T(8,128)(2,1)S(1)}, bf16[32,1408]{1,0:T(8,128)(2,1)S(1)}, u32[]{:S(2)}, u32[]{:S(2)}) collective-permute-start(bf16[32,1408]{1,0:T(8,128)(2,1)S(1)} %get-tuple-element.138.refs_0_), channel_id=1, source_target_pairs={{0,2},{1,3},{2,0},{3,1},{4,6},{5,7},{6,4},{7,5},{8,10},{9,11},{10,... | collective-permute-start | bytes 270344 | tf_op jit(solution)/shard_map/ppermute | solution.py:18
  68.6 17.3 %collective-permute-start.25 = (bf16[512,256]{1,0:T(8,128)(2,1)S(1)}, bf16[512,256]{1,0:T(8,128)(2,1)S(1)}, u32[]{:S(2)}, u32[]{:S(2)}) collective-permute-start(bf16[512,256]{1,0:T(8,128)(2,1)S(1)} %get-tuple-element.143), channel_id=1, source_target_pairs={{0,16},{16,0},{1,17},{17,1},{2,18},{18,2},{3,19},{19,3},{4,20},{20... | collective-permute-start | bytes 786440 | tf_op jit(solution)/shard_map/ppermute | solution.py:18
  81.9 11.7 %collective-permute-start.22 = (bf16[32,4224]{1,0:T(8,128)(2,1)S(1)}, bf16[32,4224]{1,0:T(8,128)(2,1)S(1)}, u32[]{:S(2)}, u32[]{:S(2)}) collective-permute-start(bf16[32,4224]{1,0:T(8,128)(2,1)S(1)} %constant_dynamic-update-slice_fusion.refs_4_), channel_id=1, source_target_pairs={{0,1},{1,0},{2,3},{3,2},{4,5},{5,4},{6,7},{7,6},{8,9},{9,8},{10,11... | collective-permute-start | bytes 811016 | tf_op jit(solution)/shard_map/ppermute | solution.py:18
  83.4 10.7 %collective-permute-start.23 = (bf16[32,4224]{1,0:T(8,128)(2,1)S(1)}, bf16[32,4224]{1,0:T(8,128)(2,1)S(1)}, u32[]{:S(2)}, u32[]{:S(2)}) collective-permute-start(bf16[32,4224]{1,0:T(8,128)(2,1)S(1)} %constant_dynamic-update-slice_fusion.refs_4_), channel_id=1, source_target_pairs={{0,2},{1,3},{2,0},{3,1},{4,6},{5,7},{6,4},{7,5},{8,10},{9,11},{10,... | collective-permute-start | bytes 811016 | tf_op jit(solution)/shard_map/ppermute | solution.py:18
  83.4 10.7 %collective-permute-start.24 = (bf16[32,4224]{1,0:T(8,128)(2,1)S(1)}, bf16[32,4224]{1,0:T(8,128)(2,1)S(1)}, u32[]{:S(2)}, u32[]{:S(2)}) collective-permute-start(bf16[32,4224]{1,0:T(8,128)(2,1)S(1)} %constant_dynamic-update-slice_fusion.refs_4_), channel_id=1, source_target_pairs={{0,3},{1,2},{2,1},{3,0},{4,7},{5,6},{6,5},{7,4},{8,11},{9,10},{10,... | collective-permute-start | bytes 811016 | tf_op jit(solution)/shard_map/ppermute | solution.py:18
  84.7 8.9 %collective-permute-start.21 = (bf16[32,1408]{1,0:T(8,128)(2,1)S(1)}, bf16[32,1408]{1,0:T(8,128)(2,1)S(1)}, u32[]{:S(2)}, u32[]{:S(2)}) collective-permute-start(bf16[32,1408]{1,0:T(8,128)(2,1)S(1)} %get-tuple-element.138.refs_0_), channel_id=1, source_target_pairs={{0,3},{1,2},{2,1},{3,0},{4,7},{5,6},{6,5},{7,4},{8,11},{9,10},{10,... | collective-permute-start | bytes 270344 | tf_op jit(solution)/shard_map/ppermute | solution.py:18
  99.6 11.5 %collective-permute-start.26 = (bf16[256,1024]{1,0:T(8,128)(2,1)S(1)}, bf16[256,1024]{1,0:T(8,128)(2,1)S(1)}, u32[]{:S(2)}, u32[]{:S(2)}) collective-permute-start(bf16[256,1024]{1,0:T(8,128)(2,1)S(1)} %get-tuple-element.146), channel_id=1, source_target_pairs={{0,16},{16,0},{1,17},{17,1},{2,18},{18,2},{3,19},{19,3},{4,20},{20... | collective-permute-start | bytes 1572872 | tf_op jit(solution)/shard_map/ppermute | solution.py:18
  105.5 5.5 %collective-permute-start.27 = (bf16[256,1024]{1,0:T(8,128)(2,1)S(1)}, bf16[256,1024]{1,0:T(8,128)(2,1)S(1)}, u32[]{:S(2)}, u32[]{:S(2)}) collective-permute-start(bf16[256,1024]{1,0:T(8,128)(2,1)S(1)} %get-tuple-element.147), channel_id=1, source_target_pairs={{0,16},{16,0},{1,17},{17,1},{2,18},{18,2},{3,19},{19,3},{4,20},{20... | collective-permute-start | bytes 1572872 | tf_op jit(solution)/shard_map/ppermute | solution.py:18
  (11 other events, 44.4 us)
